TPU v7x, 256 devices: a whole 4x4x8 slice. The times are simulated.
256 devices in a mesh: doc: 32 (over y, x, core), term: 4 (over z_lo), pair: 2 (over z_hi).
Axes of the slice: x: 4, y: 4, z: 8 (z_hi: 2, z_lo: 4; z = z_hi * 4 + z_lo), core: 2. Of those that a mesh axis runs over, the one named last changes fastest.
Arguments:
- counts: int32 [64, 16, 128, 128], P('doc', 'term'), may hold values from 0 to 11
- block_ids: int32 [64, 16], P('doc', 'term'), may hold values from 0 to 8191, as said below
- live_slots: int32 [64, 16], P('doc', 'term'), may hold values 0 or 1
- lengths: int32 [8192], P('doc'), may hold values from 1 to 24528, as said below
- pairs: int32 [4096, 2], P(('doc', 'pair')), may hold values from 0 to 63, as said below
- pair_count: int32 [64], P(('doc', 'pair')), may hold values from 1 to 64, as said below
Outputs:
- gram: float32 [4096, 128, 128], P(('doc', 'pair'), 'term')
Inputs may be any that keep to these rules, and one draw needn't show every extreme that they name: `block_ids`: columns s * 4 to (s + 1) * 4 - 1 hold term blocks of the s-th of 4 equal ranges of the 8192 blocks, distinct within one document block and range. `lengths`: document b * 128 + r has a length of the sum of counts[b, s, r, t] over all slots s and all t plus tokens outside its blocks: 1 to 2000 of them for every document but the last, whose length is exactly 24528. `pairs`: the left block of row k belongs to doc index k // 128. Rows k with k % 64 < pair_count[k // 64] are live; some entry equals 64.
All inputs are finite; a program needn't handle non-finite values. No bound on the sum of `live_slots` on one device may be relied on, other than what follows from the above.
Results may differ from a plain program's by a relative error of at most 0.0014.
Values may be sent and summed in bfloat16 or wider, within the bound.
No kernel may reach another device: no remote copies, remote signals or barrier semaphores. Data moves between devices by JAX's collectives and lax.ppermute only.
A program may use at most 64 MiB of HBM per device.

v0:
```python
import jax
import jax.numpy as jnp
from jax import lax
from jax.experimental import pallas as pl
from jax.experimental.pallas import tpu as pltpu
from jax.sharding import PartitionSpec as P


SIDE = 4
CORES = 2
UNROLL = 4
CHUNKS = (16, 24, 24)
GRAM_SCALE = 32.0
SMALL_ROWS = 32

saturation = 1.2
length_weight = 0.75
epsilon = 1e-06


def doc_of(y, x, core):
    return ((y % SIDE) * SIDE + x % SIDE) * CORES + core % CORES


def permute_doc(value, source):
    moves = [
        (doc_of(*source(y, x, c)), doc_of(y, x, c))
        for y in range(SIDE)
        for x in range(SIDE)
        for c in range(CORES)
    ]
    return lax.ppermute(value, "doc", moves)


def from_sibling(value):
    return permute_doc(value, lambda y, x, c: (y, x, c + 1))


def from_ring(value, phase, shift):
    def source(y, x, c):
        return (y, x + shift, c) if c == phase else (y + shift, x, c)

    return permute_doc(value, source)


def gather_ring(value, phase):
    return jnp.concatenate([value] + [from_ring(value, phase, s) for s in (1, 2, 3)], axis=0)


def gather_sibling(value):
    return jnp.concatenate([value, from_sibling(value)], axis=0)


def gather_rest(ring):
    half = ring.shape[0] // 2
    ahead = from_ring(ring, 1, 1)
    behind = from_ring(ring, 1, 3)
    across_low = from_ring(ahead[:half], 1, 1)
    across_high = from_ring(behind[half:], 1, 3)
    own = [ring, ahead, behind, across_low, across_high]
    return own + [from_sibling(piece) for piece in own]


def place_right(doc, doc_at):
    core = doc % CORES
    dx = (doc // CORES - doc_at // CORES) % SIDE
    dy = (doc // (SIDE * CORES) - doc_at // (SIDE * CORES)) % SIDE
    dcore = (doc - doc_at) % CORES
    inner = jnp.where(core == 0, dx, dy)
    outer = jnp.where(core == 0, dy, dx)
    piece = jnp.where(
        outer == 0, 0, jnp.where(outer == 1, 1, jnp.where(outer == 3, 2, 3 + inner // (SIDE // 2)))
    )
    spot = jnp.where(outer == 2, inner % (SIDE // 2), inner)
    return piece + dcore * 5, spot, (dcore * SIDE + outer) * SIDE + inner


def swap_term(value, bit, n_term):
    return lax.ppermute(value, "term", [(a, a ^ bit) for a in range(n_term)])


def prepare(counts, block_ids, live_slots, lengths):
    blocks, slots, rows, terms = counts.shape
    own_slots = blocks * slots
    tile_rows = own_slots * terms

    def kernel(ids_ref, live_ref, length_ref, count_ref, payload_ref, own_ref):
        cols = []
        id_rows = []
        for b in range(blocks):
            for s in range(slots):
                c = jnp.where(live_ref[b, s] > 0, count_ref[b, s], 0).astype(jnp.float32)
                at = (b * slots + s) * terms
                payload_ref[at : at + terms, :] = c.T.astype(jnp.bfloat16)
                own_ref[b, :, s * terms : (s + 1) * terms] = c.astype(jnp.bfloat16)
                cols.append(jnp.sum(jnp.where(c > 0.0, 1.0, 0.0), axis=0, keepdims=True))
                id_rows.append(jnp.full((1, rows), ids_ref[b, s], jnp.int32))
        ids = jnp.concatenate(id_rows, axis=0)
        length = length_ref[...]
        halves = lambda whole: ((whole >> 8).astype(jnp.float32), (whole & 255).astype(jnp.float32))
        spare = jnp.zeros((SMALL_ROWS - 3 * own_slots - 2 * blocks, rows), jnp.float32)
        small = jnp.concatenate(cols + [*halves(ids), *halves(length), spare], axis=0)
        payload_ref[tile_rows:, :] = small.astype(jnp.bfloat16)

    smem = pl.BlockSpec(memory_space=pltpu.SMEM)
    vmem = pl.BlockSpec(memory_space=pltpu.VMEM)
    return pl.pallas_call(
        kernel,
        in_specs=[smem, smem, vmem, vmem],
        out_specs=[vmem, vmem],
        out_shape=[
            jax.ShapeDtypeStruct((tile_rows + SMALL_ROWS, rows), jnp.bfloat16),
            jax.ShapeDtypeStruct((blocks, rows, slots * terms), jnp.bfloat16),
        ],
        name="prepare",
    )(block_ids, live_slots, lengths.reshape(blocks, rows), counts)


def weigh(block_ids, small_own, small_sibling, own_counts):
    blocks, rows, width = own_counts.shape
    slots = block_ids.shape[1]
    terms = width // slots
    own_slots = blocks * slots
    half_docs = small_own.shape[0]
    docs_all = 2 * half_docs * blocks * rows

    def kernel(ids_ref, near_ref, far_ref, own_ref, id_ref, length_ref, idf_ref, weight_ref, square_ref):
        small = jnp.concatenate([near_ref[...], far_ref[...]], axis=0).astype(jnp.float32)
        cols = small[:, :own_slots]
        ids = small[:, own_slots : 2 * own_slots] * 256.0 + small[:, 2 * own_slots : 3 * own_slots]
        ids = ids.astype(jnp.int32)
        id_ref[...] = ids
        packed = small[:, 3 * own_slots :]
        length = packed * 256.0 + pltpu.roll(packed, packed.shape[1] - blocks, 1)
        row_at = lax.broadcasted_iota(jnp.int32, length.shape, 1)
        total = jnp.sum(jnp.sum(jnp.where(row_at < blocks, length, 0.0), axis=0), keepdims=True)
        avg_len = total / docs_all
        scaled = saturation * (1.0 - length_weight + length_weight * length / avg_len[None])
        length_ref[...] = scaled
        for b in range(blocks):
            own_len = jnp.broadcast_to(scaled[0, b : b + 1, :], (rows, rows)).T
            square = jnp.zeros((rows, terms), jnp.float32)
            for s in range(slots):
                here = jnp.where(ids == ids_ref[b, s], cols, 0.0)
                doc_freq = jnp.sum(jnp.sum(here, axis=0), axis=0, keepdims=True)
                inv_freq = jnp.log(1.0 + (docs_all - doc_freq + 0.5) / (doc_freq + 0.5))
                idf = inv_freq * (saturation + 1.0)
                idf_ref[b * slots + s] = jnp.broadcast_to(idf, (rows, terms)).T
                c = own_ref[b, :, s * terms : (s + 1) * terms].astype(jnp.float32)
                weight = idf * c / (c + own_len)
                weight_ref[b, :, s * terms : (s + 1) * terms] = weight
                square = square + weight * weight
            square_ref[b : b + 1, :] = jnp.sum(square.T, axis=0, keepdims=True)

    smem = pl.BlockSpec(memory_space=pltpu.SMEM)
    vmem = pl.BlockSpec(memory_space=pltpu.VMEM)
    return pl.pallas_call(
        kernel,
        in_specs=[smem, vmem, vmem, vmem],
        out_specs=[vmem] * 5,
        out_shape=[
            jax.ShapeDtypeStruct((2 * half_docs, own_slots, rows), jnp.int32),
            jax.ShapeDtypeStruct((2 * half_docs, SMALL_ROWS - 3 * own_slots, rows), jnp.float32),
            jax.ShapeDtypeStruct((own_slots, terms, rows), jnp.float32),
            jax.ShapeDtypeStruct((blocks, rows, width), jnp.float32),
            jax.ShapeDtypeStruct((blocks, rows), jnp.float32),
        ],
        name="weigh",
    )(block_ids, small_own, small_sibling, own_counts)


def gram_chunk(first, size, select, own_ids, all_ids, order, weight, squares, idf_tiles, len_rows, pieces):
    own_slots, terms, rows = idf_tiles.shape
    blocks = weight.shape[0]
    slots = own_slots // blocks
    n_term = order.shape[0]
    part = rows // n_term
    groups = size // UNROLL

    def kernel(sel_ref, own_ref, ids_ref, order_ref, *refs):
        square_refs = refs[:n_term]
        weight_hbm, idf_hbm, length_hbm = refs[n_term : n_term + 3]
        piece_refs = refs[n_term + 3 : n_term + 3 + len(pieces)]
        out_hbm, *scratch = refs[n_term + 3 + len(pieces) :]
        weight_ref, idf_ref, length_ref, left_ref, tile_buf, gram_ref, loaded, arrived, written = scratch
        loads = [
            pltpu.make_async_copy(src, dst, loaded.at[n])
            for n, (src, dst) in enumerate(
                [(weight_hbm, weight_ref), (idf_hbm, idf_ref), (length_hbm, length_ref)]
            )
        ]
        for load in loads:
            load.start()

        def fetch(k, carry):
            piece = sel_ref[3, first + k]
            spot = pl.multiple_of(sel_ref[4, first + k], SMALL_ROWS)
            for p, ref in enumerate(piece_refs):

                @pl.when(piece == p)
                def _():
                    pltpu.make_async_copy(
                        ref.at[pl.ds(spot, slots * terms)], tile_buf.at[k], arrived.at[k]
                    ).start()

            return carry

        lax.fori_loop(0, size, fetch, 0)
        square_sum = square_refs[0][...]
        for ref in square_refs[1:]:
            square_sum = square_sum + ref[...]
        norm = lax.rsqrt(square_sum + epsilon) * GRAM_SCALE
        for load in loads:
            load.wait()
        for b in range(blocks):
            column = jnp.broadcast_to(norm[b : b + 1, :], (rows, rows)).T
            for s in range(slots):
                at = slice(s * terms, (s + 1) * terms)
                left_ref[b, :, at] = (weight_ref[b, :, at] * column).astype(jnp.bfloat16)

        def multiply(step, carry):
            for p in range(UNROLL):
                k = step * UNROLL + p
                pltpu.make_async_copy(
                    piece_refs[0].at[pl.ds(0, slots * terms)], tile_buf.at[k], arrived.at[k]
                ).wait()
            for p in range(UNROLL):
                k = step * UNROLL + p
                left = sel_ref[0, first + k]
                right_doc = sel_ref[1, first + k]
                right_block = sel_ref[2, first + k]
                len_row = length_ref[right_doc, pl.ds(right_block, 1), :]
                parts = []
                for i in range(slots):
                    wanted = own_ref[left, i]
                    found = jnp.int32(0)
                    place = jnp.int32(0)
                    for j in range(slots):
                        same = ids_ref[right_doc * own_slots + right_block * slots + j] == wanted
                        found = jnp.where(same, 1, found)
                        place = jnp.where(same, j, place)
                    start = pl.multiple_of(place * terms, terms)
                    c = tile_buf[k, pl.ds(start, terms), :].astype(jnp.float32)
                    factor = found.astype(jnp.float32) / (c + len_row)
                    parts.append((c * idf_ref[left * slots + i] * factor).astype(jnp.bfloat16))
                right_tile = jnp.concatenate(parts, axis=0)
                gram = jnp.dot(left_ref[left], right_tile, preferred_element_type=jnp.float32)
                for g in range(n_term):
                    gram_ref[order_ref[g], k] = gram[g * part : (g + 1) * part]
            span = pl.ds(step * UNROLL, UNROLL)
            pltpu.make_async_copy(
                gram_ref.at[:, span], out_hbm.at[:, span], written.at[step]
            ).start()
            return carry

        lax.fori_loop(0, groups, multiply, 0)

        def drain(step, carry):
            span = pl.ds(step * UNROLL, UNROLL)
            pltpu.make_async_copy(
                gram_ref.at[:, span], out_hbm.at[:, span], written.at[step]
            ).wait()
            return carry

        lax.fori_loop(0, groups, drain, 0)

    smem = pl.BlockSpec(memory_space=pltpu.SMEM)
    vmem = pl.BlockSpec(memory_space=pltpu.VMEM)
    anywhere = pl.BlockSpec(memory_space=pl.ANY)
    return pl.pallas_call(
        kernel,
        in_specs=[smem] * 4 + [vmem] * n_term + [anywhere] * (3 + len(pieces)),
        out_specs=anywhere,
        out_shape=jax.ShapeDtypeStruct((n_term, size, part, rows), jnp.float32),
        scratch_shapes=[
            pltpu.VMEM(weight.shape, jnp.float32),
            pltpu.VMEM(idf_tiles.shape, jnp.float32),
            pltpu.VMEM(len_rows.shape, jnp.float32),
            pltpu.VMEM(weight.shape, jnp.bfloat16),
            pltpu.VMEM((size, slots * terms, rows), jnp.bfloat16),
            pltpu.VMEM((n_term, size, part, rows), jnp.float32),
            pltpu.SemaphoreType.DMA((3,)),
            pltpu.SemaphoreType.DMA((size,)),
            pltpu.SemaphoreType.DMA((groups,)),
        ],
        name="gram",
    )(select, own_ids, all_ids, order, *squares, weight, idf_tiles, len_rows, *pieces)


def whole(counts, block_ids, live_slots, lengths, pairs, pair_count):
    blocks, slots, rows, terms = counts.shape
    n_doc = lax.axis_size("doc")
    n_term = lax.axis_size("term")
    doc_at = lax.axis_index("doc")
    term_at = lax.axis_index("term")
    tile_rows = blocks * slots * terms
    payload_rows = tile_rows + SMALL_ROWS

    payload, own_counts = prepare(counts, block_ids, live_slots, lengths)
    ring = gather_ring(payload, 0)
    small_own = gather_ring(ring.reshape(SIDE, payload_rows, rows)[:, tile_rows:], 1)
    small_sibling = from_sibling(small_own)
    pieces = gather_rest(ring)
    all_ids, len_rows, idf_tiles, weight, square_part = weigh(
        block_ids, small_own, small_sibling, own_counts
    )
    all_ids = all_ids[:, :, 0].reshape(-1)
    squares = [square_part] + [swap_term(square_part, bit, n_term) for bit in range(1, n_term)]

    left_sel = pairs[:, 0] - doc_at * blocks
    right_sel = pairs[:, 1]
    piece, spot, right_doc = place_right(right_sel // blocks, doc_at)
    right_block = right_sel % blocks
    start_row = spot * payload_rows + right_block * (slots * terms)
    select = jnp.stack([left_sel, right_doc, right_block, piece, start_row])
    apart = jnp.arange(n_term, dtype=jnp.int32) ^ term_at
    order = (apart % 2) * 2 + apart // 2
    live = jnp.arange(pairs.shape[0], dtype=jnp.int32) < pair_count[0]
    kept = []
    ready = []
    first = 0
    for step, size in enumerate(CHUNKS):
        if step >= 2:
            select, _ = lax.optimization_barrier((select, ready[step - 2]))
        grams = gram_chunk(
            first, size, select, block_ids, all_ids, order, weight, squares, idf_tiles, len_rows, pieces
        )
        first += size
        near = swap_term(grams[2:].astype(jnp.float16), 1, n_term)
        pass_on = (grams[1] + near[1].astype(jnp.float32)).astype(jnp.float16)
        ready.append(pass_on)
        far = swap_term(pass_on, 2, n_term)
        kept.append((grams[0], near[0], far))
    early, _ = lax.optimization_barrier((tuple(kept[:-1]), ready[-1]))
    totals = [
        mine + near.astype(jnp.float32) + far.astype(jnp.float32)
        for mine, near, far in (*early, kept[-1])
    ]
    norm, _ = lax.optimization_barrier((lax.rsqrt(sum(squares) + epsilon), ready[-2]))
    norm_ring = gather_ring(norm[None], 0)
    norm_ring, _ = lax.optimization_barrier((norm_ring, ready[-1]))
    norm_rows = gather_sibling(gather_ring(norm_ring, 1))
    norm_rows = norm_rows.reshape(n_doc * blocks, rows)[right_doc * blocks + right_block]
    right_norm = jnp.where(live[:, None], norm_rows * (1.0 / GRAM_SCALE), 0.0)
    return jnp.concatenate(totals, axis=0) * right_norm[:, None, :]


def solution(mesh):
    in_specs = (
        P("doc", "term", None, None),
        P("doc", "term"),
        P("doc", "term"),
        P("doc"),
        P(("doc", "pair"), None),
        P(("doc", "pair")),
    )
    out_specs = P(("doc", "pair"), "term", None)
    return jax.shard_map(whole, mesh=mesh, in_specs=in_specs, out_specs=out_specs, check_vma=False)
```

profile of v0, /device:TPU:1, one launch (start us, length us, event | category | flops | bytes accessed | tf_op | source)
XLA Modules:
  0.0 120.1 jit_solution(6983628588653798846)
XLA Ops:
  0.0 2.0 %prepare.1 = (bf16[1056,128]{1,0:T(8,128)(2,1)}, bf16[2,128,512]{2,1,0:T(8,128)(2,1)}) custom-call(s32[2,4]{1,0:T(2,128)} %own_ref.5, s32[2,4]{1,0:T(2,128)} %live_ref.1, s32[2,128]{1,0:T(2,128)} %bitcast.47, s32[2,4,128,128]{3,2,1,0:T(8,128)} %count_ref.1), custom_call_target="tpu_custom_call" | custom-call | tf_op jit(solution)/shard_map/prepare/pallas_call | solution.py:107
  2.0 3.6 %collective-permute-start = (bf16[1056,128]{1,0:T(8,128)(2,1)}, bf16[1056,128]{1,0:T(8,128)(2,1)S(1)}, u32[]{:S(2)}, u32[]{:S(2)}) collective-permute-start(bf16[1056,128]{1,0:T(8,128)(2,1)} %get-tuple-element.21), channel_id=1, source_target_pairs={{16,0},{72,8},{32,16},{88,24},{48,32},{104,40},{0,48},{120,56},{80... | collective-permute-start | bytes 811016 | tf_op jit(solution)/shard_map/ppermute | solution.py:32
  7.6 4.6 %collective-permute-done = bf16[1056,128]{1,0:T(8,128)(2,1)S(1)} collective-permute-done((bf16[1056,128]{1,0:T(8,128)(2,1)}, bf16[1056,128]{1,0:T(8,128)(2,1)S(1)}, u32[]{:S(2)}, u32[]{:S(2)}) %collective-permute-start) | collective-permute-done | bytes 270368 | tf_op jit(solution)/shard_map/ppermute | solution.py:32
  12.9 2.8 %collective-permute-done.2 = bf16[1056,128]{1,0:T(8,128)(2,1)S(1)} collective-permute-done((bf16[1056,128]{1,0:T(8,128)(2,1)}, bf16[1056,128]{1,0:T(8,128)(2,1)S(1)}, u32[]{:S(2)}, u32[]{:S(2)}) %collective-permute-start.2) | collective-permute-done | bytes 270368 | tf_op jit(solution)/shard_map/ppermute | solution.py:32
  15.8 2.3 %collective-permute-start.10 = (bf16[4224,128]{1,0:T(8,128)(2,1)S(1)}, bf16[4224,128]{1,0:T(8,128)(2,1)S(1)}, u32[]{:S(2)}, u32[]{:S(2)}) collective-permute-start(bf16[4224,128]{1,0:T(8,128)(2,1)S(1)} %constant_dynamic-update-slice_fusion.refs_7_), channel_id=1, source_target_pairs={{64,0},{24,8},{80,16},{40,24},{96,32},{56,40},{112,48},{8,56},{128... | collective-permute-start | bytes 3244040 | tf_op jit(solution)/shard_map/ppermute | solution.py:32
  18.1 2.7 %collective-permute-start.3 = (bf16[4,32,128]{2,1,0:T(8,128)(2,1)S(1)}, bf16[4,32,128]{2,1,0:T(8,128)(2,1)S(1)}, u32[]{:S(2)}, u32[]{:S(2)}) collective-permute-start(bf16[4,32,128]{2,1,0:T(8,128)(2,1)S(1)} %slice.89), channel_id=1, source_target_pairs={{64,0},{24,8},{80,16},{40,24},{96,32},{56,40},{112,48},{8,56},{128... | collective-permute-start | bytes 98312 | tf_op jit(solution)/shard_map/ppermute | solution.py:32
  21.4 9.5 %collective-permute-done.3 = bf16[4,32,128]{2,1,0:T(8,128)(2,1)S(1)} collective-permute-done((bf16[4,32,128]{2,1,0:T(8,128)(2,1)S(1)}, bf16[4,32,128]{2,1,0:T(8,128)(2,1)S(1)}, u32[]{:S(2)}, u32[]{:S(2)}) %collective-permute-start.3) | collective-permute-done | bytes 32800 | tf_op jit(solution)/shard_map/ppermute | solution.py:32
  30.9 1.9 %collective-permute-done.4 = bf16[4,32,128]{2,1,0:T(8,128)(2,1)S(1)} collective-permute-done((bf16[4,32,128]{2,1,0:T(8,128)(2,1)S(1)}, bf16[4,32,128]{2,1,0:T(8,128)(2,1)S(1)}, u32[]{:S(2)}, u32[]{:S(2)}) %collective-permute-start.4) | collective-permute-done | bytes 32800 | tf_op jit(solution)/shard_map/ppermute | solution.py:32
  32.8 1.5 %collective-permute-done.5 = bf16[4,32,128]{2,1,0:T(8,128)(2,1)S(1)} collective-permute-done((bf16[4,32,128]{2,1,0:T(8,128)(2,1)S(1)}, bf16[4,32,128]{2,1,0:T(8,128)(2,1)S(1)}, u32[]{:S(2)}, u32[]{:S(2)}) %collective-permute-start.5) | collective-permute-done | bytes 32800 | tf_op jit(solution)/shard_map/ppermute | solution.py:32
  34.3 3.3 %collective-permute-start.6 = (bf16[16,32,128]{2,1,0:T(8,128)(2,1)S(1)}, bf16[16,32,128]{2,1,0:T(8,128)(2,1)S(1)}, u32[]{:S(2)}, u32[]{:S(2)}) collective-permute-start(bf16[16,32,128]{2,1,0:T(8,128)(2,1)S(1)} %pad_maximum_fusion.near_ref), channel_id=1, source_target_pairs={{8,0},{0,8},{24,16},{16,24},{40,32},{32,40},{56,48},{48,56},{72,64... | collective-permute-start | bytes 393224 | tf_op jit(solution)/shard_map/ppermute | solution.py:32
  39.3 2.5 %weigh.1 = (s32[32,8,128]{2,1,0:T(8,128)}, f32[32,8,128]{2,1,0:T(8,128)}, f32[8,128,128]{2,1,0:T(8,128)}, f32[2,128,512]{2,1,0:T(8,128)}, f32[2,128]{1,0:T(2,128)}) custom-call(s32[2,4]{1,0:T(2,128)} %own_ref.5, bf16[16,32,128]{2,1,0:T(8,128)(2,1)} %copy-done.6, bf16[16,32,128]{2,1,0:T(8,128)(2,1)} %copy-done.10, bf16[2,128,512]{2,1,0:T(8,128)(2,1)} %get-tuple-element.22.own_ref), custom_call_target="tpu_custom_call" | custom-call | tf_op jit(solution)/shard_map/weigh/pallas_call | solution.py:157
  41.8 1.6 %collective-permute-start.7 = (f32[2,128]{1,0:T(2,128)}, f32[2,128]{1,0:T(2,128)S(1)}, u32[]{:S(2)}, u32[]{:S(2)}) collective-permute-start(f32[2,128]{1,0:T(2,128)} %get-tuple-element.24.refs_0_), channel_id=1, source_target_pairs={{0,2},{2,0},{4,6},{6,4},{1,3},{3,1},{5,7},{7,5},{8,10},{10,8},{12,... | collective-permute-start | bytes 3080 | tf_op jit(solution)/shard_map/ppermute | solution.py:79
  43.4 3.0 %collective-permute-start.8 = (f32[2,128]{1,0:T(2,128)}, f32[2,128]{1,0:T(2,128)S(1)}, u32[]{:S(2)}, u32[]{:S(2)}) collective-permute-start(f32[2,128]{1,0:T(2,128)} %get-tuple-element.24.refs_0_), channel_id=1, source_target_pairs={{0,4},{2,6},{4,0},{6,2},{1,5},{3,7},{5,1},{7,3},{8,12},{10,14},{12... | collective-permute-start | bytes 3080 | tf_op jit(solution)/shard_map/ppermute | solution.py:79
  49.8 1.6 %collective-permute-start.14 = (bf16[4224,128]{1,0:T(8,128)(2,1)S(1)}, bf16[4224,128]{1,0:T(8,128)(2,1)}, u32[]{:S(2)}, u32[]{:S(2)}) collective-permute-start(bf16[4224,128]{1,0:T(8,128)(2,1)S(1)} %constant_dynamic-update-slice_fusion.refs_7_), channel_id=1, source_target_pairs={{8,0},{0,8},{24,16},{16,24},{40,32},{32,40},{56,48},{48,56},{72,64... | collective-permute-start | bytes 3244040 | tf_op jit(solution)/shard_map/ppermute | solution.py:32
  51.5 1.5 %collective-permute-start.16 = (bf16[4224,128]{1,0:T(8,128)(2,1)S(1)}, bf16[4224,128]{1,0:T(8,128)(2,1)}, u32[]{:S(2)}, u32[]{:S(2)}) collective-permute-start(bf16[4224,128]{1,0:T(8,128)(2,1)S(1)} %collective-permute-done.11.refs_9_), channel_id=1, source_target_pairs={{8,0},{0,8},{24,16},{16,24},{40,32},{32,40},{56,48},{48,56},{72,64... | collective-permute-start | bytes 3244040 | tf_op jit(solution)/shard_map/ppermute | solution.py:32
  53.0 3.2 %collective-permute-done.12.refs_10_ = bf16[2112,128]{1,0:T(8,128)(2,1)} collective-permute-done((bf16[2112,128]{1,0:T(8,128)(2,1)}, bf16[2112,128]{1,0:T(8,128)(2,1)}, u32[]{:S(2)}, u32[]{:S(2)}) %collective-permute-start.12) | collective-permute-done | bytes 540704 | tf_op jit(solution)/shard_map/ppermute | solution.py:32
  56.2 1.8 %collective-permute-start.17 = (bf16[2112,128]{1,0:T(8,128)(2,1)}, bf16[2112,128]{1,0:T(8,128)(2,1)}, u32[]{:S(2)}, u32[]{:S(2)}) collective-permute-start(bf16[2112,128]{1,0:T(8,128)(2,1)} %collective-permute-done.12.refs_10_), channel_id=1, source_target_pairs={{8,0},{0,8},{24,16},{16,24},{40,32},{32,40},{56,48},{48,56},{72,64... | collective-permute-start | bytes 1622024 | tf_op jit(solution)/shard_map/ppermute | solution.py:32
  58.6 1.5 %collective-permute-start.18 = (bf16[2112,128]{1,0:T(8,128)(2,1)}, bf16[2112,128]{1,0:T(8,128)(2,1)}, u32[]{:S(2)}, u32[]{:S(2)}) collective-permute-start(bf16[2112,128]{1,0:T(8,128)(2,1)} %collective-permute-done.13.refs_11_), channel_id=1, source_target_pairs={{8,0},{0,8},{24,16},{16,24},{40,32},{32,40},{56,48},{48,56},{72,64... | collective-permute-start | bytes 1622024 | tf_op jit(solution)/shard_map/ppermute | solution.py:32
  63.4 5.1 %gram.3 = f32[4,16,32,128]{3,2,1,0:T(8,128)} custom-call(s32[5,64]{1,0:T(8,128)} %stack.2.sel_ref, s32[2,4]{1,0:T(2,128)} %own_ref.5, s32[256]{0:T(256)} %reshape_squeeze.3.ids_ref, s32[4]{0:T(128)} %fusion.13.order_ref, f32[2,128]{1,0:T(2,128)} %get-tuple-element.24.refs_0_, f32[2,128]{1,0:T(2,128)} %copy-done.12, f32[2,128]{1,0:T(2,128)} %copy-done.13, ...), custom_call_target="tpu_custom_call" | custom-call | tf_op jit(solution)/shard_map/gram/pallas_call | solution.py:270
  70.6 6.1 %gram.4 = f32[4,24,32,128]{3,2,1,0:T(8,128)} custom-call(s32[5,64]{1,0:T(8,128)} %stack.2.sel_ref, s32[2,4]{1,0:T(2,128)} %own_ref.5, s32[256]{0:T(256)} %reshape_squeeze.3.ids_ref, s32[4]{0:T(128)} %fusion.13.order_ref, f32[2,128]{1,0:T(2,128)} %get-tuple-element.24.refs_0_, f32[2,128]{1,0:T(2,128)} %copy-done.12, f32[2,128]{1,0:T(2,128)} %copy-done.13, ...), custom_call_target="tpu_custom_call" | custom-call | tf_op jit(solution)/shard_map/gram/pallas_call | solution.py:270
  76.7 2.0 %slice_convert_fusion.1 = f16[2,24,32,128]{3,2,1,0:T(8,128)(2,1)} fusion(f32[4,24,32,128]{3,2,1,0:T(8,128)} %gram.4), kind=kLoop, calls=%fused_computation.3 | loop fusion | flops 196608 | bytes 1179648 | tf_op jit(solution)/shard_map/convert.1
  80.6 2.4 %collective-permute-start.20 = (f16[16,32,128]{2,1,0:T(8,128)(2,1)}, f16[16,32,128]{2,1,0:T(8,128)(2,1)}, u32[]{:S(2)}, u32[]{:S(2)}) collective-permute-start(f16[16,32,128]{2,1,0:T(8,128)(2,1)} %get-tuple-element.49), channel_id=1, source_target_pairs={{0,4},{2,6},{4,0},{6,2},{1,5},{3,7},{5,1},{7,3},{8,12},{10,14},{12... | collective-permute-start | bytes 393224 | tf_op jit(solution)/shard_map/ppermute | solution.py:79
  83.0 6.1 %gram.5 = f32[4,24,32,128]{3,2,1,0:T(8,128)} custom-call(s32[5,64]{1,0:T(8,128)} %stack.2.sel_ref, s32[2,4]{1,0:T(2,128)} %own_ref.5, s32[256]{0:T(256)} %reshape_squeeze.3.ids_ref, s32[4]{0:T(128)} %fusion.13.order_ref, f32[2,128]{1,0:T(2,128)} %get-tuple-element.24.refs_0_, f32[2,128]{1,0:T(2,128)} %copy-done.12, f32[2,128]{1,0:T(2,128)} %copy-done.13, ...), custom_call_target="tpu_custom_call" | custom-call | tf_op jit(solution)/shard_map/gram/pallas_call | solution.py:270
  89.2 1.2 %slice_convert_fusion = f16[2,24,32,128]{3,2,1,0:T(8,128)(2,1)S(1)} fusion(f32[4,24,32,128]{3,2,1,0:T(8,128)} %gram.5), kind=kLoop, calls=%fused_computation.2 | loop fusion | flops 196608 | bytes 1179648 | tf_op jit(solution)/shard_map/convert
  90.4 1.5 %collective-permute-start.23 = (f16[2,24,32,128]{3,2,1,0:T(8,128)(2,1)S(1)}, f16[2,24,32,128]{3,2,1,0:T(8,128)(2,1)S(1)}, u32[]{:S(2)}, u32[]{:S(2)}) collective-permute-start(f16[2,24,32,128]{3,2,1,0:T(8,128)(2,1)S(1)} %slice_convert_fusion), channel_id=1, source_target_pairs={{0,2},{2,0},{4,6},{6,4},{1,3},{3,1},{5,7},{7,5},{8,10},{10,8},{12,... | collective-permute-start | bytes 1179656 | tf_op jit(solution)/shard_map/ppermute | solution.py:79
  94.0 2.4 %collective-permute-start.26 = (f32[1,2,128]{2,1,0:T(2,128)S(1)}, f32[1,2,128]{2,1,0:T(2,128)S(1)}, u32[]{:S(2)}, u32[]{:S(2)}) collective-permute-start(f32[1,2,128]{2,1,0:T(2,128)S(1)} %bitcast.44), channel_id=1, source_target_pairs={{32,0},{136,8},{48,16},{152,24},{0,32},{168,40},{16,48},{184,56},{... | collective-permute-start | bytes 3080 | tf_op jit(solution)/shard_map/ppermute | solution.py:32
  98.4 1.9 %collective-permute-done.27 = f32[1,2,128]{2,1,0:T(2,128)S(1)} collective-permute-done((f32[1,2,128]{2,1,0:T(2,128)S(1)}, f32[1,2,128]{2,1,0:T(2,128)S(1)}, u32[]{:S(2)}, u32[]{:S(2)}) %collective-permute-start.27) | collective-permute-done | bytes 1056 | tf_op jit(solution)/shard_map/ppermute | solution.py:32
  100.4 1.2 %collective-permute-start.28 = (f32[4,2,128]{2,1,0:T(2,128)S(1)}, f32[4,2,128]{2,1,0:T(2,128)S(1)}, u32[]{:S(2)}, u32[]{:S(2)}) collective-permute-start(f32[4,2,128]{2,1,0:T(2,128)S(1)} %pad_maximum_fusion.2), channel_id=1, source_target_pairs={{64,0},{24,8},{80,16},{40,24},{96,32},{56,40},{112,48},{8,56},{128... | collective-permute-start | bytes 12296 | tf_op jit(solution)/shard_map/ppermute | solution.py:32
  101.7 3.0 %collective-permute-start.29 = (f32[4,2,128]{2,1,0:T(2,128)S(1)}, f32[4,2,128]{2,1,0:T(2,128)S(1)}, u32[]{:S(2)}, u32[]{:S(2)}) collective-permute-start(f32[4,2,128]{2,1,0:T(2,128)S(1)} %pad_maximum_fusion.2), channel_id=1, source_target_pairs={{128,0},{40,8},{144,16},{56,24},{160,32},{8,40},{176,48},{24,56},{... | collective-permute-start | bytes 12296 | tf_op jit(solution)/shard_map/ppermute | solution.py:32
  104.6 1.3 %collective-permute-start.24 = (f16[24,32,128]{2,1,0:T(8,128)(2,1)S(1)}, f16[24,32,128]{2,1,0:T(8,128)(2,1)S(1)}, u32[]{:S(2)}, u32[]{:S(2)}) collective-permute-start(f16[24,32,128]{2,1,0:T(8,128)(2,1)S(1)} %fusion.6), channel_id=1, source_target_pairs={{0,4},{2,6},{4,0},{6,2},{1,5},{3,7},{5,1},{7,3},{8,12},{10,14},{12... | collective-permute-start | bytes 589832 | tf_op jit(solution)/shard_map/ppermute | solution.py:79
  107.0 1.4 %collective-permute-done.30 = f32[4,2,128]{2,1,0:T(2,128)S(1)} collective-permute-done((f32[4,2,128]{2,1,0:T(2,128)S(1)}, f32[4,2,128]{2,1,0:T(2,128)S(1)}, u32[]{:S(2)}, u32[]{:S(2)}) %collective-permute-start.30) | collective-permute-done | bytes 4128 | tf_op jit(solution)/shard_map/ppermute | solution.py:32
  108.5 8.0 %collective-permute-start.31 = (f32[16,2,128]{2,1,0:T(2,128)S(1)}, f32[16,2,128]{2,1,0:T(2,128)S(1)}, u32[]{:S(2)}, u32[]{:S(2)}) collective-permute-start(f32[16,2,128]{2,1,0:T(2,128)S(1)} %pad_maximum_fusion.1), channel_id=1, source_target_pairs={{8,0},{0,8},{24,16},{16,24},{40,32},{32,40},{56,48},{48,56},{72,64... | collective-permute-start | bytes 49160 | tf_op jit(solution)/shard_map/ppermute | solution.py:32
  (111 shorter events, 24.7 us)
Async XLA Ops:
  2.0 10.2 %collective-permute-start = (bf16[1056,128]{1,0:T(8,128)(2,1)}, bf16[1056,128]{1,0:T(8,128)(2,1)S(1)}, u32[]{:S(2)}, u32[]{:S(2)}) collective-permute-start(bf16[1056,128]{1,0:T(8,128)(2,1)} %get-tuple-element.21), channel_id=1, source_target_pairs={{16,0},{72,8},{32,16},{88,24},{48,32},{104,40},{0,48},{120,56},{80... | collective-permute-start | bytes 811016 | tf_op jit(solution)/shard_map/ppermute | solution.py:32
  5.5 7.4 %collective-permute-start.1 = (bf16[1056,128]{1,0:T(8,128)(2,1)}, bf16[1056,128]{1,0:T(8,128)(2,1)S(1)}, u32[]{:S(2)}, u32[]{:S(2)}) collective-permute-start(bf16[1056,128]{1,0:T(8,128)(2,1)} %get-tuple-element.21), channel_id=1, source_target_pairs={{32,0},{136,8},{48,16},{152,24},{0,32},{168,40},{16,48},{184,56},{... | collective-permute-start | bytes 811016 | tf_op jit(solution)/shard_map/ppermute | solution.py:32
  5.9 9.9 %collective-permute-start.2 = (bf16[1056,128]{1,0:T(8,128)(2,1)}, bf16[1056,128]{1,0:T(8,128)(2,1)S(1)}, u32[]{:S(2)}, u32[]{:S(2)}) collective-permute-start(bf16[1056,128]{1,0:T(8,128)(2,1)} %get-tuple-element.21), channel_id=1, source_target_pairs={{48,0},{200,8},{0,16},{216,24},{16,32},{232,40},{32,48},{248,56},{... | collective-permute-start | bytes 811016 | tf_op jit(solution)/shard_map/ppermute | solution.py:32
  15.8 30.6 %collective-permute-start.10 = (bf16[4224,128]{1,0:T(8,128)(2,1)S(1)}, bf16[4224,128]{1,0:T(8,128)(2,1)S(1)}, u32[]{:S(2)}, u32[]{:S(2)}) collective-permute-start(bf16[4224,128]{1,0:T(8,128)(2,1)S(1)} %constant_dynamic-update-slice_fusion.refs_7_), channel_id=1, source_target_pairs={{64,0},{24,8},{80,16},{40,24},{96,32},{56,40},{112,48},{8,56},{128... | collective-permute-start | bytes 3244040 | tf_op jit(solution)/shard_map/ppermute | solution.py:32
  18.1 29.6 %collective-permute-start.11 = (bf16[4224,128]{1,0:T(8,128)(2,1)S(1)}, bf16[4224,128]{1,0:T(8,128)(2,1)S(1)}, u32[]{:S(2)}, u32[]{:S(2)}) collective-permute-start(bf16[4224,128]{1,0:T(8,128)(2,1)S(1)} %constant_dynamic-update-slice_fusion.refs_7_), channel_id=1, source_target_pairs={{192,0},{56,8},{208,16},{8,24},{224,32},{24,40},{240,48},{40,56},{... | collective-permute-start | bytes 3244040 | tf_op jit(solution)/shard_map/ppermute | solution.py:32
  18.1 12.8 %collective-permute-start.3 = (bf16[4,32,128]{2,1,0:T(8,128)(2,1)S(1)}, bf16[4,32,128]{2,1,0:T(8,128)(2,1)S(1)}, u32[]{:S(2)}, u32[]{:S(2)}) collective-permute-start(bf16[4,32,128]{2,1,0:T(8,128)(2,1)S(1)} %slice.89), channel_id=1, source_target_pairs={{64,0},{24,8},{80,16},{40,24},{96,32},{56,40},{112,48},{8,56},{128... | collective-permute-start | bytes 98312 | tf_op jit(solution)/shard_map/ppermute | solution.py:32
  20.7 12.0 %collective-permute-start.4 = (bf16[4,32,128]{2,1,0:T(8,128)(2,1)S(1)}, bf16[4,32,128]{2,1,0:T(8,128)(2,1)S(1)}, u32[]{:S(2)}, u32[]{:S(2)}) collective-permute-start(bf16[4,32,128]{2,1,0:T(8,128)(2,1)S(1)} %slice.89), channel_id=1, source_target_pairs={{128,0},{40,8},{144,16},{56,24},{160,32},{8,40},{176,48},{24,56},{... | collective-permute-start | bytes 98312 | tf_op jit(solution)/shard_map/ppermute | solution.py:32
  20.7 13.5 %collective-permute-start.5 = (bf16[4,32,128]{2,1,0:T(8,128)(2,1)S(1)}, bf16[4,32,128]{2,1,0:T(8,128)(2,1)S(1)}, u32[]{:S(2)}, u32[]{:S(2)}) collective-permute-start(bf16[4,32,128]{2,1,0:T(8,128)(2,1)S(1)} %slice.89), channel_id=1, source_target_pairs={{192,0},{56,8},{208,16},{8,24},{224,32},{24,40},{240,48},{40,56},{... | collective-permute-start | bytes 98312 | tf_op jit(solution)/shard_map/ppermute | solution.py:32
  34.3 4.3 %collective-permute-start.6 = (bf16[16,32,128]{2,1,0:T(8,128)(2,1)S(1)}, bf16[16,32,128]{2,1,0:T(8,128)(2,1)S(1)}, u32[]{:S(2)}, u32[]{:S(2)}) collective-permute-start(bf16[16,32,128]{2,1,0:T(8,128)(2,1)S(1)} %pad_maximum_fusion.near_ref), channel_id=1, source_target_pairs={{8,0},{0,8},{24,16},{16,24},{40,32},{32,40},{56,48},{48,56},{72,64... | collective-permute-start | bytes 393224 | tf_op jit(solution)/shard_map/ppermute | solution.py:32
  41.8 7.9 %collective-permute-start.7 = (f32[2,128]{1,0:T(2,128)}, f32[2,128]{1,0:T(2,128)S(1)}, u32[]{:S(2)}, u32[]{:S(2)}) collective-permute-start(f32[2,128]{1,0:T(2,128)} %get-tuple-element.24.refs_0_), channel_id=1, source_target_pairs={{0,2},{2,0},{4,6},{6,4},{1,3},{3,1},{5,7},{7,5},{8,10},{10,8},{12,... | collective-permute-start | bytes 3080 | tf_op jit(solution)/shard_map/ppermute | solution.py:79
  43.4 7.9 %collective-permute-start.8 = (f32[2,128]{1,0:T(2,128)}, f32[2,128]{1,0:T(2,128)S(1)}, u32[]{:S(2)}, u32[]{:S(2)}) collective-permute-start(f32[2,128]{1,0:T(2,128)} %get-tuple-element.24.refs_0_), channel_id=1, source_target_pairs={{0,4},{2,6},{4,0},{6,2},{1,5},{3,7},{5,1},{7,3},{8,12},{10,14},{12... | collective-permute-start | bytes 3080 | tf_op jit(solution)/shard_map/ppermute | solution.py:79
  46.4 5.0 %collective-permute-start.9 = (f32[2,128]{1,0:T(2,128)}, f32[2,128]{1,0:T(2,128)S(1)}, u32[]{:S(2)}, u32[]{:S(2)}) collective-permute-start(f32[2,128]{1,0:T(2,128)} %get-tuple-element.24.refs_0_), channel_id=1, source_target_pairs={{0,6},{2,4},{4,2},{6,0},{1,7},{3,5},{5,3},{7,1},{8,14},{10,12},{12... | collective-permute-start | bytes 3080 | tf_op jit(solution)/shard_map/ppermute | solution.py:79
  47.3 8.8 %collective-permute-start.12 = (bf16[2112,128]{1,0:T(8,128)(2,1)}, bf16[2112,128]{1,0:T(8,128)(2,1)}, u32[]{:S(2)}, u32[]{:S(2)}) collective-permute-start(bf16[2112,128]{1,0:T(8,128)(2,1)} %slice.90), channel_id=1, source_target_pairs={{64,0},{24,8},{80,16},{40,24},{96,32},{56,40},{112,48},{8,56},{128... | collective-permute-start | bytes 1622024 | tf_op jit(solution)/shard_map/ppermute | solution.py:32
  48.6 10.0 %collective-permute-start.13 = (bf16[2112,128]{1,0:T(8,128)(2,1)}, bf16[2112,128]{1,0:T(8,128)(2,1)}, u32[]{:S(2)}, u32[]{:S(2)}) collective-permute-start(bf16[2112,128]{1,0:T(8,128)(2,1)} %slice.91), channel_id=1, source_target_pairs={{192,0},{56,8},{208,16},{8,24},{224,32},{24,40},{240,48},{40,56},{... | collective-permute-start | bytes 1622024 | tf_op jit(solution)/shard_map/ppermute | solution.py:32
  49.8 13.5 %collective-permute-start.14 = (bf16[4224,128]{1,0:T(8,128)(2,1)S(1)}, bf16[4224,128]{1,0:T(8,128)(2,1)}, u32[]{:S(2)}, u32[]{:S(2)}) collective-permute-start(bf16[4224,128]{1,0:T(8,128)(2,1)S(1)} %constant_dynamic-update-slice_fusion.refs_7_), channel_id=1, source_target_pairs={{8,0},{0,8},{24,16},{16,24},{40,32},{32,40},{56,48},{48,56},{72,64... | collective-permute-start | bytes 3244040 | tf_op jit(solution)/shard_map/ppermute | solution.py:32
  51.3 12.0 %collective-permute-start.15 = (bf16[4224,128]{1,0:T(8,128)(2,1)S(1)}, bf16[4224,128]{1,0:T(8,128)(2,1)}, u32[]{:S(2)}, u32[]{:S(2)}) collective-permute-start(bf16[4224,128]{1,0:T(8,128)(2,1)S(1)} %collective-permute-done.10.refs_8_), channel_id=1, source_target_pairs={{8,0},{0,8},{24,16},{16,24},{40,32},{32,40},{56,48},{48,56},{72,64... | collective-permute-start | bytes 3244040 | tf_op jit(solution)/shard_map/ppermute | solution.py:32
  51.5 11.8 %collective-permute-start.16 = (bf16[4224,128]{1,0:T(8,128)(2,1)S(1)}, bf16[4224,128]{1,0:T(8,128)(2,1)}, u32[]{:S(2)}, u32[]{:S(2)}) collective-permute-start(bf16[4224,128]{1,0:T(8,128)(2,1)S(1)} %collective-permute-done.11.refs_9_), channel_id=1, source_target_pairs={{8,0},{0,8},{24,16},{16,24},{40,32},{32,40},{56,48},{48,56},{72,64... | collective-permute-start | bytes 3244040 | tf_op jit(solution)/shard_map/ppermute | solution.py:32
  56.2 7.1 %collective-permute-start.17 = (bf16[2112,128]{1,0:T(8,128)(2,1)}, bf16[2112,128]{1,0:T(8,128)(2,1)}, u32[]{:S(2)}, u32[]{:S(2)}) collective-permute-start(bf16[2112,128]{1,0:T(8,128)(2,1)} %collective-permute-done.12.refs_10_), channel_id=1, source_target_pairs={{8,0},{0,8},{24,16},{16,24},{40,32},{32,40},{56,48},{48,56},{72,64... | collective-permute-start | bytes 1622024 | tf_op jit(solution)/shard_map/ppermute | solution.py:32
  58.6 4.7 %collective-permute-start.18 = (bf16[2112,128]{1,0:T(8,128)(2,1)}, bf16[2112,128]{1,0:T(8,128)(2,1)}, u32[]{:S(2)}, u32[]{:S(2)}) collective-permute-start(bf16[2112,128]{1,0:T(8,128)(2,1)} %collective-permute-done.13.refs_11_), channel_id=1, source_target_pairs={{8,0},{0,8},{24,16},{16,24},{40,32},{32,40},{56,48},{48,56},{72,64... | collective-permute-start | bytes 1622024 | tf_op jit(solution)/shard_map/ppermute | solution.py:32
  69.5 10.4 %collective-permute-start.19 = (f16[2,16,32,128]{3,2,1,0:T(8,128)(2,1)S(1)}, f16[2,16,32,128]{3,2,1,0:T(8,128)(2,1)S(1)}, u32[]{:S(2)}, u32[]{:S(2)}) collective-permute-start(f16[2,16,32,128]{3,2,1,0:T(8,128)(2,1)S(1)} %slice_convert_fusion.2), channel_id=1, source_target_pairs={{0,2},{2,0},{4,6},{6,4},{1,3},{3,1},{5,7},{7,5},{8,10},{10,8},{12,... | collective-permute-start | bytes 786440 | tf_op jit(solution)/shard_map/ppermute | solution.py:79
  78.7 14.1 %collective-permute-start.21 = (f16[2,24,32,128]{3,2,1,0:T(8,128)(2,1)}, f16[2,24,32,128]{3,2,1,0:T(8,128)(2,1)}, u32[]{:S(2)}, u32[]{:S(2)}) collective-permute-start(f16[2,24,32,128]{3,2,1,0:T(8,128)(2,1)} %slice_convert_fusion.1), channel_id=1, source_target_pairs={{0,2},{2,0},{4,6},{6,4},{1,3},{3,1},{5,7},{7,5},{8,10},{10,8},{12,... | collective-permute-start | bytes 1179656 | tf_op jit(solution)/shard_map/ppermute | solution.py:79
  80.6 24.0 %collective-permute-start.20 = (f16[16,32,128]{2,1,0:T(8,128)(2,1)}, f16[16,32,128]{2,1,0:T(8,128)(2,1)}, u32[]{:S(2)}, u32[]{:S(2)}) collective-permute-start(f16[16,32,128]{2,1,0:T(8,128)(2,1)} %get-tuple-element.49), channel_id=1, source_target_pairs={{0,4},{2,6},{4,0},{6,2},{1,5},{3,7},{5,1},{7,3},{8,12},{10,14},{12... | collective-permute-start | bytes 393224 | tf_op jit(solution)/shard_map/ppermute | solution.py:79
  90.4 9.9 %collective-permute-start.23 = (f16[2,24,32,128]{3,2,1,0:T(8,128)(2,1)S(1)}, f16[2,24,32,128]{3,2,1,0:T(8,128)(2,1)S(1)}, u32[]{:S(2)}, u32[]{:S(2)}) collective-permute-start(f16[2,24,32,128]{3,2,1,0:T(8,128)(2,1)S(1)} %slice_convert_fusion), channel_id=1, source_target_pairs={{0,2},{2,0},{4,6},{6,4},{1,3},{3,1},{5,7},{7,5},{8,10},{10,8},{12,... | collective-permute-start | bytes 1179656 | tf_op jit(solution)/shard_map/ppermute | solution.py:79
  93.9 3.5 %collective-permute-start.25 = (f32[1,2,128]{2,1,0:T(2,128)S(1)}, f32[1,2,128]{2,1,0:T(2,128)S(1)}, u32[]{:S(2)}, u32[]{:S(2)}) collective-permute-start(f32[1,2,128]{2,1,0:T(2,128)S(1)} %bitcast.43), channel_id=1, source_target_pairs={{16,0},{72,8},{32,16},{88,24},{48,32},{104,40},{0,48},{120,56},{80... | collective-permute-start | bytes 3080 | tf_op jit(solution)/shard_map/ppermute | solution.py:32
  94.0 4.4 %collective-permute-start.26 = (f32[1,2,128]{2,1,0:T(2,128)S(1)}, f32[1,2,128]{2,1,0:T(2,128)S(1)}, u32[]{:S(2)}, u32[]{:S(2)}) collective-permute-start(f32[1,2,128]{2,1,0:T(2,128)S(1)} %bitcast.44), channel_id=1, source_target_pairs={{32,0},{136,8},{48,16},{152,24},{0,32},{168,40},{16,48},{184,56},{... | collective-permute-start | bytes 3080 | tf_op jit(solution)/shard_map/ppermute | solution.py:32
  96.4 3.9 %collective-permute-start.27 = (f32[1,2,128]{2,1,0:T(2,128)S(1)}, f32[1,2,128]{2,1,0:T(2,128)S(1)}, u32[]{:S(2)}, u32[]{:S(2)}) collective-permute-start(f32[1,2,128]{2,1,0:T(2,128)S(1)} %bitcast.45), channel_id=1, source_target_pairs={{48,0},{200,8},{0,16},{216,24},{16,32},{232,40},{32,48},{248,56},{... | collective-permute-start | bytes 3080 | tf_op jit(solution)/shard_map/ppermute | solution.py:32
  97.4 8.5 %collective-permute-start.22 = (f16[24,32,128]{2,1,0:T(8,128)(2,1)S(1)}, f16[24,32,128]{2,1,0:T(8,128)(2,1)S(1)}, u32[]{:S(2)}, u32[]{:S(2)}) collective-permute-start(f16[24,32,128]{2,1,0:T(8,128)(2,1)S(1)} %get-tuple-element.46), channel_id=1, source_target_pairs={{0,4},{2,6},{4,0},{6,2},{1,5},{3,7},{5,1},{7,3},{8,12},{10,14},{12... | collective-permute-start | bytes 589832 | tf_op jit(solution)/shard_map/ppermute | solution.py:79
  100.4 6.6 %collective-permute-start.28 = (f32[4,2,128]{2,1,0:T(2,128)S(1)}, f32[4,2,128]{2,1,0:T(2,128)S(1)}, u32[]{:S(2)}, u32[]{:S(2)}) collective-permute-start(f32[4,2,128]{2,1,0:T(2,128)S(1)} %pad_maximum_fusion.2), channel_id=1, source_target_pairs={{64,0},{24,8},{80,16},{40,24},{96,32},{56,40},{112,48},{8,56},{128... | collective-permute-start | bytes 12296 | tf_op jit(solution)/shard_map/ppermute | solution.py:32
  101.7 5.3 %collective-permute-start.29 = (f32[4,2,128]{2,1,0:T(2,128)S(1)}, f32[4,2,128]{2,1,0:T(2,128)S(1)}, u32[]{:S(2)}, u32[]{:S(2)}) collective-permute-start(f32[4,2,128]{2,1,0:T(2,128)S(1)} %pad_maximum_fusion.2), channel_id=1, source_target_pairs={{128,0},{40,8},{144,16},{56,24},{160,32},{8,40},{176,48},{24,56},{... | collective-permute-start | bytes 12296 | tf_op jit(solution)/shard_map/ppermute | solution.py:32
  104.6 3.8 %collective-permute-start.30 = (f32[4,2,128]{2,1,0:T(2,128)S(1)}, f32[4,2,128]{2,1,0:T(2,128)S(1)}, u32[]{:S(2)}, u32[]{:S(2)}) collective-permute-start(f32[4,2,128]{2,1,0:T(2,128)S(1)} %pad_maximum_fusion.2), channel_id=1, source_target_pairs={{192,0},{56,8},{208,16},{8,24},{224,32},{24,40},{240,48},{40,56},{... | collective-permute-start | bytes 12296 | tf_op jit(solution)/shard_map/ppermute | solution.py:32
  104.6 13.4 %collective-permute-start.24 = (f16[24,32,128]{2,1,0:T(8,128)(2,1)S(1)}, f16[24,32,128]{2,1,0:T(8,128)(2,1)S(1)}, u32[]{:S(2)}, u32[]{:S(2)}) collective-permute-start(f16[24,32,128]{2,1,0:T(8,128)(2,1)S(1)} %fusion.6), channel_id=1, source_target_pairs={{0,4},{2,6},{4,0},{6,2},{1,5},{3,7},{5,1},{7,3},{8,12},{10,14},{12... | collective-permute-start | bytes 589832 | tf_op jit(solution)/shard_map/ppermute | solution.py:79
  108.5 8.9 %collective-permute-start.31 = (f32[16,2,128]{2,1,0:T(2,128)S(1)}, f32[16,2,128]{2,1,0:T(2,128)S(1)}, u32[]{:S(2)}, u32[]{:S(2)}) collective-permute-start(f32[16,2,128]{2,1,0:T(2,128)S(1)} %pad_maximum_fusion.1), channel_id=1, source_target_pairs={{8,0},{0,8},{24,16},{16,24},{40,32},{32,40},{56,48},{48,56},{72,64... | collective-permute-start | bytes 49160 | tf_op jit(solution)/shard_map/ppermute | solution.py:32
  (16 other events, 192.2 us)
where the time goes:
time: 121 us; the launch traced here: 120 us
  starting transfers between devices  48.4 us (40%)
  waiting for transfers between devices  30.1 us (25%)
  Pallas kernels  21.8 us (18%)
  other arithmetic  10.8 us (9%)
  local copies, waits for them, and re-layouts  8.03 us (7%)
    ppermute x23, starting transfers between devices, permute_doc(): return lax.ppermute(value, 'doc', moves)  36 us
    ppermute x23, waiting for transfers between devices, permute_doc(): return lax.ppermute(value, 'doc', moves)  30 us
    pallas_call x3, Pallas kernels, gram_chunk(): pl.pallas_call(kernel, in_specs=[smem] * 4 + [vmem] * n_term + [anywhere]...  17.3 us
    ppermute x9, starting transfers between devices, swap_term(): return lax.ppermute(value, 'term', [(a, a ^ bit) for a in range(n_term)])  12.4 us
    another operation x3, other arithmetic  4.32 us
    pallas_call x1, Pallas kernels, weigh(): pl.pallas_call(kernel, in_specs=[smem, vmem, vmem, vmem], out_specs=[vmem...  2.54 us
  transfers between devices with their start and end apart: 32, of which 12 were waited for; matrix products, arithmetic and copies ran while one was open for 12% of the time, Pallas kernels for 12%

commit v1 on v0

--- a/solution.py
+++ b/solution.py
@@ -51,14 +51,18 @@
     return jnp.concatenate([value, from_sibling(value)], axis=0)
 
 
-def gather_rest(ring):
-    half = ring.shape[0] // 2
-    ahead = from_ring(ring, 1, 1)
-    behind = from_ring(ring, 1, 3)
-    across_low = from_ring(ahead[:half], 1, 1)
-    across_high = from_ring(behind[half:], 1, 3)
-    own = [ring, ahead, behind, across_low, across_high]
-    return own + [from_sibling(piece) for piece in own]
+def gather_rest(low, high):
+    ahead_low = from_ring(low, 1, 1)
+    behind_high = from_ring(high, 1, 3)
+    ahead_high = from_ring(high, 1, 1)
+    behind_low = from_ring(low, 1, 3)
+    across_low = from_ring(ahead_low, 1, 1)
+    across_high = from_ring(behind_high, 1, 3)
+    early = [low, high]
+    late = [ahead_low, ahead_high, across_low, across_high, behind_low, behind_high]
+    early_far = [from_sibling(piece) for piece in early]
+    late_far = [from_sibling(piece) for piece in late]
+    return early + late + early_far + late_far
 
 
 def place_right(doc, doc_at):
@@ -68,11 +72,8 @@
     dcore = (doc - doc_at) % CORES
     inner = jnp.where(core == 0, dx, dy)
     outer = jnp.where(core == 0, dy, dx)
-    piece = jnp.where(
-        outer == 0, 0, jnp.where(outer == 1, 1, jnp.where(outer == 3, 2, 3 + inner // (SIDE // 2)))
-    )
-    spot = jnp.where(outer == 2, inner % (SIDE // 2), inner)
-    return piece + dcore * 5, spot, (dcore * SIDE + outer) * SIDE + inner
+    piece = (dcore * SIDE + outer) * 2 + inner // 2
+    return piece, inner % 2, (dcore * SIDE + outer) * SIDE + inner
 
 
 def swap_term(value, bit, n_term):
@@ -195,13 +196,19 @@
         def fetch(k, carry):
             piece = sel_ref[3, first + k]
             spot = pl.multiple_of(sel_ref[4, first + k], SMALL_ROWS)
-            for p, ref in enumerate(piece_refs):
-
-                @pl.when(piece == p)
+            for quad in range(len(pieces) // 4):
+
+                @pl.when(piece // 4 == quad)
                 def _():
-                    pltpu.make_async_copy(
-                        ref.at[pl.ds(spot, slots * terms)], tile_buf.at[k], arrived.at[k]
-                    ).start()
+                    for p in range(4 * quad, 4 * quad + 4):
+
+                        @pl.when(piece == p)
+                        def _():
+                            pltpu.make_async_copy(
+                                piece_refs[p].at[pl.ds(spot, slots * terms)],
+                                tile_buf.at[k],
+                                arrived.at[k],
+                            ).start()
 
             return carry
 
@@ -297,10 +304,13 @@
     payload_rows = tile_rows + SMALL_ROWS
 
     payload, own_counts = prepare(counts, block_ids, live_slots, lengths)
-    ring = gather_ring(payload, 0)
-    small_own = gather_ring(ring.reshape(SIDE, payload_rows, rows)[:, tile_rows:], 1)
+    ring = [payload] + [from_ring(payload, 0, s) for s in (1, 2, 3)]
+    low = jnp.concatenate(ring[:2], axis=0)
+    high = jnp.concatenate(ring[2:], axis=0)
+    small_ring = jnp.stack([piece[tile_rows:] for piece in ring])
+    small_own = gather_ring(small_ring, 1)
     small_sibling = from_sibling(small_own)
-    pieces = gather_rest(ring)
+    pieces = gather_rest(low, high)
     all_ids, len_rows, idf_tiles, weight, square_part = weigh(
         block_ids, small_own, small_sibling, own_counts
     )

time: 121 us -> 134 us (1.11)
  the two profiles are of different devices: /device:TPU:1 before, /device:TPU:8 now
where the time goes in v1:
time: 134 us; the launch traced here: 133 us
  starting transfers between devices  53.1 us (40%)
  waiting for transfers between devices  39.4 us (29%)
  Pallas kernels  22 us (16%)
  other arithmetic  10.1 us (8%)
  local copies, waits for them, and re-layouts  7.69 us (6%)
    ppermute x28, starting transfers between devices, permute_doc(): return lax.ppermute(value, 'doc', moves)  33.3 us
    ppermute x28, waiting for transfers between devices, permute_doc(): return lax.ppermute(value, 'doc', moves)  29.9 us
    ppermute x9, starting transfers between devices, swap_term(): return lax.ppermute(value, 'term', [(a, a ^ bit) for a in range(n_term)])  19.9 us
    pallas_call x3, Pallas kernels, gram_chunk(): pl.pallas_call(kernel, in_specs=[smem] * 4 + [vmem] * n_term + [anywhere]...  17.5 us
    ppermute x9, waiting for transfers between devices, swap_term(): return lax.ppermute(value, 'term', [(a, a ^ bit) for a in range(n_term)])  9.49 us
    another operation x3, other arithmetic  3.62 us
  transfers between devices with their start and end apart: 37, of which 13 were waited for; matrix products, arithmetic and copies ran while one was open for 11% of the time, Pallas kernels for 11%

profile of v1, /device:TPU:8, one launch (start us, length us, event | category | flops | bytes accessed | tf_op | source)
XLA Modules:
  0.0 133.4 jit_solution(6139027841938476141)
XLA Ops:
  0.0 2.0 %prepare.1 = (bf16[1056,128]{1,0:T(8,128)(2,1)}, bf16[2,128,512]{2,1,0:T(8,128)(2,1)}) custom-call(s32[2,4]{1,0:T(2,128)} %own_ref.5, s32[2,4]{1,0:T(2,128)} %live_ref.1, s32[2,128]{1,0:T(2,128)} %bitcast.60, s32[2,4,128,128]{3,2,1,0:T(8,128)} %count_ref.1), custom_call_target="tpu_custom_call" | custom-call | tf_op jit(solution)/shard_map/prepare/pallas_call | solution.py:108
  3.5 2.7 %collective-permute-start.1 = (bf16[1056,128]{1,0:T(8,128)(2,1)}, bf16[1056,128]{1,0:T(8,128)(2,1)S(1)}, u32[]{:S(2)}, u32[]{:S(2)}) collective-permute-start(bf16[1056,128]{1,0:T(8,128)(2,1)} %get-tuple-element.21), channel_id=1, source_target_pairs={{32,0},{136,8},{48,16},{152,24},{0,32},{168,40},{16,48},{184,56},{... | collective-permute-start | bytes 811016 | tf_op jit(solution)/shard_map/ppermute | solution.py:32
  10.0 3.7 %collective-permute-done.1 = bf16[1056,128]{1,0:T(8,128)(2,1)S(1)} collective-permute-done((bf16[1056,128]{1,0:T(8,128)(2,1)}, bf16[1056,128]{1,0:T(8,128)(2,1)S(1)}, u32[]{:S(2)}, u32[]{:S(2)}) %collective-permute-start.1) | collective-permute-done | bytes 270368 | tf_op jit(solution)/shard_map/ppermute | solution.py:32
  13.8 1.7 %collective-permute-start.13 = (bf16[2112,128]{1,0:T(8,128)(2,1)S(1)}, bf16[2112,128]{1,0:T(8,128)(2,1)S(1)}, u32[]{:S(2)}, u32[]{:S(2)}) collective-permute-start(bf16[2112,128]{1,0:T(8,128)(2,1)S(1)} %constant_dynamic-update-slice_fusion.9.refs_8_), channel_id=1, source_target_pairs={{192,0},{56,8},{208,16},{8,24},{224,32},{24,40},{240,48},{40,56},{... | collective-permute-start | bytes 1622024 | tf_op jit(solution)/shard_map/ppermute | solution.py:32
  16.0 2.4 %collective-permute-start.10 = (bf16[2112,128]{1,0:T(8,128)(2,1)S(1)}, bf16[2112,128]{1,0:T(8,128)(2,1)S(1)}, u32[]{:S(2)}, u32[]{:S(2)}) collective-permute-start(bf16[2112,128]{1,0:T(8,128)(2,1)S(1)} %constant_dynamic-update-slice_fusion.7.refs_7_), channel_id=1, source_target_pairs={{64,0},{24,8},{80,16},{40,24},{96,32},{56,40},{112,48},{8,56},{128... | collective-permute-start | bytes 1622024 | tf_op jit(solution)/shard_map/ppermute | solution.py:32
  18.4 2.1 %collective-permute-start.3 = (bf16[4,32,128]{2,1,0:T(8,128)(2,1)S(1)}, bf16[4,32,128]{2,1,0:T(8,128)(2,1)S(1)}, u32[]{:S(2)}, u32[]{:S(2)}) collective-permute-start(bf16[4,32,128]{2,1,0:T(8,128)(2,1)S(1)} %pad_maximum_fusion), channel_id=1, source_target_pairs={{64,0},{24,8},{80,16},{40,24},{96,32},{56,40},{112,48},{8,56},{128... | collective-permute-start | bytes 98312 | tf_op jit(solution)/shard_map/ppermute | solution.py:32
  20.6 10.4 %collective-permute-done.3 = bf16[4,32,128]{2,1,0:T(8,128)(2,1)S(1)} collective-permute-done((bf16[4,32,128]{2,1,0:T(8,128)(2,1)S(1)}, bf16[4,32,128]{2,1,0:T(8,128)(2,1)S(1)}, u32[]{:S(2)}, u32[]{:S(2)}) %collective-permute-start.3) | collective-permute-done | bytes 32800 | tf_op jit(solution)/shard_map/ppermute | solution.py:32
  31.0 2.8 %collective-permute-start.4 = (bf16[4,32,128]{2,1,0:T(8,128)(2,1)S(1)}, bf16[4,32,128]{2,1,0:T(8,128)(2,1)S(1)}, u32[]{:S(2)}, u32[]{:S(2)}) collective-permute-start(bf16[4,32,128]{2,1,0:T(8,128)(2,1)S(1)} %pad_maximum_fusion), channel_id=1, source_target_pairs={{128,0},{40,8},{144,16},{56,24},{160,32},{8,40},{176,48},{24,56},{... | collective-permute-start | bytes 98312 | tf_op jit(solution)/shard_map/ppermute | solution.py:32
  33.8 2.6 %collective-permute-done.4 = bf16[4,32,128]{2,1,0:T(8,128)(2,1)S(1)} collective-permute-done((bf16[4,32,128]{2,1,0:T(8,128)(2,1)S(1)}, bf16[4,32,128]{2,1,0:T(8,128)(2,1)S(1)}, u32[]{:S(2)}, u32[]{:S(2)}) %collective-permute-start.4) | collective-permute-done | bytes 32800 | tf_op jit(solution)/shard_map/ppermute | solution.py:32
  37.8 2.5 %collective-permute-done.5 = bf16[4,32,128]{2,1,0:T(8,128)(2,1)S(1)} collective-permute-done((bf16[4,32,128]{2,1,0:T(8,128)(2,1)S(1)}, bf16[4,32,128]{2,1,0:T(8,128)(2,1)S(1)}, u32[]{:S(2)}, u32[]{:S(2)}) %collective-permute-start.5) | collective-permute-done | bytes 32800 | tf_op jit(solution)/shard_map/ppermute | solution.py:32
  42.4 2.5 %weigh.1 = (s32[32,8,128]{2,1,0:T(8,128)}, f32[32,8,128]{2,1,0:T(8,128)}, f32[8,128,128]{2,1,0:T(8,128)}, f32[2,128,512]{2,1,0:T(8,128)}, f32[2,128]{1,0:T(2,128)}) custom-call(s32[2,4]{1,0:T(2,128)} %own_ref.5, bf16[16,32,128]{2,1,0:T(8,128)(2,1)} %copy-done.9, bf16[16,32,128]{2,1,0:T(8,128)(2,1)} %copy-done.10, bf16[2,128,512]{2,1,0:T(8,128)(2,1)} %get-tuple-element.22.own_ref), custom_call_target="tpu_custom_call" | custom-call | tf_op jit(solution)/shard_map/weigh/pallas_call | solution.py:158
  44.9 1.9 %collective-permute-start.7 = (f32[2,128]{1,0:T(2,128)}, f32[2,128]{1,0:T(2,128)S(1)}, u32[]{:S(2)}, u32[]{:S(2)}) collective-permute-start(f32[2,128]{1,0:T(2,128)} %get-tuple-element.24.refs_0_), channel_id=1, source_target_pairs={{0,2},{2,0},{4,6},{6,4},{1,3},{3,1},{5,7},{7,5},{8,10},{10,8},{12,... | collective-permute-start | bytes 3080 | tf_op jit(solution)/shard_map/ppermute | solution.py:80
  46.9 1.9 %collective-permute-done.7.refs_1_ = f32[2,128]{1,0:T(2,128)S(1)} collective-permute-done((f32[2,128]{1,0:T(2,128)}, f32[2,128]{1,0:T(2,128)S(1)}, u32[]{:S(2)}, u32[]{:S(2)}) %collective-permute-start.7) | collective-permute-done | bytes 1056 | tf_op jit(solution)/shard_map/ppermute | solution.py:80
  48.7 3.3 %collective-permute-start.8 = (f32[2,128]{1,0:T(2,128)}, f32[2,128]{1,0:T(2,128)S(1)}, u32[]{:S(2)}, u32[]{:S(2)}) collective-permute-start(f32[2,128]{1,0:T(2,128)} %get-tuple-element.24.refs_0_), channel_id=1, source_target_pairs={{0,4},{2,6},{4,0},{6,2},{1,5},{3,7},{5,1},{7,3},{8,12},{10,14},{12... | collective-permute-start | bytes 3080 | tf_op jit(solution)/shard_map/ppermute | solution.py:80
  52.0 1.8 %collective-permute-done.8.refs_2_ = f32[2,128]{1,0:T(2,128)S(1)} collective-permute-done((f32[2,128]{1,0:T(2,128)}, f32[2,128]{1,0:T(2,128)S(1)}, u32[]{:S(2)}, u32[]{:S(2)}) %collective-permute-start.8) | collective-permute-done | bytes 1056 | tf_op jit(solution)/shard_map/ppermute | solution.py:80
  53.8 4.3 %collective-permute-start.9 = (f32[2,128]{1,0:T(2,128)}, f32[2,128]{1,0:T(2,128)S(1)}, u32[]{:S(2)}, u32[]{:S(2)}) collective-permute-start(f32[2,128]{1,0:T(2,128)} %get-tuple-element.24.refs_0_), channel_id=1, source_target_pairs={{0,6},{2,4},{4,2},{6,0},{1,7},{3,5},{5,3},{7,1},{8,14},{10,12},{12... | collective-permute-start | bytes 3080 | tf_op jit(solution)/shard_map/ppermute | solution.py:80
  58.0 1.8 %collective-permute-done.9.refs_3_ = f32[2,128]{1,0:T(2,128)S(1)} collective-permute-done((f32[2,128]{1,0:T(2,128)}, f32[2,128]{1,0:T(2,128)S(1)}, u32[]{:S(2)}, u32[]{:S(2)}) %collective-permute-start.9) | collective-permute-done | bytes 1056 | tf_op jit(solution)/shard_map/ppermute | solution.py:80
  63.7 6.1 %collective-permute-done.14.refs_12_ = bf16[2112,128]{1,0:T(8,128)(2,1)} collective-permute-done((bf16[2112,128]{1,0:T(8,128)(2,1)S(1)}, bf16[2112,128]{1,0:T(8,128)(2,1)}, u32[]{:S(2)}, u32[]{:S(2)}) %collective-permute-start.14) | collective-permute-done | bytes 540704 | tf_op jit(solution)/shard_map/ppermute | solution.py:32
  73.6 1.5 %slice_reduce_fusion = s32[32,8]{1,0:T(8,128)S(1)} fusion(s32[32,8,128]{2,1,0:T(8,128)} %get-tuple-element.23), kind=kLoop, calls=%fused_computation.23 | loop fusion | bytes 2048 | tf_op jit(solution)/shard_map/slice | solution.py:317
  76.0 5.1 %gram.3 = f32[4,16,32,128]{3,2,1,0:T(8,128)} custom-call(s32[5,64]{1,0:T(8,128)} %stack.23.sel_ref, s32[2,4]{1,0:T(2,128)} %own_ref.5, s32[256]{0:T(256)} %reshape_squeeze.3.ids_ref, s32[4]{0:T(128)} %fusion.16.order_ref, f32[2,128]{1,0:T(2,128)} %get-tuple-element.24.refs_0_, f32[2,128]{1,0:T(2,128)} %copy-done.12, f32[2,128]{1,0:T(2,128)} %copy-done.13, ...), custom_call_target="tpu_custom_call" | custom-call | tf_op jit(solution)/shard_map/gram/pallas_call | solution.py:277
  83.0 6.3 %gram.4 = f32[4,24,32,128]{3,2,1,0:T(8,128)} custom-call(s32[5,64]{1,0:T(8,128)} %stack.23.sel_ref, s32[2,4]{1,0:T(2,128)} %own_ref.5, s32[256]{0:T(256)} %reshape_squeeze.3.ids_ref, s32[4]{0:T(128)} %fusion.16.order_ref, f32[2,128]{1,0:T(2,128)} %get-tuple-element.24.refs_0_, f32[2,128]{1,0:T(2,128)} %copy-done.12, f32[2,128]{1,0:T(2,128)} %copy-done.13, ...), custom_call_target="tpu_custom_call" | custom-call | tf_op jit(solution)/shard_map/gram/pallas_call | solution.py:277
  90.5 2.1 %collective-permute-start.26 = (f16[2,24,32,128]{3,2,1,0:T(8,128)(2,1)S(1)}, f16[2,24,32,128]{3,2,1,0:T(8,128)(2,1)S(1)}, u32[]{:S(2)}, u32[]{:S(2)}) collective-permute-start(f16[2,24,32,128]{3,2,1,0:T(8,128)(2,1)S(1)} %slice_convert_fusion.1), channel_id=1, source_target_pairs={{0,2},{2,0},{4,6},{6,4},{1,3},{3,1},{5,7},{7,5},{8,10},{10,8},{12,... | collective-permute-start | bytes 1179656 | tf_op jit(solution)/shard_map/ppermute | solution.py:80
  93.3 2.4 %collective-permute-start.25 = (f16[16,32,128]{2,1,0:T(8,128)(2,1)}, f16[16,32,128]{2,1,0:T(8,128)(2,1)}, u32[]{:S(2)}, u32[]{:S(2)}) collective-permute-start(f16[16,32,128]{2,1,0:T(8,128)(2,1)} %get-tuple-element.48), channel_id=1, source_target_pairs={{0,4},{2,6},{4,0},{6,2},{1,5},{3,7},{5,1},{7,3},{8,12},{10,14},{12... | collective-permute-start | bytes 393224 | tf_op jit(solution)/shard_map/ppermute | solution.py:80
  95.7 6.1 %gram.5 = f32[4,24,32,128]{3,2,1,0:T(8,128)} custom-call(s32[5,64]{1,0:T(8,128)} %stack.23.sel_ref, s32[2,4]{1,0:T(2,128)} %own_ref.5, s32[256]{0:T(256)} %reshape_squeeze.3.ids_ref, s32[4]{0:T(128)} %fusion.16.order_ref, f32[2,128]{1,0:T(2,128)} %get-tuple-element.24.refs_0_, f32[2,128]{1,0:T(2,128)} %copy-done.12, f32[2,128]{1,0:T(2,128)} %copy-done.13, ...), custom_call_target="tpu_custom_call" | custom-call | tf_op jit(solution)/shard_map/gram/pallas_call | solution.py:277
  103.1 2.1 %collective-permute-start.28 = (f16[2,24,32,128]{3,2,1,0:T(8,128)(2,1)S(1)}, f16[2,24,32,128]{3,2,1,0:T(8,128)(2,1)S(1)}, u32[]{:S(2)}, u32[]{:S(2)}) collective-permute-start(f16[2,24,32,128]{3,2,1,0:T(8,128)(2,1)S(1)} %slice_convert_fusion), channel_id=1, source_target_pairs={{0,2},{2,0},{4,6},{6,4},{1,3},{3,1},{5,7},{7,5},{8,10},{10,8},{12,... | collective-permute-start | bytes 1179656 | tf_op jit(solution)/shard_map/ppermute | solution.py:80
  106.6 1.9 %collective-permute-start.30 = (f32[1,2,128]{2,1,0:T(2,128)S(1)}, f32[1,2,128]{2,1,0:T(2,128)S(1)}, u32[]{:S(2)}, u32[]{:S(2)}) collective-permute-start(f32[1,2,128]{2,1,0:T(2,128)S(1)} %bitcast.56), channel_id=1, source_target_pairs={{16,0},{72,8},{32,16},{88,24},{48,32},{104,40},{0,48},{120,56},{80... | collective-permute-start | bytes 3080 | tf_op jit(solution)/shard_map/ppermute | solution.py:32
  110.4 2.0 %collective-permute-start.27 = (f16[24,32,128]{2,1,0:T(8,128)(2,1)S(1)}, f16[24,32,128]{2,1,0:T(8,128)(2,1)S(1)}, u32[]{:S(2)}, u32[]{:S(2)}) collective-permute-start(f16[24,32,128]{2,1,0:T(8,128)(2,1)S(1)} %get-tuple-element.45), channel_id=1, source_target_pairs={{0,4},{2,6},{4,0},{6,2},{1,5},{3,7},{5,1},{7,3},{8,12},{10,14},{12... | collective-permute-start | bytes 589832 | tf_op jit(solution)/shard_map/ppermute | solution.py:80
  114.3 3.8 %collective-permute-start.33 = (f32[4,2,128]{2,1,0:T(2,128)S(1)}, f32[4,2,128]{2,1,0:T(2,128)S(1)}, u32[]{:S(2)}, u32[]{:S(2)}) collective-permute-start(f32[4,2,128]{2,1,0:T(2,128)S(1)} %pad_maximum_fusion.2), channel_id=1, source_target_pairs={{64,0},{24,8},{80,16},{40,24},{96,32},{56,40},{112,48},{8,56},{128... | collective-permute-start | bytes 12296 | tf_op jit(solution)/shard_map/ppermute | solution.py:32
  118.1 2.6 %collective-permute-start.34 = (f32[4,2,128]{2,1,0:T(2,128)S(1)}, f32[4,2,128]{2,1,0:T(2,128)S(1)}, u32[]{:S(2)}, u32[]{:S(2)}) collective-permute-start(f32[4,2,128]{2,1,0:T(2,128)S(1)} %pad_maximum_fusion.2), channel_id=1, source_target_pairs={{128,0},{40,8},{144,16},{56,24},{160,32},{8,40},{176,48},{24,56},{... | collective-permute-start | bytes 12296 | tf_op jit(solution)/shard_map/ppermute | solution.py:32
  120.7 2.6 %collective-permute-start.35 = (f32[4,2,128]{2,1,0:T(2,128)S(1)}, f32[4,2,128]{2,1,0:T(2,128)S(1)}, u32[]{:S(2)}, u32[]{:S(2)}) collective-permute-start(f32[4,2,128]{2,1,0:T(2,128)S(1)} %pad_maximum_fusion.2), channel_id=1, source_target_pairs={{192,0},{56,8},{208,16},{8,24},{224,32},{24,40},{240,48},{40,56},{... | collective-permute-start | bytes 12296 | tf_op jit(solution)/shard_map/ppermute | solution.py:32
  123.3 1.7 %collective-permute-start.29 = (f16[24,32,128]{2,1,0:T(8,128)(2,1)}, f16[24,32,128]{2,1,0:T(8,128)(2,1)S(1)}, u32[]{:S(2)}, u32[]{:S(2)}) collective-permute-start(f16[24,32,128]{2,1,0:T(8,128)(2,1)} %fusion.6), channel_id=1, source_target_pairs={{0,4},{2,6},{4,0},{6,2},{1,5},{3,7},{5,1},{7,3},{8,12},{10,14},{12... | collective-permute-start | bytes 589832 | tf_op jit(solution)/shard_map/ppermute | solution.py:80
  128.1 4.1 %collective-permute-done.29 = f16[24,32,128]{2,1,0:T(8,128)(2,1)S(1)} collective-permute-done((f16[24,32,128]{2,1,0:T(8,128)(2,1)}, f16[24,32,128]{2,1,0:T(8,128)(2,1)S(1)}, u32[]{:S(2)}, u32[]{:S(2)}) %collective-permute-start.29) | collective-permute-done | bytes 196640 | tf_op jit(solution)/shard_map/ppermute | solution.py:80
  (127 shorter events, 31.6 us)
Async XLA Ops:
  2.0 11.8 %collective-permute-start.2 = (bf16[1056,128]{1,0:T(8,128)(2,1)}, bf16[1056,128]{1,0:T(8,128)(2,1)S(1)}, u32[]{:S(2)}, u32[]{:S(2)}) collective-permute-start(bf16[1056,128]{1,0:T(8,128)(2,1)} %get-tuple-element.21), channel_id=1, source_target_pairs={{48,0},{200,8},{0,16},{216,24},{16,32},{232,40},{32,48},{248,56},{... | collective-permute-start | bytes 811016 | tf_op jit(solution)/shard_map/ppermute | solution.py:32
  3.5 10.3 %collective-permute-start.1 = (bf16[1056,128]{1,0:T(8,128)(2,1)}, bf16[1056,128]{1,0:T(8,128)(2,1)S(1)}, u32[]{:S(2)}, u32[]{:S(2)}) collective-permute-start(bf16[1056,128]{1,0:T(8,128)(2,1)} %get-tuple-element.21), channel_id=1, source_target_pairs={{32,0},{136,8},{48,16},{152,24},{0,32},{168,40},{16,48},{184,56},{... | collective-permute-start | bytes 811016 | tf_op jit(solution)/shard_map/ppermute | solution.py:32
  6.2 9.7 %collective-permute-start = (bf16[1056,128]{1,0:T(8,128)(2,1)}, bf16[1056,128]{1,0:T(8,128)(2,1)S(1)}, u32[]{:S(2)}, u32[]{:S(2)}) collective-permute-start(bf16[1056,128]{1,0:T(8,128)(2,1)} %get-tuple-element.21), channel_id=1, source_target_pairs={{16,0},{72,8},{32,16},{88,24},{48,32},{104,40},{0,48},{120,56},{80... | collective-permute-start | bytes 811016 | tf_op jit(solution)/shard_map/ppermute | solution.py:32
  13.8 46.0 %collective-permute-start.13 = (bf16[2112,128]{1,0:T(8,128)(2,1)S(1)}, bf16[2112,128]{1,0:T(8,128)(2,1)S(1)}, u32[]{:S(2)}, u32[]{:S(2)}) collective-permute-start(bf16[2112,128]{1,0:T(8,128)(2,1)S(1)} %constant_dynamic-update-slice_fusion.9.refs_8_), channel_id=1, source_target_pairs={{192,0},{56,8},{208,16},{8,24},{224,32},{24,40},{240,48},{40,56},{... | collective-permute-start | bytes 1622024 | tf_op jit(solution)/shard_map/ppermute | solution.py:32
  15.5 46.2 %collective-permute-start.11 = (bf16[2112,128]{1,0:T(8,128)(2,1)S(1)}, bf16[2112,128]{1,0:T(8,128)(2,1)S(1)}, u32[]{:S(2)}, u32[]{:S(2)}) collective-permute-start(bf16[2112,128]{1,0:T(8,128)(2,1)S(1)} %constant_dynamic-update-slice_fusion.9.refs_8_), channel_id=1, source_target_pairs={{64,0},{24,8},{80,16},{40,24},{96,32},{56,40},{112,48},{8,56},{128... | collective-permute-start | bytes 1622024 | tf_op jit(solution)/shard_map/ppermute | solution.py:32
  16.0 44.3 %collective-permute-start.10 = (bf16[2112,128]{1,0:T(8,128)(2,1)S(1)}, bf16[2112,128]{1,0:T(8,128)(2,1)S(1)}, u32[]{:S(2)}, u32[]{:S(2)}) collective-permute-start(bf16[2112,128]{1,0:T(8,128)(2,1)S(1)} %constant_dynamic-update-slice_fusion.7.refs_7_), channel_id=1, source_target_pairs={{64,0},{24,8},{80,16},{40,24},{96,32},{56,40},{112,48},{8,56},{128... | collective-permute-start | bytes 1622024 | tf_op jit(solution)/shard_map/ppermute | solution.py:32
  18.4 43.3 %collective-permute-start.15 = (bf16[2112,128]{1,0:T(8,128)(2,1)S(1)}, bf16[2112,128]{1,0:T(8,128)(2,1)S(1)}, u32[]{:S(2)}, u32[]{:S(2)}) collective-permute-start(bf16[2112,128]{1,0:T(8,128)(2,1)S(1)} %constant_dynamic-update-slice_fusion.7.refs_7_), channel_id=1, source_target_pairs={{192,0},{56,8},{208,16},{8,24},{224,32},{24,40},{240,48},{40,56},{... | collective-permute-start | bytes 1622024 | tf_op jit(solution)/shard_map/ppermute | solution.py:32
  18.4 12.5 %collective-permute-start.3 = (bf16[4,32,128]{2,1,0:T(8,128)(2,1)S(1)}, bf16[4,32,128]{2,1,0:T(8,128)(2,1)S(1)}, u32[]{:S(2)}, u32[]{:S(2)}) collective-permute-start(bf16[4,32,128]{2,1,0:T(8,128)(2,1)S(1)} %pad_maximum_fusion), channel_id=1, source_target_pairs={{64,0},{24,8},{80,16},{40,24},{96,32},{56,40},{112,48},{8,56},{128... | collective-permute-start | bytes 98312 | tf_op jit(solution)/shard_map/ppermute | solution.py:32
  31.0 5.4 %collective-permute-start.4 = (bf16[4,32,128]{2,1,0:T(8,128)(2,1)S(1)}, bf16[4,32,128]{2,1,0:T(8,128)(2,1)S(1)}, u32[]{:S(2)}, u32[]{:S(2)}) collective-permute-start(bf16[4,32,128]{2,1,0:T(8,128)(2,1)S(1)} %pad_maximum_fusion), channel_id=1, source_target_pairs={{128,0},{40,8},{144,16},{56,24},{160,32},{8,40},{176,48},{24,56},{... | collective-permute-start | bytes 98312 | tf_op jit(solution)/shard_map/ppermute | solution.py:32
  36.4 3.9 %collective-permute-start.5 = (bf16[4,32,128]{2,1,0:T(8,128)(2,1)S(1)}, bf16[4,32,128]{2,1,0:T(8,128)(2,1)S(1)}, u32[]{:S(2)}, u32[]{:S(2)}) collective-permute-start(bf16[4,32,128]{2,1,0:T(8,128)(2,1)S(1)} %pad_maximum_fusion), channel_id=1, source_target_pairs={{192,0},{56,8},{208,16},{8,24},{224,32},{24,40},{240,48},{40,56},{... | collective-permute-start | bytes 98312 | tf_op jit(solution)/shard_map/ppermute | solution.py:32
  48.7 5.0 %collective-permute-start.8 = (f32[2,128]{1,0:T(2,128)}, f32[2,128]{1,0:T(2,128)S(1)}, u32[]{:S(2)}, u32[]{:S(2)}) collective-permute-start(f32[2,128]{1,0:T(2,128)} %get-tuple-element.24.refs_0_), channel_id=1, source_target_pairs={{0,4},{2,6},{4,0},{6,2},{1,5},{3,7},{5,1},{7,3},{8,12},{10,14},{12... | collective-permute-start | bytes 3080 | tf_op jit(solution)/shard_map/ppermute | solution.py:80
  53.8 6.0 %collective-permute-start.9 = (f32[2,128]{1,0:T(2,128)}, f32[2,128]{1,0:T(2,128)S(1)}, u32[]{:S(2)}, u32[]{:S(2)}) collective-permute-start(f32[2,128]{1,0:T(2,128)} %get-tuple-element.24.refs_0_), channel_id=1, source_target_pairs={{0,6},{2,4},{4,2},{6,0},{1,7},{3,5},{5,3},{7,1},{8,14},{10,12},{12... | collective-permute-start | bytes 3080 | tf_op jit(solution)/shard_map/ppermute | solution.py:80
  60.3 9.5 %collective-permute-start.14 = (bf16[2112,128]{1,0:T(8,128)(2,1)S(1)}, bf16[2112,128]{1,0:T(8,128)(2,1)}, u32[]{:S(2)}, u32[]{:S(2)}) collective-permute-start(bf16[2112,128]{1,0:T(8,128)(2,1)S(1)} %collective-permute-done.13.refs_14_), channel_id=1, source_target_pairs={{192,0},{56,8},{208,16},{8,24},{224,32},{24,40},{240,48},{40,56},{... | collective-permute-start | bytes 1622024 | tf_op jit(solution)/shard_map/ppermute | solution.py:32
  61.7 9.6 %collective-permute-start.23 = (bf16[2112,128]{1,0:T(8,128)(2,1)S(1)}, bf16[2112,128]{1,0:T(8,128)(2,1)}, u32[]{:S(2)}, u32[]{:S(2)}) collective-permute-start(bf16[2112,128]{1,0:T(8,128)(2,1)S(1)} %collective-permute-done.13.refs_14_), channel_id=1, source_target_pairs={{8,0},{0,8},{24,16},{16,24},{40,32},{32,40},{56,48},{48,56},{72,64... | collective-permute-start | bytes 1622024 | tf_op jit(solution)/shard_map/ppermute | solution.py:32
  61.7 9.5 %collective-permute-start.12 = (bf16[2112,128]{1,0:T(8,128)(2,1)S(1)}, bf16[2112,128]{1,0:T(8,128)(2,1)}, u32[]{:S(2)}, u32[]{:S(2)}) collective-permute-start(bf16[2112,128]{1,0:T(8,128)(2,1)S(1)} %collective-permute-done.10.refs_9_), channel_id=1, source_target_pairs={{64,0},{24,8},{80,16},{40,24},{96,32},{56,40},{112,48},{8,56},{128... | collective-permute-start | bytes 1622024 | tf_op jit(solution)/shard_map/ppermute | solution.py:32
  62.6 13.3 %collective-permute-start.18 = (bf16[2112,128]{1,0:T(8,128)(2,1)S(1)}, bf16[2112,128]{1,0:T(8,128)(2,1)}, u32[]{:S(2)}, u32[]{:S(2)}) collective-permute-start(bf16[2112,128]{1,0:T(8,128)(2,1)S(1)} %collective-permute-done.10.refs_9_), channel_id=1, source_target_pairs={{8,0},{0,8},{24,16},{16,24},{40,32},{32,40},{56,48},{48,56},{72,64... | collective-permute-start | bytes 1622024 | tf_op jit(solution)/shard_map/ppermute | solution.py:32
  63.6 12.3 %collective-permute-start.19 = (bf16[2112,128]{1,0:T(8,128)(2,1)S(1)}, bf16[2112,128]{1,0:T(8,128)(2,1)}, u32[]{:S(2)}, u32[]{:S(2)}) collective-permute-start(bf16[2112,128]{1,0:T(8,128)(2,1)S(1)} %collective-permute-done.11.refs_10_), channel_id=1, source_target_pairs={{8,0},{0,8},{24,16},{16,24},{40,32},{32,40},{56,48},{48,56},{72,64... | collective-permute-start | bytes 1622024 | tf_op jit(solution)/shard_map/ppermute | solution.py:32
  69.8 6.1 %collective-permute-start.22 = (bf16[2112,128]{1,0:T(8,128)(2,1)S(1)}, bf16[2112,128]{1,0:T(8,128)(2,1)}, u32[]{:S(2)}, u32[]{:S(2)}) collective-permute-start(bf16[2112,128]{1,0:T(8,128)(2,1)S(1)} %collective-permute-done.15.refs_13_), channel_id=1, source_target_pairs={{8,0},{0,8},{24,16},{16,24},{40,32},{32,40},{56,48},{48,56},{72,64... | collective-permute-start | bytes 1622024 | tf_op jit(solution)/shard_map/ppermute | solution.py:32
  71.3 4.6 %collective-permute-start.21 = (bf16[2112,128]{1,0:T(8,128)(2,1)}, bf16[2112,128]{1,0:T(8,128)(2,1)}, u32[]{:S(2)}, u32[]{:S(2)}) collective-permute-start(bf16[2112,128]{1,0:T(8,128)(2,1)} %collective-permute-done.14.refs_12_), channel_id=1, source_target_pairs={{8,0},{0,8},{24,16},{16,24},{40,32},{32,40},{56,48},{48,56},{72,64... | collective-permute-start | bytes 1622024 | tf_op jit(solution)/shard_map/ppermute | solution.py:32
  71.3 4.6 %collective-permute-start.20 = (bf16[2112,128]{1,0:T(8,128)(2,1)}, bf16[2112,128]{1,0:T(8,128)(2,1)}, u32[]{:S(2)}, u32[]{:S(2)}) collective-permute-start(bf16[2112,128]{1,0:T(8,128)(2,1)} %collective-permute-done.12.refs_11_), channel_id=1, source_target_pairs={{8,0},{0,8},{24,16},{16,24},{40,32},{32,40},{56,48},{48,56},{72,64... | collective-permute-start | bytes 1622024 | tf_op jit(solution)/shard_map/ppermute | solution.py:32
  82.2 10.4 %collective-permute-start.24 = (f16[2,16,32,128]{3,2,1,0:T(8,128)(2,1)S(1)}, f16[2,16,32,128]{3,2,1,0:T(8,128)(2,1)S(1)}, u32[]{:S(2)}, u32[]{:S(2)}) collective-permute-start(f16[2,16,32,128]{3,2,1,0:T(8,128)(2,1)S(1)} %slice_convert_fusion.2), channel_id=1, source_target_pairs={{0,2},{2,0},{4,6},{6,4},{1,3},{3,1},{5,7},{7,5},{8,10},{10,8},{12,... | collective-permute-start | bytes 786440 | tf_op jit(solution)/shard_map/ppermute | solution.py:80
  90.5 14.7 %collective-permute-start.26 = (f16[2,24,32,128]{3,2,1,0:T(8,128)(2,1)S(1)}, f16[2,24,32,128]{3,2,1,0:T(8,128)(2,1)S(1)}, u32[]{:S(2)}, u32[]{:S(2)}) collective-permute-start(f16[2,24,32,128]{3,2,1,0:T(8,128)(2,1)S(1)} %slice_convert_fusion.1), channel_id=1, source_target_pairs={{0,2},{2,0},{4,6},{6,4},{1,3},{3,1},{5,7},{7,5},{8,10},{10,8},{12,... | collective-permute-start | bytes 1179656 | tf_op jit(solution)/shard_map/ppermute | solution.py:80
  93.3 30.0 %collective-permute-start.25 = (f16[16,32,128]{2,1,0:T(8,128)(2,1)}, f16[16,32,128]{2,1,0:T(8,128)(2,1)}, u32[]{:S(2)}, u32[]{:S(2)}) collective-permute-start(f16[16,32,128]{2,1,0:T(8,128)(2,1)} %get-tuple-element.48), channel_id=1, source_target_pairs={{0,4},{2,6},{4,0},{6,2},{1,5},{3,7},{5,1},{7,3},{8,12},{10,14},{12... | collective-permute-start | bytes 393224 | tf_op jit(solution)/shard_map/ppermute | solution.py:80
  103.1 10.4 %collective-permute-start.28 = (f16[2,24,32,128]{3,2,1,0:T(8,128)(2,1)S(1)}, f16[2,24,32,128]{3,2,1,0:T(8,128)(2,1)S(1)}, u32[]{:S(2)}, u32[]{:S(2)}) collective-permute-start(f16[2,24,32,128]{3,2,1,0:T(8,128)(2,1)S(1)} %slice_convert_fusion), channel_id=1, source_target_pairs={{0,2},{2,0},{4,6},{6,4},{1,3},{3,1},{5,7},{7,5},{8,10},{10,8},{12,... | collective-permute-start | bytes 1179656 | tf_op jit(solution)/shard_map/ppermute | solution.py:80
  106.6 3.8 %collective-permute-start.30 = (f32[1,2,128]{2,1,0:T(2,128)S(1)}, f32[1,2,128]{2,1,0:T(2,128)S(1)}, u32[]{:S(2)}, u32[]{:S(2)}) collective-permute-start(f32[1,2,128]{2,1,0:T(2,128)S(1)} %bitcast.56), channel_id=1, source_target_pairs={{16,0},{72,8},{32,16},{88,24},{48,32},{104,40},{0,48},{120,56},{80... | collective-permute-start | bytes 3080 | tf_op jit(solution)/shard_map/ppermute | solution.py:32
  108.5 5.1 %collective-permute-start.31 = (f32[1,2,128]{2,1,0:T(2,128)S(1)}, f32[1,2,128]{2,1,0:T(2,128)S(1)}, u32[]{:S(2)}, u32[]{:S(2)}) collective-permute-start(f32[1,2,128]{2,1,0:T(2,128)S(1)} %bitcast.57), channel_id=1, source_target_pairs={{32,0},{136,8},{48,16},{152,24},{0,32},{168,40},{16,48},{184,56},{... | collective-permute-start | bytes 3080 | tf_op jit(solution)/shard_map/ppermute | solution.py:32
  108.5 5.1 %collective-permute-start.32 = (f32[1,2,128]{2,1,0:T(2,128)S(1)}, f32[1,2,128]{2,1,0:T(2,128)S(1)}, u32[]{:S(2)}, u32[]{:S(2)}) collective-permute-start(f32[1,2,128]{2,1,0:T(2,128)S(1)} %bitcast.58), channel_id=1, source_target_pairs={{48,0},{200,8},{0,16},{216,24},{16,32},{232,40},{32,48},{248,56},{... | collective-permute-start | bytes 3080 | tf_op jit(solution)/shard_map/ppermute | solution.py:32
  110.4 14.7 %collective-permute-start.27 = (f16[24,32,128]{2,1,0:T(8,128)(2,1)S(1)}, f16[24,32,128]{2,1,0:T(8,128)(2,1)S(1)}, u32[]{:S(2)}, u32[]{:S(2)}) collective-permute-start(f16[24,32,128]{2,1,0:T(8,128)(2,1)S(1)} %get-tuple-element.45), channel_id=1, source_target_pairs={{0,4},{2,6},{4,0},{6,2},{1,5},{3,7},{5,1},{7,3},{8,12},{10,14},{12... | collective-permute-start | bytes 589832 | tf_op jit(solution)/shard_map/ppermute | solution.py:80
  114.3 11.8 %collective-permute-start.33 = (f32[4,2,128]{2,1,0:T(2,128)S(1)}, f32[4,2,128]{2,1,0:T(2,128)S(1)}, u32[]{:S(2)}, u32[]{:S(2)}) collective-permute-start(f32[4,2,128]{2,1,0:T(2,128)S(1)} %pad_maximum_fusion.2), channel_id=1, source_target_pairs={{64,0},{24,8},{80,16},{40,24},{96,32},{56,40},{112,48},{8,56},{128... | collective-permute-start | bytes 12296 | tf_op jit(solution)/shard_map/ppermute | solution.py:32
  118.1 8.1 %collective-permute-start.34 = (f32[4,2,128]{2,1,0:T(2,128)S(1)}, f32[4,2,128]{2,1,0:T(2,128)S(1)}, u32[]{:S(2)}, u32[]{:S(2)}) collective-permute-start(f32[4,2,128]{2,1,0:T(2,128)S(1)} %pad_maximum_fusion.2), channel_id=1, source_target_pairs={{128,0},{40,8},{144,16},{56,24},{160,32},{8,40},{176,48},{24,56},{... | collective-permute-start | bytes 12296 | tf_op jit(solution)/shard_map/ppermute | solution.py:32
  120.7 5.5 %collective-permute-start.35 = (f32[4,2,128]{2,1,0:T(2,128)S(1)}, f32[4,2,128]{2,1,0:T(2,128)S(1)}, u32[]{:S(2)}, u32[]{:S(2)}) collective-permute-start(f32[4,2,128]{2,1,0:T(2,128)S(1)} %pad_maximum_fusion.2), channel_id=1, source_target_pairs={{192,0},{56,8},{208,16},{8,24},{224,32},{24,40},{240,48},{40,56},{... | collective-permute-start | bytes 12296 | tf_op jit(solution)/shard_map/ppermute | solution.py:32
  123.3 8.9 %collective-permute-start.29 = (f16[24,32,128]{2,1,0:T(8,128)(2,1)}, f16[24,32,128]{2,1,0:T(8,128)(2,1)S(1)}, u32[]{:S(2)}, u32[]{:S(2)}) collective-permute-start(f16[24,32,128]{2,1,0:T(8,128)(2,1)} %fusion.6), channel_id=1, source_target_pairs={{0,4},{2,6},{4,0},{6,2},{1,5},{3,7},{5,1},{7,3},{8,12},{10,14},{12... | collective-permute-start | bytes 589832 | tf_op jit(solution)/shard_map/ppermute | solution.py:80
  (21 other events, 354.0 us)

commit v2 on v1

--- a/solution.py
+++ b/solution.py
@@ -9,7 +9,7 @@
 SIDE = 4
 CORES = 2
 UNROLL = 4
-CHUNKS = (16, 24, 24)
+CHUNKS = (24, 24, 16)
 GRAM_SCALE = 32.0
 SMALL_ROWS = 32
 
@@ -74,6 +74,11 @@
     outer = jnp.where(core == 0, dy, dx)
     piece = (dcore * SIDE + outer) * 2 + inner // 2
     return piece, inner % 2, (dcore * SIDE + outer) * SIDE + inner
+
+
+def place_owner(owner, term_at):
+    apart = owner ^ term_at
+    return (apart % 2) * 2 + apart // 2
 
 
 def swap_term(value, bit, n_term):
@@ -117,20 +122,25 @@
     )(block_ids, live_slots, lengths.reshape(blocks, rows), counts)
 
 
-def weigh(block_ids, small_own, small_sibling, own_counts):
+def weigh(block_ids, small_parts, own_counts):
     blocks, rows, width = own_counts.shape
     slots = block_ids.shape[1]
     terms = width // slots
     own_slots = blocks * slots
-    half_docs = small_own.shape[0]
-    docs_all = 2 * half_docs * blocks * rows
-
-    def kernel(ids_ref, near_ref, far_ref, own_ref, id_ref, length_ref, idf_ref, weight_ref, square_ref):
-        small = jnp.concatenate([near_ref[...], far_ref[...]], axis=0).astype(jnp.float32)
+    n_doc = len(small_parts) * small_parts[0].shape[0]
+    docs_all = n_doc * blocks * rows
+
+    def kernel(ids_ref, own_ref, *refs):
+        small_refs = refs[: len(small_parts)]
+        id_ref, length_ref, idf_ref, weight_ref, square_ref = refs[len(small_parts) :]
+        small = jnp.concatenate([ref[...].astype(jnp.float32) for ref in small_refs], axis=0)
         cols = small[:, :own_slots]
         ids = small[:, own_slots : 2 * own_slots] * 256.0 + small[:, 2 * own_slots : 3 * own_slots]
+        flat = ids.reshape(n_doc * own_slots, rows)
+        for h in range(n_doc * own_slots // rows):
+            turned = flat[h * rows : (h + 1) * rows].T
+            id_ref[h : h + 1, :] = turned[:1].astype(jnp.int32)
         ids = ids.astype(jnp.int32)
-        id_ref[...] = ids
         packed = small[:, 3 * own_slots :]
         length = packed * 256.0 + pltpu.roll(packed, packed.shape[1] - blocks, 1)
         row_at = lax.broadcasted_iota(jnp.int32, length.shape, 1)
@@ -157,28 +167,31 @@
     vmem = pl.BlockSpec(memory_space=pltpu.VMEM)
     return pl.pallas_call(
         kernel,
-        in_specs=[smem, vmem, vmem, vmem],
+        in_specs=[smem, vmem] + [vmem] * len(small_parts),
         out_specs=[vmem] * 5,
         out_shape=[
-            jax.ShapeDtypeStruct((2 * half_docs, own_slots, rows), jnp.int32),
-            jax.ShapeDtypeStruct((2 * half_docs, SMALL_ROWS - 3 * own_slots, rows), jnp.float32),
+            jax.ShapeDtypeStruct((n_doc * own_slots // rows, rows), jnp.int32),
+            jax.ShapeDtypeStruct((n_doc, SMALL_ROWS - 3 * own_slots, rows), jnp.float32),
             jax.ShapeDtypeStruct((own_slots, terms, rows), jnp.float32),
             jax.ShapeDtypeStruct((blocks, rows, width), jnp.float32),
             jax.ShapeDtypeStruct((blocks, rows), jnp.float32),
         ],
         name="weigh",
-    )(block_ids, small_own, small_sibling, own_counts)
-
-
-def gram_chunk(first, size, select, own_ids, all_ids, order, weight, squares, idf_tiles, len_rows, pieces):
+    )(block_ids, own_counts, *small_parts)
+
+
+def gram_chunk(first, size, pairs, own_ids, all_ids, weight, squares, idf_tiles, len_rows, pieces):
     own_slots, terms, rows = idf_tiles.shape
     blocks = weight.shape[0]
     slots = own_slots // blocks
-    n_term = order.shape[0]
+    n_term = len(squares)
     part = rows // n_term
     groups = size // UNROLL
-
-    def kernel(sel_ref, own_ref, ids_ref, order_ref, *refs):
+    payload_rows = pieces[0].shape[0] // 2
+
+    def kernel(pair_ref, own_ref, ids_ref, *refs):
+        doc_at = lax.axis_index("doc")
+        term_at = lax.axis_index("term")
         square_refs = refs[:n_term]
         weight_hbm, idf_hbm, length_hbm = refs[n_term : n_term + 3]
         piece_refs = refs[n_term + 3 : n_term + 3 + len(pieces)]
@@ -194,8 +207,10 @@
             load.start()
 
         def fetch(k, carry):
-            piece = sel_ref[3, first + k]
-            spot = pl.multiple_of(sel_ref[4, first + k], SMALL_ROWS)
+            right = pair_ref[first + k, 1]
+            piece, spot, _ = place_right(right // blocks, doc_at)
+            spot = spot * payload_rows + (right % blocks) * (slots * terms)
+            spot = pl.multiple_of(spot, SMALL_ROWS)
             for quad in range(len(pieces) // 4):
 
                 @pl.when(piece // 4 == quad)
@@ -233,9 +248,11 @@
                 ).wait()
             for p in range(UNROLL):
                 k = step * UNROLL + p
-                left = sel_ref[0, first + k]
-                right_doc = sel_ref[1, first + k]
-                right_block = sel_ref[2, first + k]
+                left = pair_ref[first + k, 0] - doc_at * blocks
+                right_block = pair_ref[first + k, 1] % blocks
+                _, _, right_doc = place_right(pair_ref[first + k, 1] // blocks, doc_at)
+                id_row = right_doc * own_slots // rows
+                id_at = right_doc * own_slots % rows + right_block * slots
                 len_row = length_ref[right_doc, pl.ds(right_block, 1), :]
                 parts = []
                 for i in range(slots):
@@ -243,7 +260,7 @@
                     found = jnp.int32(0)
                     place = jnp.int32(0)
                     for j in range(slots):
-                        same = ids_ref[right_doc * own_slots + right_block * slots + j] == wanted
+                        same = ids_ref[id_row, id_at + j] == wanted
                         found = jnp.where(same, 1, found)
                         place = jnp.where(same, j, place)
                     start = pl.multiple_of(place * terms, terms)
@@ -253,7 +270,7 @@
                 right_tile = jnp.concatenate(parts, axis=0)
                 gram = jnp.dot(left_ref[left], right_tile, preferred_element_type=jnp.float32)
                 for g in range(n_term):
-                    gram_ref[order_ref[g], k] = gram[g * part : (g + 1) * part]
+                    gram_ref[place_owner(g, term_at), k] = gram[g * part : (g + 1) * part]
             span = pl.ds(step * UNROLL, UNROLL)
             pltpu.make_async_copy(
                 gram_ref.at[:, span], out_hbm.at[:, span], written.at[step]
@@ -276,7 +293,7 @@
     anywhere = pl.BlockSpec(memory_space=pl.ANY)
     return pl.pallas_call(
         kernel,
-        in_specs=[smem] * 4 + [vmem] * n_term + [anywhere] * (3 + len(pieces)),
+        in_specs=[smem] * 3 + [vmem] * n_term + [anywhere] * (3 + len(pieces)),
         out_specs=anywhere,
         out_shape=jax.ShapeDtypeStruct((n_term, size, part, rows), jnp.float32),
         scratch_shapes=[
@@ -291,7 +308,7 @@
             pltpu.SemaphoreType.DMA((groups,)),
         ],
         name="gram",
-    )(select, own_ids, all_ids, order, *squares, weight, idf_tiles, len_rows, *pieces)
+    )(pairs, own_ids, all_ids, *squares, weight, idf_tiles, len_rows, *pieces)
 
 
 def whole(counts, block_ids, live_slots, lengths, pairs, pair_count):
@@ -299,60 +316,56 @@
     n_doc = lax.axis_size("doc")
     n_term = lax.axis_size("term")
     doc_at = lax.axis_index("doc")
-    term_at = lax.axis_index("term")
     tile_rows = blocks * slots * terms
-    payload_rows = tile_rows + SMALL_ROWS
 
     payload, own_counts = prepare(counts, block_ids, live_slots, lengths)
     ring = [payload] + [from_ring(payload, 0, s) for s in (1, 2, 3)]
     low = jnp.concatenate(ring[:2], axis=0)
     high = jnp.concatenate(ring[2:], axis=0)
     small_ring = jnp.stack([piece[tile_rows:] for piece in ring])
-    small_own = gather_ring(small_ring, 1)
-    small_sibling = from_sibling(small_own)
+    small_parts = [small_ring] + [from_ring(small_ring, 1, s) for s in (1, 2, 3)]
+    small_parts = small_parts + [from_sibling(part) for part in small_parts]
     pieces = gather_rest(low, high)
     all_ids, len_rows, idf_tiles, weight, square_part = weigh(
-        block_ids, small_own, small_sibling, own_counts
+        block_ids, small_parts, own_counts
     )
-    all_ids = all_ids[:, :, 0].reshape(-1)
     squares = [square_part] + [swap_term(square_part, bit, n_term) for bit in range(1, n_term)]
 
-    left_sel = pairs[:, 0] - doc_at * blocks
-    right_sel = pairs[:, 1]
-    piece, spot, right_doc = place_right(right_sel // blocks, doc_at)
-    right_block = right_sel % blocks
-    start_row = spot * payload_rows + right_block * (slots * terms)
-    select = jnp.stack([left_sel, right_doc, right_block, piece, start_row])
-    apart = jnp.arange(n_term, dtype=jnp.int32) ^ term_at
-    order = (apart % 2) * 2 + apart // 2
-    live = jnp.arange(pairs.shape[0], dtype=jnp.int32) < pair_count[0]
     kept = []
     ready = []
     first = 0
+    chosen = pairs
     for step, size in enumerate(CHUNKS):
         if step >= 2:
-            select, _ = lax.optimization_barrier((select, ready[step - 2]))
+            chosen, _ = lax.optimization_barrier((chosen, ready[step - 2]))
         grams = gram_chunk(
-            first, size, select, block_ids, all_ids, order, weight, squares, idf_tiles, len_rows, pieces
+            first, size, chosen, block_ids, all_ids, weight, squares, idf_tiles, len_rows, pieces
         )
         first += size
         near = swap_term(grams[2:].astype(jnp.float16), 1, n_term)
         pass_on = (grams[1] + near[1].astype(jnp.float32)).astype(jnp.float16)
         ready.append(pass_on)
         far = swap_term(pass_on, 2, n_term)
-        kept.append((grams[0], near[0], far))
+        kept.append((grams, near, far))
     early, _ = lax.optimization_barrier((tuple(kept[:-1]), ready[-1]))
-    totals = [
-        mine + near.astype(jnp.float32) + far.astype(jnp.float32)
-        for mine, near, far in (*early, kept[-1])
-    ]
     norm, _ = lax.optimization_barrier((lax.rsqrt(sum(squares) + epsilon), ready[-2]))
     norm_ring = gather_ring(norm[None], 0)
     norm_ring, _ = lax.optimization_barrier((norm_ring, ready[-1]))
     norm_rows = gather_sibling(gather_ring(norm_ring, 1))
-    norm_rows = norm_rows.reshape(n_doc * blocks, rows)[right_doc * blocks + right_block]
-    right_norm = jnp.where(live[:, None], norm_rows * (1.0 / GRAM_SCALE), 0.0)
-    return jnp.concatenate(totals, axis=0) * right_norm[:, None, :]
+    right = pairs[:, 1]
+    _, _, right_doc = place_right(right // blocks, doc_at)
+    norm_rows = norm_rows.reshape(n_doc * blocks, rows)[right_doc * blocks + right % blocks]
+    live = jnp.arange(pairs.shape[0], dtype=jnp.int32) < pair_count[0]
+    right_norm = jnp.where(live[:, None], norm_rows * (1.0 / GRAM_SCALE), 0.0)[:, None, :]
+
+    def total(grams, near, far):
+        return grams[0] + near[0].astype(jnp.float32) + far.astype(jnp.float32)
+
+    last = pairs.shape[0] - CHUNKS[-1]
+    result = jnp.concatenate([total(*each) for each in early], axis=0)
+    result = jnp.pad(result, ((0, CHUNKS[-1]), (0, 0), (0, 0))) * right_norm
+    result, final = lax.optimization_barrier((result, kept[-1]))
+    return result.at[last:].set(total(*final) * right_norm[last:])
 
 
 def solution(mesh):

time: 134 us -> 145 us (1.082)
  the two profiles are of different devices: /device:TPU:8 before, /device:TPU:1 now
where the time goes in v2:
time: 145 us
  starting transfers between devices  52.3 us (36%)
  waiting for transfers between devices  49.9 us (34%)
  Pallas kernels  25.5 us (18%)
  other arithmetic  11.1 us (8%)
  local copies, waits for them, and re-layouts  4.75 us (3%)
    ppermute x31, starting transfers between devices, permute_doc(): return lax.ppermute(value, 'doc', moves)  39 us
    ppermute x31, waiting for transfers between devices, permute_doc(): return lax.ppermute(value, 'doc', moves)  29.5 us
    pallas_call x3, Pallas kernels, gram_chunk(): pl.pallas_call(kernel, in_specs=[smem] * 3 + [vmem] * n_term + [anywhere]...  21 us
    ppermute x9, waiting for transfers between devices, swap_term(): return lax.ppermute(value, 'term', [(a, a ^ bit) for a in range(n_term)])  20.4 us
    ppermute x9, starting transfers between devices, swap_term(): return lax.ppermute(value, 'term', [(a, a ^ bit) for a in range(n_term)])  13.3 us
    another operation x3, other arithmetic  3.6 us
  transfers between devices with their start and end apart: 40, of which 18 were waited for; matrix products, arithmetic and copies ran while one was open for 8% of the time, Pallas kernels for 11%

profile of v2, /device:TPU:1, one launch (start us, length us, event | category | flops | bytes accessed | tf_op | source)
XLA Modules:
  0.0 144.6 jit_solution(14323606472745221032)
XLA Ops:
  0.0 2.0 %prepare.1 = (bf16[1056,128]{1,0:T(8,128)(2,1)}, bf16[2,128,512]{2,1,0:T(8,128)(2,1)}) custom-call(s32[2,4]{1,0:T(2,128)} %own_ref.5, s32[2,4]{1,0:T(2,128)} %live_ref.1, s32[2,128]{1,0:T(2,128)} %bitcast.36, s32[2,4,128,128]{3,2,1,0:T(8,128)} %count_ref.1), custom_call_target="tpu_custom_call" | custom-call | tf_op jit(solution)/shard_map/prepare/pallas_call | solution.py:113
  2.0 2.1 %collective-permute-start.2 = (bf16[1056,128]{1,0:T(8,128)(2,1)}, bf16[1056,128]{1,0:T(8,128)(2,1)S(1)}, u32[]{:S(2)}, u32[]{:S(2)}) collective-permute-start(bf16[1056,128]{1,0:T(8,128)(2,1)} %get-tuple-element.38), channel_id=1, source_target_pairs={{48,0},{200,8},{0,16},{216,24},{16,32},{232,40},{32,48},{248,56},{... | collective-permute-start | bytes 811016 | tf_op jit(solution)/shard_map/ppermute | solution.py:32
  4.1 2.6 %collective-permute-start.1 = (bf16[1056,128]{1,0:T(8,128)(2,1)}, bf16[1056,128]{1,0:T(8,128)(2,1)S(1)}, u32[]{:S(2)}, u32[]{:S(2)}) collective-permute-start(bf16[1056,128]{1,0:T(8,128)(2,1)} %get-tuple-element.38), channel_id=1, source_target_pairs={{32,0},{136,8},{48,16},{152,24},{0,32},{168,40},{16,48},{184,56},{... | collective-permute-start | bytes 811016 | tf_op jit(solution)/shard_map/ppermute | solution.py:32
  9.5 4.5 %collective-permute-done.1 = bf16[1056,128]{1,0:T(8,128)(2,1)S(1)} collective-permute-done((bf16[1056,128]{1,0:T(8,128)(2,1)}, bf16[1056,128]{1,0:T(8,128)(2,1)S(1)}, u32[]{:S(2)}, u32[]{:S(2)}) %collective-permute-start.1) | collective-permute-done | bytes 270368 | tf_op jit(solution)/shard_map/ppermute | solution.py:32
  15.1 1.8 %collective-permute-start.14 = (bf16[2112,128]{1,0:T(8,128)(2,1)S(1)}, bf16[2112,128]{1,0:T(8,128)(2,1)S(1)}, u32[]{:S(2)}, u32[]{:S(2)}) collective-permute-start(bf16[2112,128]{1,0:T(8,128)(2,1)S(1)} %constant_dynamic-update-slice_fusion.2.refs_8_), channel_id=1, source_target_pairs={{64,0},{24,8},{80,16},{40,24},{96,32},{56,40},{112,48},{8,56},{128... | collective-permute-start | bytes 1622024 | tf_op jit(solution)/shard_map/ppermute | solution.py:32
  18.4 2.3 %collective-permute-start.3 = (bf16[4,32,128]{2,1,0:T(8,128)(2,1)S(1)}, bf16[4,32,128]{2,1,0:T(8,128)(2,1)S(1)}, u32[]{:S(2)}, u32[]{:S(2)}) collective-permute-start(bf16[4,32,128]{2,1,0:T(8,128)(2,1)S(1)} %pad_maximum_fusion.refs_0_), channel_id=1, source_target_pairs={{64,0},{24,8},{80,16},{40,24},{96,32},{56,40},{112,48},{8,56},{128... | collective-permute-start | bytes 98312 | tf_op jit(solution)/shard_map/ppermute | solution.py:32
  20.7 9.1 %collective-permute-done.3.refs_1_ = bf16[4,32,128]{2,1,0:T(8,128)(2,1)S(1)} collective-permute-done((bf16[4,32,128]{2,1,0:T(8,128)(2,1)S(1)}, bf16[4,32,128]{2,1,0:T(8,128)(2,1)S(1)}, u32[]{:S(2)}, u32[]{:S(2)}) %collective-permute-start.3) | collective-permute-done | bytes 32800 | tf_op jit(solution)/shard_map/ppermute | solution.py:32
  29.8 2.4 %collective-permute-start.4 = (bf16[4,32,128]{2,1,0:T(8,128)(2,1)S(1)}, bf16[4,32,128]{2,1,0:T(8,128)(2,1)S(1)}, u32[]{:S(2)}, u32[]{:S(2)}) collective-permute-start(bf16[4,32,128]{2,1,0:T(8,128)(2,1)S(1)} %pad_maximum_fusion.refs_0_), channel_id=1, source_target_pairs={{128,0},{40,8},{144,16},{56,24},{160,32},{8,40},{176,48},{24,56},{... | collective-permute-start | bytes 98312 | tf_op jit(solution)/shard_map/ppermute | solution.py:32
  32.2 1.9 %collective-permute-done.4.refs_2_ = bf16[4,32,128]{2,1,0:T(8,128)(2,1)S(1)} collective-permute-done((bf16[4,32,128]{2,1,0:T(8,128)(2,1)S(1)}, bf16[4,32,128]{2,1,0:T(8,128)(2,1)S(1)}, u32[]{:S(2)}, u32[]{:S(2)}) %collective-permute-start.4) | collective-permute-done | bytes 32800 | tf_op jit(solution)/shard_map/ppermute | solution.py:32
  34.1 1.2 collective-permute-start.5
  35.3 2.9 %collective-permute-done.5.refs_3_ = bf16[4,32,128]{2,1,0:T(8,128)(2,1)S(1)} collective-permute-done((bf16[4,32,128]{2,1,0:T(8,128)(2,1)S(1)}, bf16[4,32,128]{2,1,0:T(8,128)(2,1)S(1)}, u32[]{:S(2)}, u32[]{:S(2)}) %collective-permute-start.5) | collective-permute-done | bytes 32800 | tf_op jit(solution)/shard_map/ppermute | solution.py:32
  38.2 5.1 %collective-permute-start.6 = (bf16[4,32,128]{2,1,0:T(8,128)(2,1)S(1)}, bf16[4,32,128]{2,1,0:T(8,128)(2,1)S(1)}, u32[]{:S(2)}, u32[]{:S(2)}) collective-permute-start(bf16[4,32,128]{2,1,0:T(8,128)(2,1)S(1)} %pad_maximum_fusion.refs_0_), channel_id=1, source_target_pairs={{8,0},{0,8},{24,16},{16,24},{40,32},{32,40},{56,48},{48,56},{72,64... | collective-permute-start | bytes 98312 | tf_op jit(solution)/shard_map/ppermute | solution.py:32
  48.5 2.5 %weigh.1 = (s32[2,128]{1,0:T(2,128)}, f32[32,8,128]{2,1,0:T(8,128)}, f32[8,128,128]{2,1,0:T(8,128)}, f32[2,128,512]{2,1,0:T(8,128)}, f32[2,128]{1,0:T(2,128)}) custom-call(s32[2,4]{1,0:T(2,128)} %own_ref.5, bf16[2,128,512]{2,1,0:T(8,128)(2,1)} %get-tuple-element.37.own_ref, bf16[4,32,128]{2,1,0:T(8,128)(2,1)} %copy-done.15, bf16[4,32,128]{2,1,0:T(8,128)(2,1)} %copy-done.16, ...), custom_call_target="tpu_custom_call" | custom-call | tf_op jit(solution)/shard_map/weigh/pallas_call | solution.py:168
  51.0 1.3 collective-permute-start.10
  52.3 1.3 collective-permute-done.10.refs_1_
  53.6 2.8 %collective-permute-start.11 = (f32[2,128]{1,0:T(2,128)}, f32[2,128]{1,0:T(2,128)S(1)}, u32[]{:S(2)}, u32[]{:S(2)}) collective-permute-start(f32[2,128]{1,0:T(2,128)} %get-tuple-element.40.refs_0_), channel_id=1, source_target_pairs={{0,4},{2,6},{4,0},{6,2},{1,5},{3,7},{5,1},{7,3},{8,12},{10,14},{12... | collective-permute-start | bytes 3080 | tf_op jit(solution)/shard_map/ppermute | solution.py:85
  57.6 3.5 %collective-permute-start.12 = (f32[2,128]{1,0:T(2,128)}, f32[2,128]{1,0:T(2,128)S(1)}, u32[]{:S(2)}, u32[]{:S(2)}) collective-permute-start(f32[2,128]{1,0:T(2,128)} %get-tuple-element.40.refs_0_), channel_id=1, source_target_pairs={{0,6},{2,4},{4,2},{6,0},{1,7},{3,5},{5,3},{7,1},{8,14},{10,12},{12... | collective-permute-start | bytes 3080 | tf_op jit(solution)/shard_map/ppermute | solution.py:85
  62.4 3.5 %collective-permute-start.20 = (bf16[2112,128]{1,0:T(8,128)(2,1)S(1)}, bf16[2112,128]{1,0:T(8,128)(2,1)S(1)}, u32[]{:S(2)}, u32[]{:S(2)}) collective-permute-start(bf16[2112,128]{1,0:T(8,128)(2,1)S(1)} %constant_dynamic-update-slice_fusion.2.refs_8_), channel_id=1, source_target_pairs={{8,0},{0,8},{24,16},{16,24},{40,32},{32,40},{56,48},{48,56},{72,64... | collective-permute-start | bytes 1622024 | tf_op jit(solution)/shard_map/ppermute | solution.py:32
  66.0 2.7 %collective-permute-start.15 = (bf16[2112,128]{1,0:T(8,128)(2,1)S(1)}, bf16[2112,128]{1,0:T(8,128)(2,1)}, u32[]{:S(2)}, u32[]{:S(2)}) collective-permute-start(bf16[2112,128]{1,0:T(8,128)(2,1)S(1)} %collective-permute-done.13.refs_9_), channel_id=1, source_target_pairs={{64,0},{24,8},{80,16},{40,24},{96,32},{56,40},{112,48},{8,56},{128... | collective-permute-start | bytes 1622024 | tf_op jit(solution)/shard_map/ppermute | solution.py:32
  70.2 5.6 %collective-permute-done.17.refs_12_ = bf16[2112,128]{1,0:T(8,128)(2,1)} collective-permute-done((bf16[2112,128]{1,0:T(8,128)(2,1)S(1)}, bf16[2112,128]{1,0:T(8,128)(2,1)}, u32[]{:S(2)}, u32[]{:S(2)}) %collective-permute-start.17) | collective-permute-done | bytes 540704 | tf_op jit(solution)/shard_map/ppermute | solution.py:32
  75.8 1.3 collective-permute-start.25
  80.6 7.5 %gram.3 = f32[4,24,32,128]{3,2,1,0:T(8,128)} custom-call(s32[64,2]{1,0:T(8,128)} %copy.7.pair_ref, s32[2,4]{1,0:T(2,128)} %own_ref.5, s32[2,128]{1,0:T(2,128)} %get-tuple-element.39.ids_ref, f32[2,128]{1,0:T(2,128)} %get-tuple-element.40.refs_0_, f32[2,128]{1,0:T(2,128)} %copy-done.24, f32[2,128]{1,0:T(2,128)} %copy-done.25, f32[2,128]{1,0:T(2,128)} %copy-done.26, ...), custom_call_target="tpu_custom_call" | custom-call | tf_op jit(solution)/shard_map/gram/pallas_call | solution.py:294
  88.1 1.2 slice_convert_fusion.1
  90.2 7.6 %gram.4 = f32[4,24,32,128]{3,2,1,0:T(8,128)} custom-call(s32[64,2]{1,0:T(8,128)} %copy.7.pair_ref, s32[2,4]{1,0:T(2,128)} %own_ref.5, s32[2,128]{1,0:T(2,128)} %get-tuple-element.39.ids_ref, f32[2,128]{1,0:T(2,128)} %get-tuple-element.40.refs_0_, f32[2,128]{1,0:T(2,128)} %copy-done.24, f32[2,128]{1,0:T(2,128)} %copy-done.25, f32[2,128]{1,0:T(2,128)} %copy-done.26, ...), custom_call_target="tpu_custom_call" | custom-call | tf_op jit(solution)/shard_map/gram/pallas_call | solution.py:294
  98.9 1.5 %collective-permute-start.29 = (f16[2,24,32,128]{3,2,1,0:T(8,128)(2,1)S(1)}, f16[2,24,32,128]{3,2,1,0:T(8,128)(2,1)S(1)}, u32[]{:S(2)}, u32[]{:S(2)}) collective-permute-start(f16[2,24,32,128]{3,2,1,0:T(8,128)(2,1)S(1)} %slice_convert_fusion), channel_id=1, source_target_pairs={{0,2},{2,0},{4,6},{6,4},{1,3},{3,1},{5,7},{7,5},{8,10},{10,8},{12,... | collective-permute-start | bytes 1179656 | tf_op jit(solution)/shard_map/ppermute | solution.py:85
  102.0 5.9 %gram.5 = f32[4,16,32,128]{3,2,1,0:T(8,128)} custom-call(s32[64,2]{1,0:T(8,128)} %copy.9.pair_ref, s32[2,4]{1,0:T(2,128)} %own_ref.5, s32[2,128]{1,0:T(2,128)} %get-tuple-element.39.ids_ref, f32[2,128]{1,0:T(2,128)} %get-tuple-element.40.refs_0_, f32[2,128]{1,0:T(2,128)} %copy-done.24, f32[2,128]{1,0:T(2,128)} %copy-done.25, f32[2,128]{1,0:T(2,128)} %copy-done.26, ...), custom_call_target="tpu_custom_call" | custom-call | tf_op jit(solution)/shard_map/gram/pallas_call | solution.py:294
  110.5 2.3 %collective-permute-start.32 = (f32[1,2,128]{2,1,0:T(2,128)S(1)}, f32[1,2,128]{2,1,0:T(2,128)S(1)}, u32[]{:S(2)}, u32[]{:S(2)}) collective-permute-start(f32[1,2,128]{2,1,0:T(2,128)S(1)} %bitcast.32), channel_id=1, source_target_pairs={{16,0},{72,8},{32,16},{88,24},{48,32},{104,40},{0,48},{120,56},{80... | collective-permute-start | bytes 3080 | tf_op jit(solution)/shard_map/ppermute | solution.py:32
  113.4 3.7 %collective-permute-start.30 = (f16[24,32,128]{2,1,0:T(8,128)(2,1)S(1)}, f16[24,32,128]{2,1,0:T(8,128)(2,1)S(1)}, u32[]{:S(2)}, u32[]{:S(2)}) collective-permute-start(f16[24,32,128]{2,1,0:T(8,128)(2,1)S(1)} %fusion.7), channel_id=1, source_target_pairs={{0,4},{2,6},{4,0},{6,2},{1,5},{3,7},{5,1},{7,3},{8,12},{10,14},{12... | collective-permute-start | bytes 589832 | tf_op jit(solution)/shard_map/ppermute | solution.py:85
  119.5 11.0 %collective-permute-done.30 = f16[24,32,128]{2,1,0:T(8,128)(2,1)S(1)} collective-permute-done((f16[24,32,128]{2,1,0:T(8,128)(2,1)S(1)}, f16[24,32,128]{2,1,0:T(8,128)(2,1)S(1)}, u32[]{:S(2)}, u32[]{:S(2)}) %collective-permute-start.30) | collective-permute-done | bytes 196640 | tf_op jit(solution)/shard_map/ppermute | solution.py:85
  130.6 5.6 %collective-permute-done.28 = f16[24,32,128]{2,1,0:T(8,128)(2,1)S(1)} collective-permute-done((f16[24,32,128]{2,1,0:T(8,128)(2,1)}, f16[24,32,128]{2,1,0:T(8,128)(2,1)S(1)}, u32[]{:S(2)}, u32[]{:S(2)}) %collective-permute-start.28) | collective-permute-done | bytes 196640 | tf_op jit(solution)/shard_map/ppermute | solution.py:85
  137.4 2.9 %collective-permute-start.38 = (f32[16,2,128]{2,1,0:T(2,128)S(1)}, f32[16,2,128]{2,1,0:T(2,128)S(1)}, u32[]{:S(2)}, u32[]{:S(2)}) collective-permute-start(f32[16,2,128]{2,1,0:T(2,128)S(1)} %pad_maximum_fusion.1), channel_id=1, source_target_pairs={{8,0},{0,8},{24,16},{16,24},{40,32},{32,40},{56,48},{48,56},{72,64... | collective-permute-start | bytes 49160 | tf_op jit(solution)/shard_map/ppermute | solution.py:32
  142.9 1.7 %fusion.5 = f32[64,32,128]{2,1,0:T(8,128)} fusion(f32[64,32,128]{2,1,0:T(8,128)} %fusion, f16[16,32,128]{2,1,0:T(8,128)(2,1)} %collective-permute-done.39, f32[4,16,32,128]{3,2,1,0:T(8,128)S(1)} %copy-done.9, f32[16,128]{1,0:T(8,128)S(1)} %slice.124, f16[2,16,32,128]{3,2,1,0:T(8,128)(2,1)S(1)} %copy-done.14), kind=kLoop, calls=%fused_computation.17 | loop fusion | flops 327680 | bytes 794624 | tf_op jit(solution)/shard_map/scatter | solution.py:368
  (143 shorter events, 30.2 us)
Async XLA Ops:
  2.0 12.0 %collective-permute-start.2 = (bf16[1056,128]{1,0:T(8,128)(2,1)}, bf16[1056,128]{1,0:T(8,128)(2,1)S(1)}, u32[]{:S(2)}, u32[]{:S(2)}) collective-permute-start(bf16[1056,128]{1,0:T(8,128)(2,1)} %get-tuple-element.38), channel_id=1, source_target_pairs={{48,0},{200,8},{0,16},{216,24},{16,32},{232,40},{32,48},{248,56},{... | collective-permute-start | bytes 811016 | tf_op jit(solution)/shard_map/ppermute | solution.py:32
  4.1 9.9 %collective-permute-start.1 = (bf16[1056,128]{1,0:T(8,128)(2,1)}, bf16[1056,128]{1,0:T(8,128)(2,1)S(1)}, u32[]{:S(2)}, u32[]{:S(2)}) collective-permute-start(bf16[1056,128]{1,0:T(8,128)(2,1)} %get-tuple-element.38), channel_id=1, source_target_pairs={{32,0},{136,8},{48,16},{152,24},{0,32},{168,40},{16,48},{184,56},{... | collective-permute-start | bytes 811016 | tf_op jit(solution)/shard_map/ppermute | solution.py:32
  6.7 10.1 %collective-permute-start = (bf16[1056,128]{1,0:T(8,128)(2,1)}, bf16[1056,128]{1,0:T(8,128)(2,1)S(1)}, u32[]{:S(2)}, u32[]{:S(2)}) collective-permute-start(bf16[1056,128]{1,0:T(8,128)(2,1)} %get-tuple-element.38), channel_id=1, source_target_pairs={{16,0},{72,8},{32,16},{88,24},{48,32},{104,40},{0,48},{120,56},{80... | collective-permute-start | bytes 811016 | tf_op jit(solution)/shard_map/ppermute | solution.py:32
  14.1 51.8 %collective-permute-start.16 = (bf16[2112,128]{1,0:T(8,128)(2,1)S(1)}, bf16[2112,128]{1,0:T(8,128)(2,1)S(1)}, u32[]{:S(2)}, u32[]{:S(2)}) collective-permute-start(bf16[2112,128]{1,0:T(8,128)(2,1)S(1)} %constant_dynamic-update-slice_fusion.2.refs_8_), channel_id=1, source_target_pairs={{192,0},{56,8},{208,16},{8,24},{224,32},{24,40},{240,48},{40,56},{... | collective-permute-start | bytes 1622024 | tf_op jit(solution)/shard_map/ppermute | solution.py:32
  15.1 51.0 %collective-permute-start.14 = (bf16[2112,128]{1,0:T(8,128)(2,1)S(1)}, bf16[2112,128]{1,0:T(8,128)(2,1)S(1)}, u32[]{:S(2)}, u32[]{:S(2)}) collective-permute-start(bf16[2112,128]{1,0:T(8,128)(2,1)S(1)} %constant_dynamic-update-slice_fusion.2.refs_8_), channel_id=1, source_target_pairs={{64,0},{24,8},{80,16},{40,24},{96,32},{56,40},{112,48},{8,56},{128... | collective-permute-start | bytes 1622024 | tf_op jit(solution)/shard_map/ppermute | solution.py:32
  16.9 49.1 %collective-permute-start.13 = (bf16[2112,128]{1,0:T(8,128)(2,1)S(1)}, bf16[2112,128]{1,0:T(8,128)(2,1)S(1)}, u32[]{:S(2)}, u32[]{:S(2)}) collective-permute-start(bf16[2112,128]{1,0:T(8,128)(2,1)S(1)} %constant_dynamic-update-slice_fusion.refs_7_), channel_id=1, source_target_pairs={{64,0},{24,8},{80,16},{40,24},{96,32},{56,40},{112,48},{8,56},{128... | collective-permute-start | bytes 1622024 | tf_op jit(solution)/shard_map/ppermute | solution.py:32
  17.9 50.8 %collective-permute-start.18 = (bf16[2112,128]{1,0:T(8,128)(2,1)S(1)}, bf16[2112,128]{1,0:T(8,128)(2,1)}, u32[]{:S(2)}, u32[]{:S(2)}) collective-permute-start(bf16[2112,128]{1,0:T(8,128)(2,1)S(1)} %constant_dynamic-update-slice_fusion.refs_7_), channel_id=1, source_target_pairs={{192,0},{56,8},{208,16},{8,24},{224,32},{24,40},{240,48},{40,56},{... | collective-permute-start | bytes 1622024 | tf_op jit(solution)/shard_map/ppermute | solution.py:32
  18.4 11.4 %collective-permute-start.3 = (bf16[4,32,128]{2,1,0:T(8,128)(2,1)S(1)}, bf16[4,32,128]{2,1,0:T(8,128)(2,1)S(1)}, u32[]{:S(2)}, u32[]{:S(2)}) collective-permute-start(bf16[4,32,128]{2,1,0:T(8,128)(2,1)S(1)} %pad_maximum_fusion.refs_0_), channel_id=1, source_target_pairs={{64,0},{24,8},{80,16},{40,24},{96,32},{56,40},{112,48},{8,56},{128... | collective-permute-start | bytes 98312 | tf_op jit(solution)/shard_map/ppermute | solution.py:32
  29.8 4.3 %collective-permute-start.4 = (bf16[4,32,128]{2,1,0:T(8,128)(2,1)S(1)}, bf16[4,32,128]{2,1,0:T(8,128)(2,1)S(1)}, u32[]{:S(2)}, u32[]{:S(2)}) collective-permute-start(bf16[4,32,128]{2,1,0:T(8,128)(2,1)S(1)} %pad_maximum_fusion.refs_0_), channel_id=1, source_target_pairs={{128,0},{40,8},{144,16},{56,24},{160,32},{8,40},{176,48},{24,56},{... | collective-permute-start | bytes 98312 | tf_op jit(solution)/shard_map/ppermute | solution.py:32
  34.1 4.2 %collective-permute-start.5 = (bf16[4,32,128]{2,1,0:T(8,128)(2,1)S(1)}, bf16[4,32,128]{2,1,0:T(8,128)(2,1)S(1)}, u32[]{:S(2)}, u32[]{:S(2)}) collective-permute-start(bf16[4,32,128]{2,1,0:T(8,128)(2,1)S(1)} %pad_maximum_fusion.refs_0_), channel_id=1, source_target_pairs={{192,0},{56,8},{208,16},{8,24},{224,32},{24,40},{240,48},{40,56},{... | collective-permute-start | bytes 98312 | tf_op jit(solution)/shard_map/ppermute | solution.py:32
  38.2 6.0 %collective-permute-start.6 = (bf16[4,32,128]{2,1,0:T(8,128)(2,1)S(1)}, bf16[4,32,128]{2,1,0:T(8,128)(2,1)S(1)}, u32[]{:S(2)}, u32[]{:S(2)}) collective-permute-start(bf16[4,32,128]{2,1,0:T(8,128)(2,1)S(1)} %pad_maximum_fusion.refs_0_), channel_id=1, source_target_pairs={{8,0},{0,8},{24,16},{16,24},{40,32},{32,40},{56,48},{48,56},{72,64... | collective-permute-start | bytes 98312 | tf_op jit(solution)/shard_map/ppermute | solution.py:32
  53.6 4.0 %collective-permute-start.11 = (f32[2,128]{1,0:T(2,128)}, f32[2,128]{1,0:T(2,128)S(1)}, u32[]{:S(2)}, u32[]{:S(2)}) collective-permute-start(f32[2,128]{1,0:T(2,128)} %get-tuple-element.40.refs_0_), channel_id=1, source_target_pairs={{0,4},{2,6},{4,0},{6,2},{1,5},{3,7},{5,1},{7,3},{8,12},{10,14},{12... | collective-permute-start | bytes 3080 | tf_op jit(solution)/shard_map/ppermute | solution.py:85
  57.6 4.7 %collective-permute-start.12 = (f32[2,128]{1,0:T(2,128)}, f32[2,128]{1,0:T(2,128)S(1)}, u32[]{:S(2)}, u32[]{:S(2)}) collective-permute-start(f32[2,128]{1,0:T(2,128)} %get-tuple-element.40.refs_0_), channel_id=1, source_target_pairs={{0,6},{2,4},{4,2},{6,0},{1,7},{3,5},{5,3},{7,1},{8,14},{10,12},{12... | collective-permute-start | bytes 3080 | tf_op jit(solution)/shard_map/ppermute | solution.py:85
  62.4 7.3 %collective-permute-start.20 = (bf16[2112,128]{1,0:T(8,128)(2,1)S(1)}, bf16[2112,128]{1,0:T(8,128)(2,1)S(1)}, u32[]{:S(2)}, u32[]{:S(2)}) collective-permute-start(bf16[2112,128]{1,0:T(8,128)(2,1)S(1)} %constant_dynamic-update-slice_fusion.2.refs_8_), channel_id=1, source_target_pairs={{8,0},{0,8},{24,16},{16,24},{40,32},{32,40},{56,48},{48,56},{72,64... | collective-permute-start | bytes 1622024 | tf_op jit(solution)/shard_map/ppermute | solution.py:32
  65.9 3.9 %collective-permute-start.19 = (bf16[2112,128]{1,0:T(8,128)(2,1)S(1)}, bf16[2112,128]{1,0:T(8,128)(2,1)S(1)}, u32[]{:S(2)}, u32[]{:S(2)}) collective-permute-start(bf16[2112,128]{1,0:T(8,128)(2,1)S(1)} %constant_dynamic-update-slice_fusion.refs_7_), channel_id=1, source_target_pairs={{8,0},{0,8},{24,16},{16,24},{40,32},{32,40},{56,48},{48,56},{72,64... | collective-permute-start | bytes 1622024 | tf_op jit(solution)/shard_map/ppermute | solution.py:32
  66.0 9.8 %collective-permute-start.17 = (bf16[2112,128]{1,0:T(8,128)(2,1)S(1)}, bf16[2112,128]{1,0:T(8,128)(2,1)}, u32[]{:S(2)}, u32[]{:S(2)}) collective-permute-start(bf16[2112,128]{1,0:T(8,128)(2,1)S(1)} %collective-permute-done.16.refs_14_), channel_id=1, source_target_pairs={{192,0},{56,8},{208,16},{8,24},{224,32},{24,40},{240,48},{40,56},{... | collective-permute-start | bytes 1622024 | tf_op jit(solution)/shard_map/ppermute | solution.py:32
  66.0 11.1 %collective-permute-start.15 = (bf16[2112,128]{1,0:T(8,128)(2,1)S(1)}, bf16[2112,128]{1,0:T(8,128)(2,1)}, u32[]{:S(2)}, u32[]{:S(2)}) collective-permute-start(bf16[2112,128]{1,0:T(8,128)(2,1)S(1)} %collective-permute-done.13.refs_9_), channel_id=1, source_target_pairs={{64,0},{24,8},{80,16},{40,24},{96,32},{56,40},{112,48},{8,56},{128... | collective-permute-start | bytes 1622024 | tf_op jit(solution)/shard_map/ppermute | solution.py:32
  68.7 8.4 %collective-permute-start.26 = (bf16[2112,128]{1,0:T(8,128)(2,1)S(1)}, bf16[2112,128]{1,0:T(8,128)(2,1)S(1)}, u32[]{:S(2)}, u32[]{:S(2)}) collective-permute-start(bf16[2112,128]{1,0:T(8,128)(2,1)S(1)} %collective-permute-done.16.refs_14_), channel_id=1, source_target_pairs={{8,0},{0,8},{24,16},{16,24},{40,32},{32,40},{56,48},{48,56},{72,64... | collective-permute-start | bytes 1622024 | tf_op jit(solution)/shard_map/ppermute | solution.py:32
  69.7 9.7 %collective-permute-start.21 = (bf16[2112,128]{1,0:T(8,128)(2,1)S(1)}, bf16[2112,128]{1,0:T(8,128)(2,1)}, u32[]{:S(2)}, u32[]{:S(2)}) collective-permute-start(bf16[2112,128]{1,0:T(8,128)(2,1)S(1)} %collective-permute-done.13.refs_9_), channel_id=1, source_target_pairs={{8,0},{0,8},{24,16},{16,24},{40,32},{32,40},{56,48},{48,56},{72,64... | collective-permute-start | bytes 1622024 | tf_op jit(solution)/shard_map/ppermute | solution.py:32
  69.8 9.6 %collective-permute-start.22 = (bf16[2112,128]{1,0:T(8,128)(2,1)S(1)}, bf16[2112,128]{1,0:T(8,128)(2,1)}, u32[]{:S(2)}, u32[]{:S(2)}) collective-permute-start(bf16[2112,128]{1,0:T(8,128)(2,1)S(1)} %collective-permute-done.14.refs_10_), channel_id=1, source_target_pairs={{8,0},{0,8},{24,16},{16,24},{40,32},{32,40},{56,48},{48,56},{72,64... | collective-permute-start | bytes 1622024 | tf_op jit(solution)/shard_map/ppermute | solution.py:32
  89.4 11.1 %collective-permute-start.27 = (f16[2,24,32,128]{3,2,1,0:T(8,128)(2,1)S(1)}, f16[2,24,32,128]{3,2,1,0:T(8,128)(2,1)S(1)}, u32[]{:S(2)}, u32[]{:S(2)}) collective-permute-start(f16[2,24,32,128]{3,2,1,0:T(8,128)(2,1)S(1)} %slice_convert_fusion.1), channel_id=1, source_target_pairs={{0,2},{2,0},{4,6},{6,4},{1,3},{3,1},{5,7},{7,5},{8,10},{10,8},{12,... | collective-permute-start | bytes 1179656 | tf_op jit(solution)/shard_map/ppermute | solution.py:85
  98.9 10.4 %collective-permute-start.29 = (f16[2,24,32,128]{3,2,1,0:T(8,128)(2,1)S(1)}, f16[2,24,32,128]{3,2,1,0:T(8,128)(2,1)S(1)}, u32[]{:S(2)}, u32[]{:S(2)}) collective-permute-start(f16[2,24,32,128]{3,2,1,0:T(8,128)(2,1)S(1)} %slice_convert_fusion), channel_id=1, source_target_pairs={{0,2},{2,0},{4,6},{6,4},{1,3},{3,1},{5,7},{7,5},{8,10},{10,8},{12,... | collective-permute-start | bytes 1179656 | tf_op jit(solution)/shard_map/ppermute | solution.py:85
  109.1 8.2 %collective-permute-start.31 = (f16[2,16,32,128]{3,2,1,0:T(8,128)(2,1)S(1)}, f16[2,16,32,128]{3,2,1,0:T(8,128)(2,1)S(1)}, u32[]{:S(2)}, u32[]{:S(2)}) collective-permute-start(f16[2,16,32,128]{3,2,1,0:T(8,128)(2,1)S(1)} %slice_convert_fusion.2), channel_id=1, source_target_pairs={{0,2},{2,0},{4,6},{6,4},{1,3},{3,1},{5,7},{7,5},{8,10},{10,8},{12,... | collective-permute-start | bytes 786440 | tf_op jit(solution)/shard_map/ppermute | solution.py:85
  110.5 6.7 %collective-permute-start.32 = (f32[1,2,128]{2,1,0:T(2,128)S(1)}, f32[1,2,128]{2,1,0:T(2,128)S(1)}, u32[]{:S(2)}, u32[]{:S(2)}) collective-permute-start(f32[1,2,128]{2,1,0:T(2,128)S(1)} %bitcast.32), channel_id=1, source_target_pairs={{16,0},{72,8},{32,16},{88,24},{48,32},{104,40},{0,48},{120,56},{80... | collective-permute-start | bytes 3080 | tf_op jit(solution)/shard_map/ppermute | solution.py:32
  112.8 4.5 %collective-permute-start.33 = (f32[1,2,128]{2,1,0:T(2,128)S(1)}, f32[1,2,128]{2,1,0:T(2,128)S(1)}, u32[]{:S(2)}, u32[]{:S(2)}) collective-permute-start(f32[1,2,128]{2,1,0:T(2,128)S(1)} %bitcast.33), channel_id=1, source_target_pairs={{32,0},{136,8},{48,16},{152,24},{0,32},{168,40},{16,48},{184,56},{... | collective-permute-start | bytes 3080 | tf_op jit(solution)/shard_map/ppermute | solution.py:32
  112.8 4.5 %collective-permute-start.34 = (f32[1,2,128]{2,1,0:T(2,128)S(1)}, f32[1,2,128]{2,1,0:T(2,128)S(1)}, u32[]{:S(2)}, u32[]{:S(2)}) collective-permute-start(f32[1,2,128]{2,1,0:T(2,128)S(1)} %bitcast.34), channel_id=1, source_target_pairs={{48,0},{200,8},{0,16},{216,24},{16,32},{232,40},{32,48},{248,56},{... | collective-permute-start | bytes 3080 | tf_op jit(solution)/shard_map/ppermute | solution.py:32
  113.4 17.1 %collective-permute-start.30 = (f16[24,32,128]{2,1,0:T(8,128)(2,1)S(1)}, f16[24,32,128]{2,1,0:T(8,128)(2,1)S(1)}, u32[]{:S(2)}, u32[]{:S(2)}) collective-permute-start(f16[24,32,128]{2,1,0:T(8,128)(2,1)S(1)} %fusion.7), channel_id=1, source_target_pairs={{0,4},{2,6},{4,0},{6,2},{1,5},{3,7},{5,1},{7,3},{8,12},{10,14},{12... | collective-permute-start | bytes 589832 | tf_op jit(solution)/shard_map/ppermute | solution.py:85
  117.2 19.0 %collective-permute-start.28 = (f16[24,32,128]{2,1,0:T(8,128)(2,1)}, f16[24,32,128]{2,1,0:T(8,128)(2,1)S(1)}, u32[]{:S(2)}, u32[]{:S(2)}) collective-permute-start(f16[24,32,128]{2,1,0:T(8,128)(2,1)} %fusion.6), channel_id=1, source_target_pairs={{0,4},{2,6},{4,0},{6,2},{1,5},{3,7},{5,1},{7,3},{8,12},{10,14},{12... | collective-permute-start | bytes 589832 | tf_op jit(solution)/shard_map/ppermute | solution.py:85
  118.0 19.4 %collective-permute-start.35 = (f32[4,2,128]{2,1,0:T(2,128)S(1)}, f32[4,2,128]{2,1,0:T(2,128)S(1)}, u32[]{:S(2)}, u32[]{:S(2)}) collective-permute-start(f32[4,2,128]{2,1,0:T(2,128)S(1)} %pad_maximum_fusion.2), channel_id=1, source_target_pairs={{64,0},{24,8},{80,16},{40,24},{96,32},{56,40},{112,48},{8,56},{128... | collective-permute-start | bytes 12296 | tf_op jit(solution)/shard_map/ppermute | solution.py:32
  118.6 18.8 %collective-permute-start.36 = (f32[4,2,128]{2,1,0:T(2,128)S(1)}, f32[4,2,128]{2,1,0:T(2,128)S(1)}, u32[]{:S(2)}, u32[]{:S(2)}) collective-permute-start(f32[4,2,128]{2,1,0:T(2,128)S(1)} %pad_maximum_fusion.2), channel_id=1, source_target_pairs={{128,0},{40,8},{144,16},{56,24},{160,32},{8,40},{176,48},{24,56},{... | collective-permute-start | bytes 12296 | tf_op jit(solution)/shard_map/ppermute | solution.py:32
  119.0 18.4 %collective-permute-start.37 = (f32[4,2,128]{2,1,0:T(2,128)S(1)}, f32[4,2,128]{2,1,0:T(2,128)S(1)}, u32[]{:S(2)}, u32[]{:S(2)}) collective-permute-start(f32[4,2,128]{2,1,0:T(2,128)S(1)} %pad_maximum_fusion.2), channel_id=1, source_target_pairs={{192,0},{56,8},{208,16},{8,24},{224,32},{24,40},{240,48},{40,56},{... | collective-permute-start | bytes 12296 | tf_op jit(solution)/shard_map/ppermute | solution.py:32
  130.5 12.4 %collective-permute-start.39 = (f16[16,32,128]{2,1,0:T(8,128)(2,1)}, f16[16,32,128]{2,1,0:T(8,128)(2,1)}, u32[]{:S(2)}, u32[]{:S(2)}) collective-permute-start(f16[16,32,128]{2,1,0:T(8,128)(2,1)} %fusion.8), channel_id=1, source_target_pairs={{0,4},{2,6},{4,0},{6,2},{1,5},{3,7},{5,1},{7,3},{8,12},{10,14},{12... | collective-permute-start | bytes 393224 | tf_op jit(solution)/shard_map/ppermute | solution.py:85
  (36 other events, 533.0 us)

commit v3 on v2

--- a/solution.py
+++ b/solution.py
@@ -10,7 +10,7 @@
 CORES = 2
 UNROLL = 4
 CHUNKS = (24, 24, 16)
-GRAM_SCALE = 32.0
+ROOT_SCALE = 64.0
 SMALL_ROWS = 32
 
 saturation = 1.2
@@ -66,19 +66,27 @@
 
 
 def place_right(doc, doc_at):
-    core = doc % CORES
-    dx = (doc // CORES - doc_at // CORES) % SIDE
-    dy = (doc // (SIDE * CORES) - doc_at // (SIDE * CORES)) % SIDE
-    dcore = (doc - doc_at) % CORES
-    inner = jnp.where(core == 0, dx, dy)
-    outer = jnp.where(core == 0, dy, dx)
-    piece = (dcore * SIDE + outer) * 2 + inner // 2
-    return piece, inner % 2, (dcore * SIDE + outer) * SIDE + inner
+    dx = ((doc >> 1) - (doc_at >> 1)) & (SIDE - 1)
+    dy = ((doc >> 3) - (doc_at >> 3)) & (SIDE - 1)
+    dcore = (doc ^ doc_at) & (CORES - 1)
+    inner = jnp.where((doc & 1) == 0, dx, dy)
+    outer = jnp.where((doc & 1) == 0, dy, dx)
+    plane = (dcore << 2) | outer
+    return (plane << 1) | (inner >> 1), inner & 1, (plane << 2) | inner
+
+
+def pack_root(value):
+    return (jnp.sqrt(value) * ROOT_SCALE).astype(jnp.float16)
+
+
+def unpack_root(value):
+    root = value.astype(jnp.float32) * (1.0 / ROOT_SCALE)
+    return root * root
 
 
 def place_owner(owner, term_at):
     apart = owner ^ term_at
-    return (apart % 2) * 2 + apart // 2
+    return ((apart & 1) << 1) | (apart >> 1)
 
 
 def swap_term(value, bit, n_term):
@@ -132,7 +140,7 @@
 
     def kernel(ids_ref, own_ref, *refs):
         small_refs = refs[: len(small_parts)]
-        id_ref, length_ref, idf_ref, weight_ref, square_ref = refs[len(small_parts) :]
+        id_ref, length_ref, idf_ref, left_ref, stat_ref = refs[len(small_parts) :]
         small = jnp.concatenate([ref[...].astype(jnp.float32) for ref in small_refs], axis=0)
         cols = small[:, :own_slots]
         ids = small[:, own_slots : 2 * own_slots] * 256.0 + small[:, 2 * own_slots : 3 * own_slots]
@@ -159,9 +167,9 @@
                 idf_ref[b * slots + s] = jnp.broadcast_to(idf, (rows, terms)).T
                 c = own_ref[b, :, s * terms : (s + 1) * terms].astype(jnp.float32)
                 weight = idf * c / (c + own_len)
-                weight_ref[b, :, s * terms : (s + 1) * terms] = weight
+                left_ref[b, :, s * terms : (s + 1) * terms] = weight.astype(jnp.bfloat16)
                 square = square + weight * weight
-            square_ref[b : b + 1, :] = jnp.sum(square.T, axis=0, keepdims=True)
+            stat_ref[b : b + 1, :] = jnp.sum(square.T, axis=0, keepdims=True)
 
     smem = pl.BlockSpec(memory_space=pltpu.SMEM)
     vmem = pl.BlockSpec(memory_space=pltpu.VMEM)
@@ -173,18 +181,17 @@
             jax.ShapeDtypeStruct((n_doc * own_slots // rows, rows), jnp.int32),
             jax.ShapeDtypeStruct((n_doc, SMALL_ROWS - 3 * own_slots, rows), jnp.float32),
             jax.ShapeDtypeStruct((own_slots, terms, rows), jnp.float32),
-            jax.ShapeDtypeStruct((blocks, rows, width), jnp.float32),
+            jax.ShapeDtypeStruct((blocks, rows, width), jnp.bfloat16),
             jax.ShapeDtypeStruct((blocks, rows), jnp.float32),
         ],
         name="weigh",
     )(block_ids, own_counts, *small_parts)
 
 
-def gram_chunk(first, size, pairs, own_ids, all_ids, weight, squares, idf_tiles, len_rows, pieces):
+def gram_chunk(first, size, pairs, own_ids, all_ids, n_term, left_tiles, idf_tiles, len_rows, pieces):
     own_slots, terms, rows = idf_tiles.shape
-    blocks = weight.shape[0]
+    blocks = left_tiles.shape[0]
     slots = own_slots // blocks
-    n_term = len(squares)
     part = rows // n_term
     groups = size // UNROLL
     payload_rows = pieces[0].shape[0] // 2
@@ -192,15 +199,15 @@
     def kernel(pair_ref, own_ref, ids_ref, *refs):
         doc_at = lax.axis_index("doc")
         term_at = lax.axis_index("term")
-        square_refs = refs[:n_term]
-        weight_hbm, idf_hbm, length_hbm = refs[n_term : n_term + 3]
-        piece_refs = refs[n_term + 3 : n_term + 3 + len(pieces)]
-        out_hbm, *scratch = refs[n_term + 3 + len(pieces) :]
-        weight_ref, idf_ref, length_ref, left_ref, tile_buf, gram_ref, loaded, arrived, written = scratch
+        left_hbm, idf_hbm, length_hbm = refs[:3]
+        piece_refs = refs[3 : 3 + len(pieces)]
+        out_hbm, *scratch = refs[3 + len(pieces) :]
+        left_ref, idf_ref, length_ref, tile_buf, gram_ref, note_ref = scratch[:6]
+        loaded, arrived, written = scratch[6:]
         loads = [
             pltpu.make_async_copy(src, dst, loaded.at[n])
             for n, (src, dst) in enumerate(
-                [(weight_hbm, weight_ref), (idf_hbm, idf_ref), (length_hbm, length_ref)]
+                [(left_hbm, left_ref), (idf_hbm, idf_ref), (length_hbm, length_ref)]
             )
         ]
         for load in loads:
@@ -208,12 +215,13 @@
 
         def fetch(k, carry):
             right = pair_ref[first + k, 1]
-            piece, spot, _ = place_right(right // blocks, doc_at)
-            spot = spot * payload_rows + (right % blocks) * (slots * terms)
+            piece, spot, right_doc = place_right(right >> 1, doc_at)
+            note_ref[k] = right_doc
+            spot = spot * payload_rows + (right & 1) * (slots * terms)
             spot = pl.multiple_of(spot, SMALL_ROWS)
             for quad in range(len(pieces) // 4):
 
-                @pl.when(piece // 4 == quad)
+                @pl.when((piece >> 2) == quad)
                 def _():
                     for p in range(4 * quad, 4 * quad + 4):
 
@@ -228,17 +236,8 @@
             return carry
 
         lax.fori_loop(0, size, fetch, 0)
-        square_sum = square_refs[0][...]
-        for ref in square_refs[1:]:
-            square_sum = square_sum + ref[...]
-        norm = lax.rsqrt(square_sum + epsilon) * GRAM_SCALE
         for load in loads:
             load.wait()
-        for b in range(blocks):
-            column = jnp.broadcast_to(norm[b : b + 1, :], (rows, rows)).T
-            for s in range(slots):
-                at = slice(s * terms, (s + 1) * terms)
-                left_ref[b, :, at] = (weight_ref[b, :, at] * column).astype(jnp.bfloat16)
 
         def multiply(step, carry):
             for p in range(UNROLL):
@@ -249,10 +248,11 @@
             for p in range(UNROLL):
                 k = step * UNROLL + p
                 left = pair_ref[first + k, 0] - doc_at * blocks
-                right_block = pair_ref[first + k, 1] % blocks
-                _, _, right_doc = place_right(pair_ref[first + k, 1] // blocks, doc_at)
-                id_row = right_doc * own_slots // rows
-                id_at = right_doc * own_slots % rows + right_block * slots
+                right_block = pair_ref[first + k, 1] & 1
+                right_doc = note_ref[k]
+                id_row = right_doc >> 4
+                id_at = ((right_doc & 15) << 3) + right_block * slots
+                their_ids = [ids_ref[id_row, id_at + j] for j in range(slots)]
                 len_row = length_ref[right_doc, pl.ds(right_block, 1), :]
                 parts = []
                 for i in range(slots):
@@ -260,7 +260,7 @@
                     found = jnp.int32(0)
                     place = jnp.int32(0)
                     for j in range(slots):
-                        same = ids_ref[id_row, id_at + j] == wanted
+                        same = their_ids[j] == wanted
                         found = jnp.where(same, 1, found)
                         place = jnp.where(same, j, place)
                     start = pl.multiple_of(place * terms, terms)
@@ -289,26 +289,25 @@
         lax.fori_loop(0, groups, drain, 0)
 
     smem = pl.BlockSpec(memory_space=pltpu.SMEM)
-    vmem = pl.BlockSpec(memory_space=pltpu.VMEM)
     anywhere = pl.BlockSpec(memory_space=pl.ANY)
     return pl.pallas_call(
         kernel,
-        in_specs=[smem] * 3 + [vmem] * n_term + [anywhere] * (3 + len(pieces)),
+        in_specs=[smem] * 3 + [anywhere] * (3 + len(pieces)),
         out_specs=anywhere,
         out_shape=jax.ShapeDtypeStruct((n_term, size, part, rows), jnp.float32),
         scratch_shapes=[
-            pltpu.VMEM(weight.shape, jnp.float32),
+            pltpu.VMEM(left_tiles.shape, jnp.bfloat16),
             pltpu.VMEM(idf_tiles.shape, jnp.float32),
             pltpu.VMEM(len_rows.shape, jnp.float32),
-            pltpu.VMEM(weight.shape, jnp.bfloat16),
             pltpu.VMEM((size, slots * terms, rows), jnp.bfloat16),
             pltpu.VMEM((n_term, size, part, rows), jnp.float32),
+            pltpu.SMEM((size,), jnp.int32),
             pltpu.SemaphoreType.DMA((3,)),
             pltpu.SemaphoreType.DMA((size,)),
             pltpu.SemaphoreType.DMA((groups,)),
         ],
         name="gram",
-    )(pairs, own_ids, all_ids, *squares, weight, idf_tiles, len_rows, *pieces)
+    )(pairs, own_ids, all_ids, left_tiles, idf_tiles, len_rows, *pieces)
 
 
 def whole(counts, block_ids, live_slots, lengths, pairs, pair_count):
@@ -316,6 +315,7 @@
     n_doc = lax.axis_size("doc")
     n_term = lax.axis_size("term")
     doc_at = lax.axis_index("doc")
+    term_at = lax.axis_index("term")
     tile_rows = blocks * slots * terms
 
     payload, own_counts = prepare(counts, block_ids, live_slots, lengths)
@@ -326,46 +326,48 @@
     small_parts = [small_ring] + [from_ring(small_ring, 1, s) for s in (1, 2, 3)]
     small_parts = small_parts + [from_sibling(part) for part in small_parts]
     pieces = gather_rest(low, high)
-    all_ids, len_rows, idf_tiles, weight, square_part = weigh(
-        block_ids, small_parts, own_counts
-    )
-    squares = [square_part] + [swap_term(square_part, bit, n_term) for bit in range(1, n_term)]
+    all_ids, len_rows, idf_tiles, left_tiles, stat = weigh(block_ids, small_parts, own_counts)
+    stats = [stat] + [swap_term(stat, bit, n_term) for bit in range(1, n_term)]
+    norm = lax.rsqrt(sum(stats) + epsilon)
 
     kept = []
     ready = []
     first = 0
-    chosen = pairs
-    for step, size in enumerate(CHUNKS):
-        if step >= 2:
-            chosen, _ = lax.optimization_barrier((chosen, ready[step - 2]))
+    for size in CHUNKS:
         grams = gram_chunk(
-            first, size, chosen, block_ids, all_ids, weight, squares, idf_tiles, len_rows, pieces
+            first, size, pairs, block_ids, all_ids, n_term, left_tiles, idf_tiles, len_rows, pieces
         )
         first += size
-        near = swap_term(grams[2:].astype(jnp.float16), 1, n_term)
-        pass_on = (grams[1] + near[1].astype(jnp.float32)).astype(jnp.float16)
+        near = swap_term(pack_root(grams[2:]), 1, n_term)
+        pass_on = pack_root(grams[1] + unpack_root(near[1]))
         ready.append(pass_on)
         far = swap_term(pass_on, 2, n_term)
         kept.append((grams, near, far))
     early, _ = lax.optimization_barrier((tuple(kept[:-1]), ready[-1]))
-    norm, _ = lax.optimization_barrier((lax.rsqrt(sum(squares) + epsilon), ready[-2]))
-    norm_ring = gather_ring(norm[None], 0)
+    late_norm, _ = lax.optimization_barrier((norm, ready[-2]))
+    norm_ring = gather_ring(late_norm[None], 0)
     norm_ring, _ = lax.optimization_barrier((norm_ring, ready[-1]))
     norm_rows = gather_sibling(gather_ring(norm_ring, 1))
     right = pairs[:, 1]
     _, _, right_doc = place_right(right // blocks, doc_at)
     norm_rows = norm_rows.reshape(n_doc * blocks, rows)[right_doc * blocks + right % blocks]
     live = jnp.arange(pairs.shape[0], dtype=jnp.int32) < pair_count[0]
-    right_norm = jnp.where(live[:, None], norm_rows * (1.0 / GRAM_SCALE), 0.0)[:, None, :]
-
-    def total(grams, near, far):
-        return grams[0] + near[0].astype(jnp.float32) + far.astype(jnp.float32)
-
-    last = pairs.shape[0] - CHUNKS[-1]
-    result = jnp.concatenate([total(*each) for each in early], axis=0)
+    right_norm = jnp.where(live[:, None], norm_rows, 0.0)[:, None, :]
+    part = rows // n_term
+    own_norm = lax.dynamic_slice_in_dim(norm, term_at * part, part, 1)
+    own_norm = jnp.broadcast_to(own_norm[:, :, None], (blocks, part, rows))
+    left = (pairs[:, 0] - doc_at * blocks)[:, None, None]
+
+    def total(at, grams, near, far):
+        value = grams[0] + unpack_root(near[0]) + unpack_root(far)
+        return value * jnp.where(left[at] == 0, own_norm[0], own_norm[1])
+
+    ends = [sum(CHUNKS[: n + 1]) for n in range(len(CHUNKS))]
+    spans = [slice(end - size, end) for end, size in zip(ends, CHUNKS)]
+    result = jnp.concatenate([total(at, *each) for at, each in zip(spans, early)], axis=0)
     result = jnp.pad(result, ((0, CHUNKS[-1]), (0, 0), (0, 0))) * right_norm
     result, final = lax.optimization_barrier((result, kept[-1]))
-    return result.at[last:].set(total(*final) * right_norm[last:])
+    return result.at[spans[-1]].set(total(spans[-1], *final) * right_norm[spans[-1]])
 
 
 def solution(mesh):

time: 145 us -> 145 us (level)
  the two profiles are of different devices: /device:TPU:1 before, /device:TPU:26 now
where the time goes in v3:
time: 145 us; the launch traced here: 144 us
  waiting for transfers between devices  60.5 us (42%)
  starting transfers between devices  39.8 us (27%)
  Pallas kernels  22.7 us (16%)
  other arithmetic  15 us (10%)
  local copies, waits for them, and re-layouts  4.65 us (3%)
    ppermute x31, waiting for transfers between devices, permute_doc(): return lax.ppermute(value, 'doc', moves)  43.8 us
    ppermute x31, starting transfers between devices, permute_doc(): return lax.ppermute(value, 'doc', moves)  23.5 us
    pallas_call x3, Pallas kernels, gram_chunk(): pl.pallas_call(kernel, in_specs=[smem] * 3 + [anywhere] * (3 + len(pieces...  18.2 us
    ppermute x9, waiting for transfers between devices, swap_term(): return lax.ppermute(value, 'term', [(a, a ^ bit) for a in range(n_term)])  16.7 us
    ppermute x9, starting transfers between devices, swap_term(): return lax.ppermute(value, 'term', [(a, a ^ bit) for a in range(n_term)])  16.3 us
    convert_element_type x6, other arithmetic, pack_root(): return (jnp.sqrt(value) * ROOT_SCALE).astype(jnp.float16)  8.09 us
    unnamed x71, local copies, waits for them, and re-layouts  3.15 us
  transfers between devices with their start and end apart: 40, of which 21 were waited for; matrix products, arithmetic and copies ran while one was open for 11% of the time, Pallas kernels for 11%

profile of v3, /device:TPU:26, one launch (start us, length us, event | category | flops | bytes accessed | tf_op | source)
XLA Modules:
  0.0 143.8 jit_solution(10307627190685461039)
XLA Ops:
  0.0 2.0 %prepare.1 = (bf16[1056,128]{1,0:T(8,128)(2,1)}, bf16[2,128,512]{2,1,0:T(8,128)(2,1)}) custom-call(s32[2,4]{1,0:T(2,128)} %own_ref.5, s32[2,4]{1,0:T(2,128)} %live_ref.1, s32[2,128]{1,0:T(2,128)} %bitcast.52, s32[2,4,128,128]{3,2,1,0:T(8,128)} %count_ref.1), custom_call_target="tpu_custom_call" | custom-call | tf_op jit(solution)/shard_map/prepare/pallas_call | solution.py:121
  2.0 1.5 %collective-permute-start.2 = (bf16[1056,128]{1,0:T(8,128)(2,1)}, bf16[1056,128]{1,0:T(8,128)(2,1)S(1)}, u32[]{:S(2)}, u32[]{:S(2)}) collective-permute-start(bf16[1056,128]{1,0:T(8,128)(2,1)} %get-tuple-element.37), channel_id=1, source_target_pairs={{48,0},{200,8},{0,16},{216,24},{16,32},{232,40},{32,48},{248,56},{... | collective-permute-start | bytes 811016 | tf_op jit(solution)/shard_map/ppermute | solution.py:32
  4.6 2.2 %collective-permute-start = (bf16[1056,128]{1,0:T(8,128)(2,1)}, bf16[1056,128]{1,0:T(8,128)(2,1)S(1)}, u32[]{:S(2)}, u32[]{:S(2)}) collective-permute-start(bf16[1056,128]{1,0:T(8,128)(2,1)} %get-tuple-element.37), channel_id=1, source_target_pairs={{16,0},{72,8},{32,16},{88,24},{48,32},{104,40},{0,48},{120,56},{80... | collective-permute-start | bytes 811016 | tf_op jit(solution)/shard_map/ppermute | solution.py:32
  8.5 5.7 %collective-permute-done = bf16[1056,128]{1,0:T(8,128)(2,1)S(1)} collective-permute-done((bf16[1056,128]{1,0:T(8,128)(2,1)}, bf16[1056,128]{1,0:T(8,128)(2,1)S(1)}, u32[]{:S(2)}, u32[]{:S(2)}) %collective-permute-start) | collective-permute-done | bytes 270368 | tf_op jit(solution)/shard_map/ppermute | solution.py:32
  16.7 1.9 %collective-permute-start.13 = (bf16[2112,128]{1,0:T(8,128)(2,1)S(1)}, bf16[2112,128]{1,0:T(8,128)(2,1)S(1)}, u32[]{:S(2)}, u32[]{:S(2)}) collective-permute-start(bf16[2112,128]{1,0:T(8,128)(2,1)S(1)} %constant_dynamic-update-slice_fusion.2.refs_4_), channel_id=1, source_target_pairs={{192,0},{56,8},{208,16},{8,24},{224,32},{24,40},{240,48},{40,56},{... | collective-permute-start | bytes 1622024 | tf_op jit(solution)/shard_map/ppermute | solution.py:32
  19.6 10.3 %collective-permute-done.5.refs_3_ = bf16[4,32,128]{2,1,0:T(8,128)(2,1)S(1)} collective-permute-done((bf16[4,32,128]{2,1,0:T(8,128)(2,1)S(1)}, bf16[4,32,128]{2,1,0:T(8,128)(2,1)S(1)}, u32[]{:S(2)}, u32[]{:S(2)}) %collective-permute-start.5) | collective-permute-done | bytes 32800 | tf_op jit(solution)/shard_map/ppermute | solution.py:32
  31.1 4.2 %collective-permute-done.4.refs_2_ = bf16[4,32,128]{2,1,0:T(8,128)(2,1)S(1)} collective-permute-done((bf16[4,32,128]{2,1,0:T(8,128)(2,1)S(1)}, bf16[4,32,128]{2,1,0:T(8,128)(2,1)S(1)}, u32[]{:S(2)}, u32[]{:S(2)}) %collective-permute-start.4) | collective-permute-done | bytes 32800 | tf_op jit(solution)/shard_map/ppermute | solution.py:32
  36.1 4.4 %collective-permute-done.3.refs_1_ = bf16[4,32,128]{2,1,0:T(8,128)(2,1)S(1)} collective-permute-done((bf16[4,32,128]{2,1,0:T(8,128)(2,1)S(1)}, bf16[4,32,128]{2,1,0:T(8,128)(2,1)S(1)}, u32[]{:S(2)}, u32[]{:S(2)}) %collective-permute-start.3) | collective-permute-done | bytes 32800 | tf_op jit(solution)/shard_map/ppermute | solution.py:32
  44.7 2.5 %weigh.1 = (s32[2,128]{1,0:T(2,128)}, f32[32,8,128]{2,1,0:T(8,128)}, f32[8,128,128]{2,1,0:T(8,128)}, bf16[2,128,512]{2,1,0:T(8,128)(2,1)}, f32[2,128]{1,0:T(2,128)}) custom-call(s32[2,4]{1,0:T(2,128)} %own_ref.5, bf16[2,128,512]{2,1,0:T(8,128)(2,1)} %get-tuple-element.36.own_ref, bf16[4,32,128]{2,1,0:T(8,128)(2,1)} %copy-done.19, ...), custom_call_target="tpu_custom_call" | custom-call | tf_op jit(solution)/shard_map/weigh/pallas_call | solution.py:176
  47.1 4.6 %collective-permute-start.31 = (f32[2,128]{1,0:T(2,128)}, f32[2,128]{1,0:T(2,128)S(1)}, u32[]{:S(2)}, u32[]{:S(2)}) collective-permute-start(f32[2,128]{1,0:T(2,128)} %get-tuple-element.45), channel_id=1, source_target_pairs={{0,6},{2,4},{4,2},{6,0},{1,7},{3,5},{5,3},{7,1},{8,14},{10,12},{12... | collective-permute-start | bytes 3080 | tf_op jit(solution)/shard_map/ppermute | solution.py:93
  51.8 1.8 %collective-permute-done.31 = f32[2,128]{1,0:T(2,128)S(1)} collective-permute-done((f32[2,128]{1,0:T(2,128)}, f32[2,128]{1,0:T(2,128)S(1)}, u32[]{:S(2)}, u32[]{:S(2)}) %collective-permute-start.31) | collective-permute-done | bytes 1056 | tf_op jit(solution)/shard_map/ppermute | solution.py:93
  54.2 4.0 %collective-permute-done.30 = f32[2,128]{1,0:T(2,128)S(1)} collective-permute-done((f32[2,128]{1,0:T(2,128)}, f32[2,128]{1,0:T(2,128)S(1)}, u32[]{:S(2)}, u32[]{:S(2)}) %collective-permute-start.30) | collective-permute-done | bytes 1056 | tf_op jit(solution)/shard_map/ppermute | solution.py:93
  58.2 1.5 %collective-permute-start.29 = (f32[2,128]{1,0:T(2,128)}, f32[2,128]{1,0:T(2,128)S(1)}, u32[]{:S(2)}, u32[]{:S(2)}) collective-permute-start(f32[2,128]{1,0:T(2,128)} %get-tuple-element.45), channel_id=1, source_target_pairs={{0,2},{2,0},{4,6},{6,4},{1,3},{3,1},{5,7},{7,5},{8,10},{10,8},{12,... | collective-permute-start | bytes 3080 | tf_op jit(solution)/shard_map/ppermute | solution.py:93
  62.7 3.2 %collective-permute-start.14 = (bf16[2112,128]{1,0:T(8,128)(2,1)S(1)}, bf16[2112,128]{1,0:T(8,128)(2,1)S(1)}, u32[]{:S(2)}, u32[]{:S(2)}) collective-permute-start(bf16[2112,128]{1,0:T(8,128)(2,1)S(1)} %collective-permute-done.13.refs_10_), channel_id=1, source_target_pairs={{192,0},{56,8},{208,16},{8,24},{224,32},{24,40},{240,48},{40,56},{... | collective-permute-start | bytes 1622024 | tf_op jit(solution)/shard_map/ppermute | solution.py:32
  67.7 4.9 %collective-permute-done.11.refs_6_ = bf16[2112,128]{1,0:T(8,128)(2,1)S(1)} collective-permute-done((bf16[2112,128]{1,0:T(8,128)(2,1)S(1)}, bf16[2112,128]{1,0:T(8,128)(2,1)S(1)}, u32[]{:S(2)}, u32[]{:S(2)}) %collective-permute-start.11) | collective-permute-done | bytes 540704 | tf_op jit(solution)/shard_map/ppermute | solution.py:32
  73.2 5.3 %collective-permute-done.12.refs_7_ = bf16[2112,128]{1,0:T(8,128)(2,1)S(1)} collective-permute-done((bf16[2112,128]{1,0:T(8,128)(2,1)S(1)}, bf16[2112,128]{1,0:T(8,128)(2,1)S(1)}, u32[]{:S(2)}, u32[]{:S(2)}) %collective-permute-start.12) | collective-permute-done | bytes 540704 | tf_op jit(solution)/shard_map/ppermute | solution.py:32
  82.0 5.4 %gram.5 = f32[4,16,32,128]{3,2,1,0:T(8,128)} custom-call(s32[64,2]{1,0:T(8,128)} %copy.7.pair_ref, s32[2,4]{1,0:T(2,128)} %own_ref.5, s32[2,128]{1,0:T(2,128)} %get-tuple-element.38.ids_ref, bf16[2,128,512]{2,1,0:T(8,128)(2,1)} %get-tuple-element.39.refs_0_, f32[8,128,128]{2,1,0:T(8,128)} %get-tuple-element.40.refs_1_, ...), custom_call_target="tpu_custom_call" | custom-call | tf_op jit(solution)/shard_map/gram/pallas_call | solution.py:293
  88.7 1.5 %collective-permute-start.28 = (f16[2,16,32,128]{3,2,1,0:T(8,128)(2,1)S(1)}, f16[2,16,32,128]{3,2,1,0:T(8,128)(2,1)}, u32[]{:S(2)}, u32[]{:S(2)}) collective-permute-start(f16[2,16,32,128]{3,2,1,0:T(8,128)(2,1)S(1)} %fusion.6), channel_id=1, source_target_pairs={{0,2},{2,0},{4,6},{6,4},{1,3},{3,1},{5,7},{7,5},{8,10},{10,8},{12,... | collective-permute-start | bytes 786440 | tf_op jit(solution)/shard_map/ppermute | solution.py:93
  90.2 6.4 %gram.4 = f32[4,24,32,128]{3,2,1,0:T(8,128)} custom-call(s32[64,2]{1,0:T(8,128)} %copy.7.pair_ref, s32[2,4]{1,0:T(2,128)} %own_ref.5, s32[2,128]{1,0:T(2,128)} %get-tuple-element.38.ids_ref, bf16[2,128,512]{2,1,0:T(8,128)(2,1)} %get-tuple-element.39.refs_0_, f32[8,128,128]{2,1,0:T(8,128)} %get-tuple-element.40.refs_1_, ...), custom_call_target="tpu_custom_call" | custom-call | tf_op jit(solution)/shard_map/gram/pallas_call | solution.py:293
  98.7 6.4 %gram.3 = f32[4,24,32,128]{3,2,1,0:T(8,128)} custom-call(s32[64,2]{1,0:T(8,128)} %copy.7.pair_ref, s32[2,4]{1,0:T(2,128)} %own_ref.5, s32[2,128]{1,0:T(2,128)} %get-tuple-element.38.ids_ref, bf16[2,128,512]{2,1,0:T(8,128)(2,1)} %get-tuple-element.39.refs_0_, f32[8,128,128]{2,1,0:T(8,128)} %get-tuple-element.40.refs_1_, ...), custom_call_target="tpu_custom_call" | custom-call | tf_op jit(solution)/shard_map/gram/pallas_call | solution.py:293
  105.1 1.5 %fusion.4 = f16[2,24,32,128]{3,2,1,0:T(8,128)(2,1)S(1)} fusion(f32[4,24,32,128]{3,2,1,0:T(8,128)} %gram.3), kind=kLoop, calls=%fused_computation.9 | loop fusion | flops 393216 | bytes 1179648 | tf_op jit(solution)/shard_map/convert_element_type | solution.py:79
  106.6 1.5 %collective-permute-start.24 = (f16[2,24,32,128]{3,2,1,0:T(8,128)(2,1)S(1)}, f16[2,24,32,128]{3,2,1,0:T(8,128)(2,1)S(1)}, u32[]{:S(2)}, u32[]{:S(2)}) collective-permute-start(f16[2,24,32,128]{3,2,1,0:T(8,128)(2,1)S(1)} %fusion.4), channel_id=1, source_target_pairs={{0,2},{2,0},{4,6},{6,4},{1,3},{3,1},{5,7},{7,5},{8,10},{10,8},{12,... | collective-permute-start | bytes 1179656 | tf_op jit(solution)/shard_map/ppermute | solution.py:93
  108.2 1.7 %fusion.23 = f16[16,32,128]{2,1,0:T(8,128)(2,1)} fusion(f32[4,16,32,128]{3,2,1,0:T(8,128)S(1)} %copy-done.17, f16[2,16,32,128]{3,2,1,0:T(8,128)(2,1)} %collective-permute-done.28), kind=kLoop, calls=%fused_computation.35 | loop fusion | flops 393216 | bytes 524288 | tf_op jit(solution)/shard_map/convert_element_type | solution.py:79
  109.9 2.9 %collective-permute-start.39 = (f16[16,32,128]{2,1,0:T(8,128)(2,1)}, f16[16,32,128]{2,1,0:T(8,128)(2,1)S(1)}, u32[]{:S(2)}, u32[]{:S(2)}) collective-permute-start(f16[16,32,128]{2,1,0:T(8,128)(2,1)} %fusion.23), channel_id=1, source_target_pairs={{0,4},{2,6},{4,0},{6,2},{1,5},{3,7},{5,1},{7,3},{8,12},{10,14},{12... | collective-permute-start | bytes 393224 | tf_op jit(solution)/shard_map/ppermute | solution.py:93
  116.0 2.1 %collective-permute-start.32 = (f32[1,2,128]{2,1,0:T(2,128)S(1)}, f32[1,2,128]{2,1,0:T(2,128)S(1)}, u32[]{:S(2)}, u32[]{:S(2)}) collective-permute-start(f32[1,2,128]{2,1,0:T(2,128)S(1)} %bitcast.50), channel_id=1, source_target_pairs={{16,0},{72,8},{32,16},{88,24},{48,32},{104,40},{0,48},{120,56},{80... | collective-permute-start | bytes 3080 | tf_op jit(solution)/shard_map/ppermute | solution.py:32
  118.1 2.0 %collective-permute-done.24 = f16[2,24,32,128]{3,2,1,0:T(8,128)(2,1)S(1)} collective-permute-done((f16[2,24,32,128]{3,2,1,0:T(8,128)(2,1)S(1)}, f16[2,24,32,128]{3,2,1,0:T(8,128)(2,1)S(1)}, u32[]{:S(2)}, u32[]{:S(2)}) %collective-permute-start.24) | collective-permute-done | bytes 393248 | tf_op jit(solution)/shard_map/ppermute | solution.py:93
  120.2 1.8 %collective-permute-start.27 = (f16[24,32,128]{2,1,0:T(8,128)(2,1)S(1)}, f16[24,32,128]{2,1,0:T(8,128)(2,1)S(1)}, u32[]{:S(2)}, u32[]{:S(2)}) collective-permute-start(f16[24,32,128]{2,1,0:T(8,128)(2,1)S(1)} %fusion.22), channel_id=1, source_target_pairs={{0,4},{2,6},{4,0},{6,2},{1,5},{3,7},{5,1},{7,3},{8,12},{10,14},{12... | collective-permute-start | bytes 589832 | tf_op jit(solution)/shard_map/ppermute | solution.py:93
  125.3 1.6 %collective-permute-done.37 = f32[4,2,128]{2,1,0:T(2,128)S(1)} collective-permute-done((f32[4,2,128]{2,1,0:T(2,128)S(1)}, f32[4,2,128]{2,1,0:T(2,128)S(1)}, u32[]{:S(2)}, u32[]{:S(2)}) %collective-permute-start.37) | collective-permute-done | bytes 4128 | tf_op jit(solution)/shard_map/ppermute | solution.py:32
  131.5 4.6 %collective-permute-done.27 = f16[24,32,128]{2,1,0:T(8,128)(2,1)S(1)} collective-permute-done((f16[24,32,128]{2,1,0:T(8,128)(2,1)S(1)}, f16[24,32,128]{2,1,0:T(8,128)(2,1)S(1)}, u32[]{:S(2)}, u32[]{:S(2)}) %collective-permute-start.27) | collective-permute-done | bytes 196640 | tf_op jit(solution)/shard_map/ppermute | solution.py:93
  136.1 3.3 %collective-permute-done.25 = f16[24,32,128]{2,1,0:T(8,128)(2,1)} collective-permute-done((f16[24,32,128]{2,1,0:T(8,128)(2,1)S(1)}, f16[24,32,128]{2,1,0:T(8,128)(2,1)}, u32[]{:S(2)}, u32[]{:S(2)}) %collective-permute-start.25) | collective-permute-done | bytes 196640 | tf_op jit(solution)/shard_map/ppermute | solution.py:93
  139.5 1.5 %fusion.14 = (f32[24,32,128]{2,1,0:T(8,128)S(1)}, f32[24,32,128]{2,1,0:T(8,128)S(1)}) fusion(f16[24,32,128]{2,1,0:T(8,128)(2,1)} %collective-permute-done.25, f32[4,24,32,128]{3,2,1,0:T(8,128)} %gram.3, f32[32]{0:T(128)S(1)} %get-tuple-element.60, f32[32]{0:T(128)S(1)} %get-tuple-element.59, f16[2,24,32,128]{3,2,1,0:T(8,128)(2,1)} %copy-done.18, ...), kind=kLoop, calls=%fused_computation.24 | loop fusion | flops 1966080 | bytes 2359600 | tf_op jit(solution)/shard_map/mul | solution.py:363
  142.1 1.7 %fusion.20 = f32[64,32,128]{2,1,0:T(8,128)} fusion(f32[64,32,128]{2,1,0:T(8,128)} %fusion, f16[16,32,128]{2,1,0:T(8,128)(2,1)S(1)} %collective-permute-done.39, f32[4,16,32,128]{3,2,1,0:T(8,128)S(1)} %copy-done.17, f32[16,128]{1,0:T(8,128)S(1)} %slice.158, f32[32]{0:T(128)S(1)} %get-tuple-element.60, f32[32]{0:T(128)S(1)} %get-tuple-element.59, ...), kind=kLoop, calls=%fused_computation.32 | loop fusion | flops 720896 | bytes 794896 | tf_op jit(solution)/shard_map/scatter | solution.py:370
  (154 shorter events, 36.7 us)
Async XLA Ops:
  2.0 14.4 %collective-permute-start.2 = (bf16[1056,128]{1,0:T(8,128)(2,1)}, bf16[1056,128]{1,0:T(8,128)(2,1)S(1)}, u32[]{:S(2)}, u32[]{:S(2)}) collective-permute-start(bf16[1056,128]{1,0:T(8,128)(2,1)} %get-tuple-element.37), channel_id=1, source_target_pairs={{48,0},{200,8},{0,16},{216,24},{16,32},{232,40},{32,48},{248,56},{... | collective-permute-start | bytes 811016 | tf_op jit(solution)/shard_map/ppermute | solution.py:32
  3.5 12.9 %collective-permute-start.1 = (bf16[1056,128]{1,0:T(8,128)(2,1)}, bf16[1056,128]{1,0:T(8,128)(2,1)S(1)}, u32[]{:S(2)}, u32[]{:S(2)}) collective-permute-start(bf16[1056,128]{1,0:T(8,128)(2,1)} %get-tuple-element.37), channel_id=1, source_target_pairs={{32,0},{136,8},{48,16},{152,24},{0,32},{168,40},{16,48},{184,56},{... | collective-permute-start | bytes 811016 | tf_op jit(solution)/shard_map/ppermute | solution.py:32
  4.6 9.6 %collective-permute-start = (bf16[1056,128]{1,0:T(8,128)(2,1)}, bf16[1056,128]{1,0:T(8,128)(2,1)S(1)}, u32[]{:S(2)}, u32[]{:S(2)}) collective-permute-start(bf16[1056,128]{1,0:T(8,128)(2,1)} %get-tuple-element.37), channel_id=1, source_target_pairs={{16,0},{72,8},{32,16},{88,24},{48,32},{104,40},{0,48},{120,56},{80... | collective-permute-start | bytes 811016 | tf_op jit(solution)/shard_map/ppermute | solution.py:32
  14.2 47.8 %collective-permute-start.16 = (bf16[2112,128]{1,0:T(8,128)(2,1)S(1)}, bf16[2112,128]{1,0:T(8,128)(2,1)S(1)}, u32[]{:S(2)}, u32[]{:S(2)}) collective-permute-start(bf16[2112,128]{1,0:T(8,128)(2,1)S(1)} %constant_dynamic-update-slice_fusion.refs_3_), channel_id=1, source_target_pairs={{8,0},{0,8},{24,16},{16,24},{40,32},{32,40},{56,48},{48,56},{72,64... | collective-permute-start | bytes 1622024 | tf_op jit(solution)/shard_map/ppermute | solution.py:32
  14.3 47.8 %collective-permute-start.15 = (bf16[2112,128]{1,0:T(8,128)(2,1)S(1)}, bf16[2112,128]{1,0:T(8,128)(2,1)S(1)}, u32[]{:S(2)}, u32[]{:S(2)}) collective-permute-start(bf16[2112,128]{1,0:T(8,128)(2,1)S(1)} %constant_dynamic-update-slice_fusion.refs_3_), channel_id=1, source_target_pairs={{192,0},{56,8},{208,16},{8,24},{224,32},{24,40},{240,48},{40,56},{... | collective-permute-start | bytes 1622024 | tf_op jit(solution)/shard_map/ppermute | solution.py:32
  15.0 47.6 %collective-permute-start.10 = (bf16[2112,128]{1,0:T(8,128)(2,1)S(1)}, bf16[2112,128]{1,0:T(8,128)(2,1)S(1)}, u32[]{:S(2)}, u32[]{:S(2)}) collective-permute-start(bf16[2112,128]{1,0:T(8,128)(2,1)S(1)} %constant_dynamic-update-slice_fusion.refs_3_), channel_id=1, source_target_pairs={{64,0},{24,8},{80,16},{40,24},{96,32},{56,40},{112,48},{8,56},{128... | collective-permute-start | bytes 1622024 | tf_op jit(solution)/shard_map/ppermute | solution.py:32
  16.7 46.0 %collective-permute-start.13 = (bf16[2112,128]{1,0:T(8,128)(2,1)S(1)}, bf16[2112,128]{1,0:T(8,128)(2,1)S(1)}, u32[]{:S(2)}, u32[]{:S(2)}) collective-permute-start(bf16[2112,128]{1,0:T(8,128)(2,1)S(1)} %constant_dynamic-update-slice_fusion.2.refs_4_), channel_id=1, source_target_pairs={{192,0},{56,8},{208,16},{8,24},{224,32},{24,40},{240,48},{40,56},{... | collective-permute-start | bytes 1622024 | tf_op jit(solution)/shard_map/ppermute | solution.py:32
  18.6 11.3 %collective-permute-start.5 = (bf16[4,32,128]{2,1,0:T(8,128)(2,1)S(1)}, bf16[4,32,128]{2,1,0:T(8,128)(2,1)S(1)}, u32[]{:S(2)}, u32[]{:S(2)}) collective-permute-start(bf16[4,32,128]{2,1,0:T(8,128)(2,1)S(1)} %pad_maximum_fusion.refs_0_), channel_id=1, source_target_pairs={{192,0},{56,8},{208,16},{8,24},{224,32},{24,40},{240,48},{40,56},{... | collective-permute-start | bytes 98312 | tf_op jit(solution)/shard_map/ppermute | solution.py:32
  29.9 5.4 %collective-permute-start.4 = (bf16[4,32,128]{2,1,0:T(8,128)(2,1)S(1)}, bf16[4,32,128]{2,1,0:T(8,128)(2,1)S(1)}, u32[]{:S(2)}, u32[]{:S(2)}) collective-permute-start(bf16[4,32,128]{2,1,0:T(8,128)(2,1)S(1)} %pad_maximum_fusion.refs_0_), channel_id=1, source_target_pairs={{128,0},{40,8},{144,16},{56,24},{160,32},{8,40},{176,48},{24,56},{... | collective-permute-start | bytes 98312 | tf_op jit(solution)/shard_map/ppermute | solution.py:32
  35.3 5.1 %collective-permute-start.3 = (bf16[4,32,128]{2,1,0:T(8,128)(2,1)S(1)}, bf16[4,32,128]{2,1,0:T(8,128)(2,1)S(1)}, u32[]{:S(2)}, u32[]{:S(2)}) collective-permute-start(bf16[4,32,128]{2,1,0:T(8,128)(2,1)S(1)} %pad_maximum_fusion.refs_0_), channel_id=1, source_target_pairs={{64,0},{24,8},{80,16},{40,24},{96,32},{56,40},{112,48},{8,56},{128... | collective-permute-start | bytes 98312 | tf_op jit(solution)/shard_map/ppermute | solution.py:32
  47.1 6.4 %collective-permute-start.31 = (f32[2,128]{1,0:T(2,128)}, f32[2,128]{1,0:T(2,128)S(1)}, u32[]{:S(2)}, u32[]{:S(2)}) collective-permute-start(f32[2,128]{1,0:T(2,128)} %get-tuple-element.45), channel_id=1, source_target_pairs={{0,6},{2,4},{4,2},{6,0},{1,7},{3,5},{5,3},{7,1},{8,14},{10,12},{12... | collective-permute-start | bytes 3080 | tf_op jit(solution)/shard_map/ppermute | solution.py:93
  53.5 4.7 %collective-permute-start.30 = (f32[2,128]{1,0:T(2,128)}, f32[2,128]{1,0:T(2,128)S(1)}, u32[]{:S(2)}, u32[]{:S(2)}) collective-permute-start(f32[2,128]{1,0:T(2,128)} %get-tuple-element.45), channel_id=1, source_target_pairs={{0,4},{2,6},{4,0},{6,2},{1,5},{3,7},{5,1},{7,3},{8,12},{10,14},{12... | collective-permute-start | bytes 3080 | tf_op jit(solution)/shard_map/ppermute | solution.py:93
  58.2 3.8 %collective-permute-start.29 = (f32[2,128]{1,0:T(2,128)}, f32[2,128]{1,0:T(2,128)S(1)}, u32[]{:S(2)}, u32[]{:S(2)}) collective-permute-start(f32[2,128]{1,0:T(2,128)} %get-tuple-element.45), channel_id=1, source_target_pairs={{0,2},{2,0},{4,6},{6,4},{1,3},{3,1},{5,7},{7,5},{8,10},{10,8},{12,... | collective-permute-start | bytes 3080 | tf_op jit(solution)/shard_map/ppermute | solution.py:93
  62.0 5.7 %collective-permute-start.17 = (bf16[2112,128]{1,0:T(8,128)(2,1)S(1)}, bf16[2112,128]{1,0:T(8,128)(2,1)S(1)}, u32[]{:S(2)}, u32[]{:S(2)}) collective-permute-start(bf16[2112,128]{1,0:T(8,128)(2,1)S(1)} %constant_dynamic-update-slice_fusion.2.refs_4_), channel_id=1, source_target_pairs={{8,0},{0,8},{24,16},{16,24},{40,32},{32,40},{56,48},{48,56},{72,64... | collective-permute-start | bytes 1622024 | tf_op jit(solution)/shard_map/ppermute | solution.py:32
  62.0 10.6 %collective-permute-start.11 = (bf16[2112,128]{1,0:T(8,128)(2,1)S(1)}, bf16[2112,128]{1,0:T(8,128)(2,1)S(1)}, u32[]{:S(2)}, u32[]{:S(2)}) collective-permute-start(bf16[2112,128]{1,0:T(8,128)(2,1)S(1)} %constant_dynamic-update-slice_fusion.2.refs_4_), channel_id=1, source_target_pairs={{64,0},{24,8},{80,16},{40,24},{96,32},{56,40},{112,48},{8,56},{128... | collective-permute-start | bytes 1622024 | tf_op jit(solution)/shard_map/ppermute | solution.py:32
  62.1 10.5 %collective-permute-start.22 = (bf16[2112,128]{1,0:T(8,128)(2,1)S(1)}, bf16[2112,128]{1,0:T(8,128)(2,1)S(1)}, u32[]{:S(2)}, u32[]{:S(2)}) collective-permute-start(bf16[2112,128]{1,0:T(8,128)(2,1)S(1)} %collective-permute-done.15.refs_9_), channel_id=1, source_target_pairs={{8,0},{0,8},{24,16},{16,24},{40,32},{32,40},{56,48},{48,56},{72,64... | collective-permute-start | bytes 1622024 | tf_op jit(solution)/shard_map/ppermute | solution.py:32
  62.6 15.8 %collective-permute-start.12 = (bf16[2112,128]{1,0:T(8,128)(2,1)S(1)}, bf16[2112,128]{1,0:T(8,128)(2,1)S(1)}, u32[]{:S(2)}, u32[]{:S(2)}) collective-permute-start(bf16[2112,128]{1,0:T(8,128)(2,1)S(1)} %collective-permute-done.10.refs_5_), channel_id=1, source_target_pairs={{64,0},{24,8},{80,16},{40,24},{96,32},{56,40},{112,48},{8,56},{128... | collective-permute-start | bytes 1622024 | tf_op jit(solution)/shard_map/ppermute | solution.py:32
  62.7 15.8 %collective-permute-start.14 = (bf16[2112,128]{1,0:T(8,128)(2,1)S(1)}, bf16[2112,128]{1,0:T(8,128)(2,1)S(1)}, u32[]{:S(2)}, u32[]{:S(2)}) collective-permute-start(bf16[2112,128]{1,0:T(8,128)(2,1)S(1)} %collective-permute-done.13.refs_10_), channel_id=1, source_target_pairs={{192,0},{56,8},{208,16},{8,24},{224,32},{24,40},{240,48},{40,56},{... | collective-permute-start | bytes 1622024 | tf_op jit(solution)/shard_map/ppermute | solution.py:32
  67.7 11.9 %collective-permute-start.18 = (bf16[2112,128]{1,0:T(8,128)(2,1)S(1)}, bf16[2112,128]{1,0:T(8,128)(2,1)S(1)}, u32[]{:S(2)}, u32[]{:S(2)}) collective-permute-start(bf16[2112,128]{1,0:T(8,128)(2,1)S(1)} %collective-permute-done.10.refs_5_), channel_id=1, source_target_pairs={{8,0},{0,8},{24,16},{16,24},{40,32},{32,40},{56,48},{48,56},{72,64... | collective-permute-start | bytes 1622024 | tf_op jit(solution)/shard_map/ppermute | solution.py:32
  72.7 7.0 %collective-permute-start.23 = (bf16[2112,128]{1,0:T(8,128)(2,1)S(1)}, bf16[2112,128]{1,0:T(8,128)(2,1)S(1)}, u32[]{:S(2)}, u32[]{:S(2)}) collective-permute-start(bf16[2112,128]{1,0:T(8,128)(2,1)S(1)} %collective-permute-done.13.refs_10_), channel_id=1, source_target_pairs={{8,0},{0,8},{24,16},{16,24},{40,32},{32,40},{56,48},{48,56},{72,64... | collective-permute-start | bytes 1622024 | tf_op jit(solution)/shard_map/ppermute | solution.py:32
  72.7 7.0 %collective-permute-start.19 = (bf16[2112,128]{1,0:T(8,128)(2,1)S(1)}, bf16[2112,128]{1,0:T(8,128)(2,1)S(1)}, u32[]{:S(2)}, u32[]{:S(2)}) collective-permute-start(bf16[2112,128]{1,0:T(8,128)(2,1)S(1)} %collective-permute-done.11.refs_6_), channel_id=1, source_target_pairs={{8,0},{0,8},{24,16},{16,24},{40,32},{32,40},{56,48},{48,56},{72,64... | collective-permute-start | bytes 1622024 | tf_op jit(solution)/shard_map/ppermute | solution.py:32
  88.7 19.5 %collective-permute-start.28 = (f16[2,16,32,128]{3,2,1,0:T(8,128)(2,1)S(1)}, f16[2,16,32,128]{3,2,1,0:T(8,128)(2,1)}, u32[]{:S(2)}, u32[]{:S(2)}) collective-permute-start(f16[2,16,32,128]{3,2,1,0:T(8,128)(2,1)S(1)} %fusion.6), channel_id=1, source_target_pairs={{0,2},{2,0},{4,6},{6,4},{1,3},{3,1},{5,7},{7,5},{8,10},{10,8},{12,... | collective-permute-start | bytes 786440 | tf_op jit(solution)/shard_map/ppermute | solution.py:93
  98.0 14.8 %collective-permute-start.26 = (f16[2,24,32,128]{3,2,1,0:T(8,128)(2,1)S(1)}, f16[2,24,32,128]{3,2,1,0:T(8,128)(2,1)}, u32[]{:S(2)}, u32[]{:S(2)}) collective-permute-start(f16[2,24,32,128]{3,2,1,0:T(8,128)(2,1)S(1)} %fusion.2), channel_id=1, source_target_pairs={{0,2},{2,0},{4,6},{6,4},{1,3},{3,1},{5,7},{7,5},{8,10},{10,8},{12,... | collective-permute-start | bytes 1179656 | tf_op jit(solution)/shard_map/ppermute | solution.py:93
  106.6 13.5 %collective-permute-start.24 = (f16[2,24,32,128]{3,2,1,0:T(8,128)(2,1)S(1)}, f16[2,24,32,128]{3,2,1,0:T(8,128)(2,1)S(1)}, u32[]{:S(2)}, u32[]{:S(2)}) collective-permute-start(f16[2,24,32,128]{3,2,1,0:T(8,128)(2,1)S(1)} %fusion.4), channel_id=1, source_target_pairs={{0,2},{2,0},{4,6},{6,4},{1,3},{3,1},{5,7},{7,5},{8,10},{10,8},{12,... | collective-permute-start | bytes 1179656 | tf_op jit(solution)/shard_map/ppermute | solution.py:93
  109.9 32.2 %collective-permute-start.39 = (f16[16,32,128]{2,1,0:T(8,128)(2,1)}, f16[16,32,128]{2,1,0:T(8,128)(2,1)S(1)}, u32[]{:S(2)}, u32[]{:S(2)}) collective-permute-start(f16[16,32,128]{2,1,0:T(8,128)(2,1)} %fusion.23), channel_id=1, source_target_pairs={{0,4},{2,6},{4,0},{6,2},{1,5},{3,7},{5,1},{7,3},{8,12},{10,14},{12... | collective-permute-start | bytes 393224 | tf_op jit(solution)/shard_map/ppermute | solution.py:93
  113.9 9.3 %collective-permute-start.34 = (f32[1,2,128]{2,1,0:T(2,128)S(1)}, f32[1,2,128]{2,1,0:T(2,128)S(1)}, u32[]{:S(2)}, u32[]{:S(2)}) collective-permute-start(f32[1,2,128]{2,1,0:T(2,128)S(1)} %bitcast.48), channel_id=1, source_target_pairs={{48,0},{200,8},{0,16},{216,24},{16,32},{232,40},{32,48},{248,56},{... | collective-permute-start | bytes 3080 | tf_op jit(solution)/shard_map/ppermute | solution.py:32
  115.0 8.2 %collective-permute-start.33 = (f32[1,2,128]{2,1,0:T(2,128)S(1)}, f32[1,2,128]{2,1,0:T(2,128)S(1)}, u32[]{:S(2)}, u32[]{:S(2)}) collective-permute-start(f32[1,2,128]{2,1,0:T(2,128)S(1)} %bitcast.49), channel_id=1, source_target_pairs={{32,0},{136,8},{48,16},{152,24},{0,32},{168,40},{16,48},{184,56},{... | collective-permute-start | bytes 3080 | tf_op jit(solution)/shard_map/ppermute | solution.py:32
  116.0 7.2 %collective-permute-start.32 = (f32[1,2,128]{2,1,0:T(2,128)S(1)}, f32[1,2,128]{2,1,0:T(2,128)S(1)}, u32[]{:S(2)}, u32[]{:S(2)}) collective-permute-start(f32[1,2,128]{2,1,0:T(2,128)S(1)} %bitcast.50), channel_id=1, source_target_pairs={{16,0},{72,8},{32,16},{88,24},{48,32},{104,40},{0,48},{120,56},{80... | collective-permute-start | bytes 3080 | tf_op jit(solution)/shard_map/ppermute | solution.py:32
  120.2 16.0 %collective-permute-start.27 = (f16[24,32,128]{2,1,0:T(8,128)(2,1)S(1)}, f16[24,32,128]{2,1,0:T(8,128)(2,1)S(1)}, u32[]{:S(2)}, u32[]{:S(2)}) collective-permute-start(f16[24,32,128]{2,1,0:T(8,128)(2,1)S(1)} %fusion.22), channel_id=1, source_target_pairs={{0,4},{2,6},{4,0},{6,2},{1,5},{3,7},{5,1},{7,3},{8,12},{10,14},{12... | collective-permute-start | bytes 589832 | tf_op jit(solution)/shard_map/ppermute | solution.py:93
  123.3 5.2 %collective-permute-start.36 = (f32[4,2,128]{2,1,0:T(2,128)S(1)}, f32[4,2,128]{2,1,0:T(2,128)S(1)}, u32[]{:S(2)}, u32[]{:S(2)}) collective-permute-start(f32[4,2,128]{2,1,0:T(2,128)S(1)} %pad_maximum_fusion.2), channel_id=1, source_target_pairs={{128,0},{40,8},{144,16},{56,24},{160,32},{8,40},{176,48},{24,56},{... | collective-permute-start | bytes 12296 | tf_op jit(solution)/shard_map/ppermute | solution.py:32
  124.2 5.4 %collective-permute-start.35 = (f32[4,2,128]{2,1,0:T(2,128)S(1)}, f32[4,2,128]{2,1,0:T(2,128)S(1)}, u32[]{:S(2)}, u32[]{:S(2)}) collective-permute-start(f32[4,2,128]{2,1,0:T(2,128)S(1)} %pad_maximum_fusion.2), channel_id=1, source_target_pairs={{64,0},{24,8},{80,16},{40,24},{96,32},{56,40},{112,48},{8,56},{128... | collective-permute-start | bytes 12296 | tf_op jit(solution)/shard_map/ppermute | solution.py:32
  126.9 12.6 %collective-permute-start.25 = (f16[24,32,128]{2,1,0:T(8,128)(2,1)S(1)}, f16[24,32,128]{2,1,0:T(8,128)(2,1)}, u32[]{:S(2)}, u32[]{:S(2)}) collective-permute-start(f16[24,32,128]{2,1,0:T(8,128)(2,1)S(1)} %fusion.21), channel_id=1, source_target_pairs={{0,4},{2,6},{4,0},{6,2},{1,5},{3,7},{5,1},{7,3},{8,12},{10,14},{12... | collective-permute-start | bytes 589832 | tf_op jit(solution)/shard_map/ppermute | solution.py:93
  (40 other events, 526.6 us)

commit v4 on v3

--- a/solution.py
+++ b/solution.py
@@ -327,8 +327,9 @@
     small_parts = small_parts + [from_sibling(part) for part in small_parts]
     pieces = gather_rest(low, high)
     all_ids, len_rows, idf_tiles, left_tiles, stat = weigh(block_ids, small_parts, own_counts)
-    stats = [stat] + [swap_term(stat, bit, n_term) for bit in range(1, n_term)]
-    norm = lax.rsqrt(sum(stats) + epsilon)
+    square_pair = stat + swap_term(stat, 1, n_term)
+    square_sum = square_pair + swap_term(square_pair, 2, n_term)
+    norm = lax.rsqrt(square_sum + epsilon)
 
     kept = []
     ready = []

time: 145 us -> 140 us (0.966)
  waiting for transfers between devices: 60.5 us -> 56.5 us
    ppermute x9 -> x8, waiting for transfers between devices: 16.7 us -> 12 us  [swap_term(): return lax.ppermute(value, 'term', [(a, a ^ bit) for a in range(n_term)])]
    ppermute x9 -> x8, starting transfers between devices: 16.3 us -> 15.1 us  [swap_term(): return lax.ppermute(value, 'term', [(a, a ^ bit) for a in range(n_term)])]
  transfers between devices with their start and end apart: 40 -> 39, of which waited for: 21 -> 20; matrix products, arithmetic and copies ran while one was open for 11% -> 11% of each run, Pallas kernels for 11% -> 11%
where the time goes in v4:
time: 140 us; the launch traced here: 139 us
  waiting for transfers between devices  56.5 us (40%)
  starting transfers between devices  38.6 us (28%)
  Pallas kernels  22.9 us (16%)
  other arithmetic  15.2 us (11%)
  local copies, waits for them, and re-layouts  4.68 us (3%)
    ppermute x31, waiting for transfers between devices, permute_doc(): return lax.ppermute(value, 'doc', moves)  44.6 us
    ppermute x31, starting transfers between devices, permute_doc(): return lax.ppermute(value, 'doc', moves)  23.5 us
    pallas_call x3, Pallas kernels, gram_chunk(): pl.pallas_call(kernel, in_specs=[smem] * 3 + [anywhere] * (3 + len(pieces...  18.4 us
    ppermute x8, starting transfers between devices, swap_term(): return lax.ppermute(value, 'term', [(a, a ^ bit) for a in range(n_term)])  15.1 us
    ppermute x8, waiting for transfers between devices, swap_term(): return lax.ppermute(value, 'term', [(a, a ^ bit) for a in range(n_term)])  12 us
    convert_element_type x6, other arithmetic, pack_root(): return (jnp.sqrt(value) * ROOT_SCALE).astype(jnp.float16)  8.1 us
    unnamed x71, local copies, waits for them, and re-layouts  3.18 us
  transfers between devices with their start and end apart: 39, of which 20 were waited for; matrix products, arithmetic and copies ran while one was open for 11% of the time, Pallas kernels for 11%

profile of v4, /device:TPU:26, one launch (start us, length us, event | category | flops | bytes accessed | tf_op | source)
XLA Modules:
  0.0 139.0 jit_solution(16667880118587653403)
XLA Ops:
  0.0 2.0 %prepare.1 = (bf16[1056,128]{1,0:T(8,128)(2,1)}, bf16[2,128,512]{2,1,0:T(8,128)(2,1)}) custom-call(s32[2,4]{1,0:T(2,128)} %own_ref.5, s32[2,4]{1,0:T(2,128)} %live_ref.1, s32[2,128]{1,0:T(2,128)} %bitcast.52, s32[2,4,128,128]{3,2,1,0:T(8,128)} %count_ref.1), custom_call_target="tpu_custom_call" | custom-call | tf_op jit(solution)/shard_map/prepare/pallas_call | solution.py:121
  2.0 1.5 %collective-permute-start.2 = (bf16[1056,128]{1,0:T(8,128)(2,1)}, bf16[1056,128]{1,0:T(8,128)(2,1)S(1)}, u32[]{:S(2)}, u32[]{:S(2)}) collective-permute-start(bf16[1056,128]{1,0:T(8,128)(2,1)} %get-tuple-element.37), channel_id=1, source_target_pairs={{48,0},{200,8},{0,16},{216,24},{16,32},{232,40},{32,48},{248,56},{... | collective-permute-start | bytes 811016 | tf_op jit(solution)/shard_map/ppermute | solution.py:32
  4.6 2.2 %collective-permute-start = (bf16[1056,128]{1,0:T(8,128)(2,1)}, bf16[1056,128]{1,0:T(8,128)(2,1)S(1)}, u32[]{:S(2)}, u32[]{:S(2)}) collective-permute-start(bf16[1056,128]{1,0:T(8,128)(2,1)} %get-tuple-element.37), channel_id=1, source_target_pairs={{16,0},{72,8},{32,16},{88,24},{48,32},{104,40},{0,48},{120,56},{80... | collective-permute-start | bytes 811016 | tf_op jit(solution)/shard_map/ppermute | solution.py:32
  8.5 5.7 %collective-permute-done = bf16[1056,128]{1,0:T(8,128)(2,1)S(1)} collective-permute-done((bf16[1056,128]{1,0:T(8,128)(2,1)}, bf16[1056,128]{1,0:T(8,128)(2,1)S(1)}, u32[]{:S(2)}, u32[]{:S(2)}) %collective-permute-start) | collective-permute-done | bytes 270368 | tf_op jit(solution)/shard_map/ppermute | solution.py:32
  15.0 1.4 %collective-permute-start.10 = (bf16[2112,128]{1,0:T(8,128)(2,1)S(1)}, bf16[2112,128]{1,0:T(8,128)(2,1)S(1)}, u32[]{:S(2)}, u32[]{:S(2)}) collective-permute-start(bf16[2112,128]{1,0:T(8,128)(2,1)S(1)} %constant_dynamic-update-slice_fusion.refs_3_), channel_id=1, source_target_pairs={{64,0},{24,8},{80,16},{40,24},{96,32},{56,40},{112,48},{8,56},{128... | collective-permute-start | bytes 1622024 | tf_op jit(solution)/shard_map/ppermute | solution.py:32
  16.7 1.9 %collective-permute-start.13 = (bf16[2112,128]{1,0:T(8,128)(2,1)S(1)}, bf16[2112,128]{1,0:T(8,128)(2,1)S(1)}, u32[]{:S(2)}, u32[]{:S(2)}) collective-permute-start(bf16[2112,128]{1,0:T(8,128)(2,1)S(1)} %constant_dynamic-update-slice_fusion.2.refs_4_), channel_id=1, source_target_pairs={{192,0},{56,8},{208,16},{8,24},{224,32},{24,40},{240,48},{40,56},{... | collective-permute-start | bytes 1622024 | tf_op jit(solution)/shard_map/ppermute | solution.py:32
  19.6 10.3 %collective-permute-done.5.refs_3_ = bf16[4,32,128]{2,1,0:T(8,128)(2,1)S(1)} collective-permute-done((bf16[4,32,128]{2,1,0:T(8,128)(2,1)S(1)}, bf16[4,32,128]{2,1,0:T(8,128)(2,1)S(1)}, u32[]{:S(2)}, u32[]{:S(2)}) %collective-permute-start.5) | collective-permute-done | bytes 32800 | tf_op jit(solution)/shard_map/ppermute | solution.py:32
  31.1 4.2 %collective-permute-done.4.refs_2_ = bf16[4,32,128]{2,1,0:T(8,128)(2,1)S(1)} collective-permute-done((bf16[4,32,128]{2,1,0:T(8,128)(2,1)S(1)}, bf16[4,32,128]{2,1,0:T(8,128)(2,1)S(1)}, u32[]{:S(2)}, u32[]{:S(2)}) %collective-permute-start.4) | collective-permute-done | bytes 32800 | tf_op jit(solution)/shard_map/ppermute | solution.py:32
  36.1 4.4 %collective-permute-done.3.refs_1_ = bf16[4,32,128]{2,1,0:T(8,128)(2,1)S(1)} collective-permute-done((bf16[4,32,128]{2,1,0:T(8,128)(2,1)S(1)}, bf16[4,32,128]{2,1,0:T(8,128)(2,1)S(1)}, u32[]{:S(2)}, u32[]{:S(2)}) %collective-permute-start.3) | collective-permute-done | bytes 32800 | tf_op jit(solution)/shard_map/ppermute | solution.py:32
  44.7 2.5 %weigh.1 = (s32[2,128]{1,0:T(2,128)}, f32[32,8,128]{2,1,0:T(8,128)}, f32[8,128,128]{2,1,0:T(8,128)}, bf16[2,128,512]{2,1,0:T(8,128)(2,1)}, f32[2,128]{1,0:T(2,128)}) custom-call(s32[2,4]{1,0:T(2,128)} %own_ref.5, bf16[2,128,512]{2,1,0:T(8,128)(2,1)} %get-tuple-element.36.own_ref, bf16[4,32,128]{2,1,0:T(8,128)(2,1)} %copy-done.19, ...), custom_call_target="tpu_custom_call" | custom-call | tf_op jit(solution)/shard_map/weigh/pallas_call | solution.py:176
  47.2 1.9 %collective-permute-start.29 = (f32[2,128]{1,0:T(2,128)}, f32[2,128]{1,0:T(2,128)S(1)}, u32[]{:S(2)}, u32[]{:S(2)}) collective-permute-start(f32[2,128]{1,0:T(2,128)} %get-tuple-element.45), channel_id=1, source_target_pairs={{0,2},{2,0},{4,6},{6,4},{1,3},{3,1},{5,7},{7,5},{8,10},{10,8},{12,... | collective-permute-start | bytes 3080 | tf_op jit(solution)/shard_map/ppermute | solution.py:93
  49.1 1.7 %collective-permute-done.29 = f32[2,128]{1,0:T(2,128)S(1)} collective-permute-done((f32[2,128]{1,0:T(2,128)}, f32[2,128]{1,0:T(2,128)S(1)}, u32[]{:S(2)}, u32[]{:S(2)}) %collective-permute-start.29) | collective-permute-done | bytes 1056 | tf_op jit(solution)/shard_map/ppermute | solution.py:93
  51.5 3.3 %collective-permute-start.30 = (f32[2,128]{1,0:T(2,128)S(1)}, f32[2,128]{1,0:T(2,128)S(1)}, u32[]{:S(2)}, u32[]{:S(2)}) collective-permute-start(f32[2,128]{1,0:T(2,128)S(1)} %add.93), channel_id=1, source_target_pairs={{0,4},{2,6},{4,0},{6,2},{1,5},{3,7},{5,1},{7,3},{8,12},{10,14},{12... | collective-permute-start | bytes 3080 | tf_op jit(solution)/shard_map/ppermute | solution.py:93
  57.0 3.2 %collective-permute-start.14 = (bf16[2112,128]{1,0:T(8,128)(2,1)S(1)}, bf16[2112,128]{1,0:T(8,128)(2,1)S(1)}, u32[]{:S(2)}, u32[]{:S(2)}) collective-permute-start(bf16[2112,128]{1,0:T(8,128)(2,1)S(1)} %collective-permute-done.13.refs_10_), channel_id=1, source_target_pairs={{192,0},{56,8},{208,16},{8,24},{224,32},{24,40},{240,48},{40,56},{... | collective-permute-start | bytes 1622024 | tf_op jit(solution)/shard_map/ppermute | solution.py:32
  62.1 5.0 %collective-permute-done.11.refs_6_ = bf16[2112,128]{1,0:T(8,128)(2,1)S(1)} collective-permute-done((bf16[2112,128]{1,0:T(8,128)(2,1)S(1)}, bf16[2112,128]{1,0:T(8,128)(2,1)S(1)}, u32[]{:S(2)}, u32[]{:S(2)}) %collective-permute-start.11) | collective-permute-done | bytes 540704 | tf_op jit(solution)/shard_map/ppermute | solution.py:32
  67.7 5.3 %collective-permute-done.12.refs_7_ = bf16[2112,128]{1,0:T(8,128)(2,1)S(1)} collective-permute-done((bf16[2112,128]{1,0:T(8,128)(2,1)S(1)}, bf16[2112,128]{1,0:T(8,128)(2,1)S(1)}, u32[]{:S(2)}, u32[]{:S(2)}) %collective-permute-start.12) | collective-permute-done | bytes 540704 | tf_op jit(solution)/shard_map/ppermute | solution.py:32
  76.5 5.4 %gram.5 = f32[4,16,32,128]{3,2,1,0:T(8,128)} custom-call(s32[64,2]{1,0:T(8,128)} %copy.7.pair_ref, s32[2,4]{1,0:T(2,128)} %own_ref.5, s32[2,128]{1,0:T(2,128)} %get-tuple-element.38.ids_ref, bf16[2,128,512]{2,1,0:T(8,128)(2,1)} %get-tuple-element.39.refs_0_, f32[8,128,128]{2,1,0:T(8,128)} %get-tuple-element.40.refs_1_, ...), custom_call_target="tpu_custom_call" | custom-call | tf_op jit(solution)/shard_map/gram/pallas_call | solution.py:293
  83.1 2.0 %collective-permute-start.28 = (f16[2,16,32,128]{3,2,1,0:T(8,128)(2,1)S(1)}, f16[2,16,32,128]{3,2,1,0:T(8,128)(2,1)}, u32[]{:S(2)}, u32[]{:S(2)}) collective-permute-start(f16[2,16,32,128]{3,2,1,0:T(8,128)(2,1)S(1)} %fusion.6), channel_id=1, source_target_pairs={{0,2},{2,0},{4,6},{6,4},{1,3},{3,1},{5,7},{7,5},{8,10},{10,8},{12,... | collective-permute-start | bytes 786440 | tf_op jit(solution)/shard_map/ppermute | solution.py:93
  85.1 6.4 %gram.4 = f32[4,24,32,128]{3,2,1,0:T(8,128)} custom-call(s32[64,2]{1,0:T(8,128)} %copy.7.pair_ref, s32[2,4]{1,0:T(2,128)} %own_ref.5, s32[2,128]{1,0:T(2,128)} %get-tuple-element.38.ids_ref, bf16[2,128,512]{2,1,0:T(8,128)(2,1)} %get-tuple-element.39.refs_0_, f32[8,128,128]{2,1,0:T(8,128)} %get-tuple-element.40.refs_1_, ...), custom_call_target="tpu_custom_call" | custom-call | tf_op jit(solution)/shard_map/gram/pallas_call | solution.py:293
  93.2 6.6 %gram.3 = f32[4,24,32,128]{3,2,1,0:T(8,128)} custom-call(s32[64,2]{1,0:T(8,128)} %copy.7.pair_ref, s32[2,4]{1,0:T(2,128)} %own_ref.5, s32[2,128]{1,0:T(2,128)} %get-tuple-element.38.ids_ref, bf16[2,128,512]{2,1,0:T(8,128)(2,1)} %get-tuple-element.39.refs_0_, f32[8,128,128]{2,1,0:T(8,128)} %get-tuple-element.40.refs_1_, ...), custom_call_target="tpu_custom_call" | custom-call | tf_op jit(solution)/shard_map/gram/pallas_call | solution.py:293
  99.8 1.5 %fusion.4 = f16[2,24,32,128]{3,2,1,0:T(8,128)(2,1)S(1)} fusion(f32[4,24,32,128]{3,2,1,0:T(8,128)} %gram.3), kind=kLoop, calls=%fused_computation.9 | loop fusion | flops 393216 | bytes 1179648 | tf_op jit(solution)/shard_map/convert_element_type | solution.py:79
  101.3 1.9 %collective-permute-start.24 = (f16[2,24,32,128]{3,2,1,0:T(8,128)(2,1)S(1)}, f16[2,24,32,128]{3,2,1,0:T(8,128)(2,1)S(1)}, u32[]{:S(2)}, u32[]{:S(2)}) collective-permute-start(f16[2,24,32,128]{3,2,1,0:T(8,128)(2,1)S(1)} %fusion.4), channel_id=1, source_target_pairs={{0,2},{2,0},{4,6},{6,4},{1,3},{3,1},{5,7},{7,5},{8,10},{10,8},{12,... | collective-permute-start | bytes 1179656 | tf_op jit(solution)/shard_map/ppermute | solution.py:93
  103.2 1.7 %fusion.23 = f16[16,32,128]{2,1,0:T(8,128)(2,1)} fusion(f32[4,16,32,128]{3,2,1,0:T(8,128)S(1)} %copy-done.17, f16[2,16,32,128]{3,2,1,0:T(8,128)(2,1)} %collective-permute-done.28), kind=kLoop, calls=%fused_computation.35 | loop fusion | flops 393216 | bytes 524288 | tf_op jit(solution)/shard_map/convert_element_type | solution.py:79
  104.9 2.9 %collective-permute-start.38 = (f16[16,32,128]{2,1,0:T(8,128)(2,1)}, f16[16,32,128]{2,1,0:T(8,128)(2,1)S(1)}, u32[]{:S(2)}, u32[]{:S(2)}) collective-permute-start(f16[16,32,128]{2,1,0:T(8,128)(2,1)} %fusion.23), channel_id=1, source_target_pairs={{0,4},{2,6},{4,0},{6,2},{1,5},{3,7},{5,1},{7,3},{8,12},{10,14},{12... | collective-permute-start | bytes 393224 | tf_op jit(solution)/shard_map/ppermute | solution.py:93
  111.0 2.1 %collective-permute-start.31 = (f32[1,2,128]{2,1,0:T(2,128)S(1)}, f32[1,2,128]{2,1,0:T(2,128)S(1)}, u32[]{:S(2)}, u32[]{:S(2)}) collective-permute-start(f32[1,2,128]{2,1,0:T(2,128)S(1)} %bitcast.50), channel_id=1, source_target_pairs={{16,0},{72,8},{32,16},{88,24},{48,32},{104,40},{0,48},{120,56},{80... | collective-permute-start | bytes 3080 | tf_op jit(solution)/shard_map/ppermute | solution.py:32
  113.1 2.0 %collective-permute-done.24 = f16[2,24,32,128]{3,2,1,0:T(8,128)(2,1)S(1)} collective-permute-done((f16[2,24,32,128]{3,2,1,0:T(8,128)(2,1)S(1)}, f16[2,24,32,128]{3,2,1,0:T(8,128)(2,1)S(1)}, u32[]{:S(2)}, u32[]{:S(2)}) %collective-permute-start.24) | collective-permute-done | bytes 393248 | tf_op jit(solution)/shard_map/ppermute | solution.py:93
  115.1 1.9 %collective-permute-start.27 = (f16[24,32,128]{2,1,0:T(8,128)(2,1)S(1)}, f16[24,32,128]{2,1,0:T(8,128)(2,1)S(1)}, u32[]{:S(2)}, u32[]{:S(2)}) collective-permute-start(f16[24,32,128]{2,1,0:T(8,128)(2,1)S(1)} %fusion.22), channel_id=1, source_target_pairs={{0,4},{2,6},{4,0},{6,2},{1,5},{3,7},{5,1},{7,3},{8,12},{10,14},{12... | collective-permute-start | bytes 589832 | tf_op jit(solution)/shard_map/ppermute | solution.py:93
  120.3 1.6 %collective-permute-done.36 = f32[4,2,128]{2,1,0:T(2,128)S(1)} collective-permute-done((f32[4,2,128]{2,1,0:T(2,128)S(1)}, f32[4,2,128]{2,1,0:T(2,128)S(1)}, u32[]{:S(2)}, u32[]{:S(2)}) %collective-permute-start.36) | collective-permute-done | bytes 4128 | tf_op jit(solution)/shard_map/ppermute | solution.py:32
  126.6 4.6 %collective-permute-done.27 = f16[24,32,128]{2,1,0:T(8,128)(2,1)S(1)} collective-permute-done((f16[24,32,128]{2,1,0:T(8,128)(2,1)S(1)}, f16[24,32,128]{2,1,0:T(8,128)(2,1)S(1)}, u32[]{:S(2)}, u32[]{:S(2)}) %collective-permute-start.27) | collective-permute-done | bytes 196640 | tf_op jit(solution)/shard_map/ppermute | solution.py:93
  131.2 3.4 %collective-permute-done.25 = f16[24,32,128]{2,1,0:T(8,128)(2,1)} collective-permute-done((f16[24,32,128]{2,1,0:T(8,128)(2,1)S(1)}, f16[24,32,128]{2,1,0:T(8,128)(2,1)}, u32[]{:S(2)}, u32[]{:S(2)}) %collective-permute-start.25) | collective-permute-done | bytes 196640 | tf_op jit(solution)/shard_map/ppermute | solution.py:93
  134.6 1.5 %fusion.14 = (f32[24,32,128]{2,1,0:T(8,128)S(1)}, f32[24,32,128]{2,1,0:T(8,128)S(1)}) fusion(f16[24,32,128]{2,1,0:T(8,128)(2,1)} %collective-permute-done.25, f32[4,24,32,128]{3,2,1,0:T(8,128)} %gram.3, f32[32]{0:T(128)S(1)} %get-tuple-element.60, f32[32]{0:T(128)S(1)} %get-tuple-element.59, f16[2,24,32,128]{3,2,1,0:T(8,128)(2,1)} %copy-done.18, ...), kind=kLoop, calls=%fused_computation.24 | loop fusion | flops 1966080 | bytes 2359600 | tf_op jit(solution)/shard_map/mul | solution.py:364
  137.2 1.7 %fusion.20 = f32[64,32,128]{2,1,0:T(8,128)} fusion(f32[64,32,128]{2,1,0:T(8,128)} %fusion, f16[16,32,128]{2,1,0:T(8,128)(2,1)S(1)} %collective-permute-done.38, f32[4,16,32,128]{3,2,1,0:T(8,128)S(1)} %copy-done.17, f32[16,128]{1,0:T(8,128)S(1)} %slice.158, f32[32]{0:T(128)S(1)} %get-tuple-element.60, f32[32]{0:T(128)S(1)} %get-tuple-element.59, ...), kind=kLoop, calls=%fused_computation.32 | loop fusion | flops 720896 | bytes 794896 | tf_op jit(solution)/shard_map/scatter | solution.py:371
  (153 shorter events, 34.2 us)
Async XLA Ops:
  2.0 14.4 %collective-permute-start.2 = (bf16[1056,128]{1,0:T(8,128)(2,1)}, bf16[1056,128]{1,0:T(8,128)(2,1)S(1)}, u32[]{:S(2)}, u32[]{:S(2)}) collective-permute-start(bf16[1056,128]{1,0:T(8,128)(2,1)} %get-tuple-element.37), channel_id=1, source_target_pairs={{48,0},{200,8},{0,16},{216,24},{16,32},{232,40},{32,48},{248,56},{... | collective-permute-start | bytes 811016 | tf_op jit(solution)/shard_map/ppermute | solution.py:32
  3.5 12.9 %collective-permute-start.1 = (bf16[1056,128]{1,0:T(8,128)(2,1)}, bf16[1056,128]{1,0:T(8,128)(2,1)S(1)}, u32[]{:S(2)}, u32[]{:S(2)}) collective-permute-start(bf16[1056,128]{1,0:T(8,128)(2,1)} %get-tuple-element.37), channel_id=1, source_target_pairs={{32,0},{136,8},{48,16},{152,24},{0,32},{168,40},{16,48},{184,56},{... | collective-permute-start | bytes 811016 | tf_op jit(solution)/shard_map/ppermute | solution.py:32
  4.6 9.6 %collective-permute-start = (bf16[1056,128]{1,0:T(8,128)(2,1)}, bf16[1056,128]{1,0:T(8,128)(2,1)S(1)}, u32[]{:S(2)}, u32[]{:S(2)}) collective-permute-start(bf16[1056,128]{1,0:T(8,128)(2,1)} %get-tuple-element.37), channel_id=1, source_target_pairs={{16,0},{72,8},{32,16},{88,24},{48,32},{104,40},{0,48},{120,56},{80... | collective-permute-start | bytes 811016 | tf_op jit(solution)/shard_map/ppermute | solution.py:32
  14.2 42.1 %collective-permute-start.16 = (bf16[2112,128]{1,0:T(8,128)(2,1)S(1)}, bf16[2112,128]{1,0:T(8,128)(2,1)S(1)}, u32[]{:S(2)}, u32[]{:S(2)}) collective-permute-start(bf16[2112,128]{1,0:T(8,128)(2,1)S(1)} %constant_dynamic-update-slice_fusion.refs_3_), channel_id=1, source_target_pairs={{8,0},{0,8},{24,16},{16,24},{40,32},{32,40},{56,48},{48,56},{72,64... | collective-permute-start | bytes 1622024 | tf_op jit(solution)/shard_map/ppermute | solution.py:32
  14.3 42.3 %collective-permute-start.15 = (bf16[2112,128]{1,0:T(8,128)(2,1)S(1)}, bf16[2112,128]{1,0:T(8,128)(2,1)S(1)}, u32[]{:S(2)}, u32[]{:S(2)}) collective-permute-start(bf16[2112,128]{1,0:T(8,128)(2,1)S(1)} %constant_dynamic-update-slice_fusion.refs_3_), channel_id=1, source_target_pairs={{192,0},{56,8},{208,16},{8,24},{224,32},{24,40},{240,48},{40,56},{... | collective-permute-start | bytes 1622024 | tf_op jit(solution)/shard_map/ppermute | solution.py:32
  15.0 41.9 %collective-permute-start.10 = (bf16[2112,128]{1,0:T(8,128)(2,1)S(1)}, bf16[2112,128]{1,0:T(8,128)(2,1)S(1)}, u32[]{:S(2)}, u32[]{:S(2)}) collective-permute-start(bf16[2112,128]{1,0:T(8,128)(2,1)S(1)} %constant_dynamic-update-slice_fusion.refs_3_), channel_id=1, source_target_pairs={{64,0},{24,8},{80,16},{40,24},{96,32},{56,40},{112,48},{8,56},{128... | collective-permute-start | bytes 1622024 | tf_op jit(solution)/shard_map/ppermute | solution.py:32
  16.7 40.3 %collective-permute-start.13 = (bf16[2112,128]{1,0:T(8,128)(2,1)S(1)}, bf16[2112,128]{1,0:T(8,128)(2,1)S(1)}, u32[]{:S(2)}, u32[]{:S(2)}) collective-permute-start(bf16[2112,128]{1,0:T(8,128)(2,1)S(1)} %constant_dynamic-update-slice_fusion.2.refs_4_), channel_id=1, source_target_pairs={{192,0},{56,8},{208,16},{8,24},{224,32},{24,40},{240,48},{40,56},{... | collective-permute-start | bytes 1622024 | tf_op jit(solution)/shard_map/ppermute | solution.py:32
  18.6 11.3 %collective-permute-start.5 = (bf16[4,32,128]{2,1,0:T(8,128)(2,1)S(1)}, bf16[4,32,128]{2,1,0:T(8,128)(2,1)S(1)}, u32[]{:S(2)}, u32[]{:S(2)}) collective-permute-start(bf16[4,32,128]{2,1,0:T(8,128)(2,1)S(1)} %pad_maximum_fusion.refs_0_), channel_id=1, source_target_pairs={{192,0},{56,8},{208,16},{8,24},{224,32},{24,40},{240,48},{40,56},{... | collective-permute-start | bytes 98312 | tf_op jit(solution)/shard_map/ppermute | solution.py:32
  29.9 5.4 %collective-permute-start.4 = (bf16[4,32,128]{2,1,0:T(8,128)(2,1)S(1)}, bf16[4,32,128]{2,1,0:T(8,128)(2,1)S(1)}, u32[]{:S(2)}, u32[]{:S(2)}) collective-permute-start(bf16[4,32,128]{2,1,0:T(8,128)(2,1)S(1)} %pad_maximum_fusion.refs_0_), channel_id=1, source_target_pairs={{128,0},{40,8},{144,16},{56,24},{160,32},{8,40},{176,48},{24,56},{... | collective-permute-start | bytes 98312 | tf_op jit(solution)/shard_map/ppermute | solution.py:32
  35.3 5.1 %collective-permute-start.3 = (bf16[4,32,128]{2,1,0:T(8,128)(2,1)S(1)}, bf16[4,32,128]{2,1,0:T(8,128)(2,1)S(1)}, u32[]{:S(2)}, u32[]{:S(2)}) collective-permute-start(bf16[4,32,128]{2,1,0:T(8,128)(2,1)S(1)} %pad_maximum_fusion.refs_0_), channel_id=1, source_target_pairs={{64,0},{24,8},{80,16},{40,24},{96,32},{56,40},{112,48},{8,56},{128... | collective-permute-start | bytes 98312 | tf_op jit(solution)/shard_map/ppermute | solution.py:32
  47.2 3.6 %collective-permute-start.29 = (f32[2,128]{1,0:T(2,128)}, f32[2,128]{1,0:T(2,128)S(1)}, u32[]{:S(2)}, u32[]{:S(2)}) collective-permute-start(f32[2,128]{1,0:T(2,128)} %get-tuple-element.45), channel_id=1, source_target_pairs={{0,2},{2,0},{4,6},{6,4},{1,3},{3,1},{5,7},{7,5},{8,10},{10,8},{12,... | collective-permute-start | bytes 3080 | tf_op jit(solution)/shard_map/ppermute | solution.py:93
  51.5 4.8 %collective-permute-start.30 = (f32[2,128]{1,0:T(2,128)S(1)}, f32[2,128]{1,0:T(2,128)S(1)}, u32[]{:S(2)}, u32[]{:S(2)}) collective-permute-start(f32[2,128]{1,0:T(2,128)S(1)} %add.93), channel_id=1, source_target_pairs={{0,4},{2,6},{4,0},{6,2},{1,5},{3,7},{5,1},{7,3},{8,12},{10,14},{12... | collective-permute-start | bytes 3080 | tf_op jit(solution)/shard_map/ppermute | solution.py:93
  56.3 5.8 %collective-permute-start.17 = (bf16[2112,128]{1,0:T(8,128)(2,1)S(1)}, bf16[2112,128]{1,0:T(8,128)(2,1)S(1)}, u32[]{:S(2)}, u32[]{:S(2)}) collective-permute-start(bf16[2112,128]{1,0:T(8,128)(2,1)S(1)} %constant_dynamic-update-slice_fusion.2.refs_4_), channel_id=1, source_target_pairs={{8,0},{0,8},{24,16},{16,24},{40,32},{32,40},{56,48},{48,56},{72,64... | collective-permute-start | bytes 1622024 | tf_op jit(solution)/shard_map/ppermute | solution.py:32
  56.3 10.8 %collective-permute-start.11 = (bf16[2112,128]{1,0:T(8,128)(2,1)S(1)}, bf16[2112,128]{1,0:T(8,128)(2,1)S(1)}, u32[]{:S(2)}, u32[]{:S(2)}) collective-permute-start(bf16[2112,128]{1,0:T(8,128)(2,1)S(1)} %constant_dynamic-update-slice_fusion.2.refs_4_), channel_id=1, source_target_pairs={{64,0},{24,8},{80,16},{40,24},{96,32},{56,40},{112,48},{8,56},{128... | collective-permute-start | bytes 1622024 | tf_op jit(solution)/shard_map/ppermute | solution.py:32
  56.6 10.5 %collective-permute-start.22 = (bf16[2112,128]{1,0:T(8,128)(2,1)S(1)}, bf16[2112,128]{1,0:T(8,128)(2,1)S(1)}, u32[]{:S(2)}, u32[]{:S(2)}) collective-permute-start(bf16[2112,128]{1,0:T(8,128)(2,1)S(1)} %collective-permute-done.15.refs_9_), channel_id=1, source_target_pairs={{8,0},{0,8},{24,16},{16,24},{40,32},{32,40},{56,48},{48,56},{72,64... | collective-permute-start | bytes 1622024 | tf_op jit(solution)/shard_map/ppermute | solution.py:32
  56.9 16.0 %collective-permute-start.12 = (bf16[2112,128]{1,0:T(8,128)(2,1)S(1)}, bf16[2112,128]{1,0:T(8,128)(2,1)S(1)}, u32[]{:S(2)}, u32[]{:S(2)}) collective-permute-start(bf16[2112,128]{1,0:T(8,128)(2,1)S(1)} %collective-permute-done.10.refs_5_), channel_id=1, source_target_pairs={{64,0},{24,8},{80,16},{40,24},{96,32},{56,40},{112,48},{8,56},{128... | collective-permute-start | bytes 1622024 | tf_op jit(solution)/shard_map/ppermute | solution.py:32
  57.0 16.0 %collective-permute-start.14 = (bf16[2112,128]{1,0:T(8,128)(2,1)S(1)}, bf16[2112,128]{1,0:T(8,128)(2,1)S(1)}, u32[]{:S(2)}, u32[]{:S(2)}) collective-permute-start(bf16[2112,128]{1,0:T(8,128)(2,1)S(1)} %collective-permute-done.13.refs_10_), channel_id=1, source_target_pairs={{192,0},{56,8},{208,16},{8,24},{224,32},{24,40},{240,48},{40,56},{... | collective-permute-start | bytes 1622024 | tf_op jit(solution)/shard_map/ppermute | solution.py:32
  62.1 11.4 %collective-permute-start.18 = (bf16[2112,128]{1,0:T(8,128)(2,1)S(1)}, bf16[2112,128]{1,0:T(8,128)(2,1)S(1)}, u32[]{:S(2)}, u32[]{:S(2)}) collective-permute-start(bf16[2112,128]{1,0:T(8,128)(2,1)S(1)} %collective-permute-done.10.refs_5_), channel_id=1, source_target_pairs={{8,0},{0,8},{24,16},{16,24},{40,32},{32,40},{56,48},{48,56},{72,64... | collective-permute-start | bytes 1622024 | tf_op jit(solution)/shard_map/ppermute | solution.py:32
  67.1 6.4 %collective-permute-start.23 = (bf16[2112,128]{1,0:T(8,128)(2,1)S(1)}, bf16[2112,128]{1,0:T(8,128)(2,1)S(1)}, u32[]{:S(2)}, u32[]{:S(2)}) collective-permute-start(bf16[2112,128]{1,0:T(8,128)(2,1)S(1)} %collective-permute-done.13.refs_10_), channel_id=1, source_target_pairs={{8,0},{0,8},{24,16},{16,24},{40,32},{32,40},{56,48},{48,56},{72,64... | collective-permute-start | bytes 1622024 | tf_op jit(solution)/shard_map/ppermute | solution.py:32
  67.2 6.4 %collective-permute-start.19 = (bf16[2112,128]{1,0:T(8,128)(2,1)S(1)}, bf16[2112,128]{1,0:T(8,128)(2,1)S(1)}, u32[]{:S(2)}, u32[]{:S(2)}) collective-permute-start(bf16[2112,128]{1,0:T(8,128)(2,1)S(1)} %collective-permute-done.11.refs_6_), channel_id=1, source_target_pairs={{8,0},{0,8},{24,16},{16,24},{40,32},{32,40},{56,48},{48,56},{72,64... | collective-permute-start | bytes 1622024 | tf_op jit(solution)/shard_map/ppermute | solution.py:32
  83.1 20.1 %collective-permute-start.28 = (f16[2,16,32,128]{3,2,1,0:T(8,128)(2,1)S(1)}, f16[2,16,32,128]{3,2,1,0:T(8,128)(2,1)}, u32[]{:S(2)}, u32[]{:S(2)}) collective-permute-start(f16[2,16,32,128]{3,2,1,0:T(8,128)(2,1)S(1)} %fusion.6), channel_id=1, source_target_pairs={{0,2},{2,0},{4,6},{6,4},{1,3},{3,1},{5,7},{7,5},{8,10},{10,8},{12,... | collective-permute-start | bytes 786440 | tf_op jit(solution)/shard_map/ppermute | solution.py:93
  93.0 14.8 %collective-permute-start.26 = (f16[2,24,32,128]{3,2,1,0:T(8,128)(2,1)S(1)}, f16[2,24,32,128]{3,2,1,0:T(8,128)(2,1)}, u32[]{:S(2)}, u32[]{:S(2)}) collective-permute-start(f16[2,24,32,128]{3,2,1,0:T(8,128)(2,1)S(1)} %fusion.2), channel_id=1, source_target_pairs={{0,2},{2,0},{4,6},{6,4},{1,3},{3,1},{5,7},{7,5},{8,10},{10,8},{12,... | collective-permute-start | bytes 1179656 | tf_op jit(solution)/shard_map/ppermute | solution.py:93
  101.3 13.8 %collective-permute-start.24 = (f16[2,24,32,128]{3,2,1,0:T(8,128)(2,1)S(1)}, f16[2,24,32,128]{3,2,1,0:T(8,128)(2,1)S(1)}, u32[]{:S(2)}, u32[]{:S(2)}) collective-permute-start(f16[2,24,32,128]{3,2,1,0:T(8,128)(2,1)S(1)} %fusion.4), channel_id=1, source_target_pairs={{0,2},{2,0},{4,6},{6,4},{1,3},{3,1},{5,7},{7,5},{8,10},{10,8},{12,... | collective-permute-start | bytes 1179656 | tf_op jit(solution)/shard_map/ppermute | solution.py:93
  104.9 32.4 %collective-permute-start.38 = (f16[16,32,128]{2,1,0:T(8,128)(2,1)}, f16[16,32,128]{2,1,0:T(8,128)(2,1)S(1)}, u32[]{:S(2)}, u32[]{:S(2)}) collective-permute-start(f16[16,32,128]{2,1,0:T(8,128)(2,1)} %fusion.23), channel_id=1, source_target_pairs={{0,4},{2,6},{4,0},{6,2},{1,5},{3,7},{5,1},{7,3},{8,12},{10,14},{12... | collective-permute-start | bytes 393224 | tf_op jit(solution)/shard_map/ppermute | solution.py:93
  108.9 9.3 %collective-permute-start.33 = (f32[1,2,128]{2,1,0:T(2,128)S(1)}, f32[1,2,128]{2,1,0:T(2,128)S(1)}, u32[]{:S(2)}, u32[]{:S(2)}) collective-permute-start(f32[1,2,128]{2,1,0:T(2,128)S(1)} %bitcast.48), channel_id=1, source_target_pairs={{48,0},{200,8},{0,16},{216,24},{16,32},{232,40},{32,48},{248,56},{... | collective-permute-start | bytes 3080 | tf_op jit(solution)/shard_map/ppermute | solution.py:32
  110.0 8.2 %collective-permute-start.32 = (f32[1,2,128]{2,1,0:T(2,128)S(1)}, f32[1,2,128]{2,1,0:T(2,128)S(1)}, u32[]{:S(2)}, u32[]{:S(2)}) collective-permute-start(f32[1,2,128]{2,1,0:T(2,128)S(1)} %bitcast.49), channel_id=1, source_target_pairs={{32,0},{136,8},{48,16},{152,24},{0,32},{168,40},{16,48},{184,56},{... | collective-permute-start | bytes 3080 | tf_op jit(solution)/shard_map/ppermute | solution.py:32
  111.0 7.2 %collective-permute-start.31 = (f32[1,2,128]{2,1,0:T(2,128)S(1)}, f32[1,2,128]{2,1,0:T(2,128)S(1)}, u32[]{:S(2)}, u32[]{:S(2)}) collective-permute-start(f32[1,2,128]{2,1,0:T(2,128)S(1)} %bitcast.50), channel_id=1, source_target_pairs={{16,0},{72,8},{32,16},{88,24},{48,32},{104,40},{0,48},{120,56},{80... | collective-permute-start | bytes 3080 | tf_op jit(solution)/shard_map/ppermute | solution.py:32
  115.1 16.0 %collective-permute-start.27 = (f16[24,32,128]{2,1,0:T(8,128)(2,1)S(1)}, f16[24,32,128]{2,1,0:T(8,128)(2,1)S(1)}, u32[]{:S(2)}, u32[]{:S(2)}) collective-permute-start(f16[24,32,128]{2,1,0:T(8,128)(2,1)S(1)} %fusion.22), channel_id=1, source_target_pairs={{0,4},{2,6},{4,0},{6,2},{1,5},{3,7},{5,1},{7,3},{8,12},{10,14},{12... | collective-permute-start | bytes 589832 | tf_op jit(solution)/shard_map/ppermute | solution.py:93
  118.2 3.7 %collective-permute-start.36 = (f32[4,2,128]{2,1,0:T(2,128)S(1)}, f32[4,2,128]{2,1,0:T(2,128)S(1)}, u32[]{:S(2)}, u32[]{:S(2)}) collective-permute-start(f32[4,2,128]{2,1,0:T(2,128)S(1)} %pad_maximum_fusion.2), channel_id=1, source_target_pairs={{192,0},{56,8},{208,16},{8,24},{224,32},{24,40},{240,48},{40,56},{... | collective-permute-start | bytes 12296 | tf_op jit(solution)/shard_map/ppermute | solution.py:32
  118.3 5.2 %collective-permute-start.35 = (f32[4,2,128]{2,1,0:T(2,128)S(1)}, f32[4,2,128]{2,1,0:T(2,128)S(1)}, u32[]{:S(2)}, u32[]{:S(2)}) collective-permute-start(f32[4,2,128]{2,1,0:T(2,128)S(1)} %pad_maximum_fusion.2), channel_id=1, source_target_pairs={{128,0},{40,8},{144,16},{56,24},{160,32},{8,40},{176,48},{24,56},{... | collective-permute-start | bytes 12296 | tf_op jit(solution)/shard_map/ppermute | solution.py:32
  119.2 5.4 %collective-permute-start.34 = (f32[4,2,128]{2,1,0:T(2,128)S(1)}, f32[4,2,128]{2,1,0:T(2,128)S(1)}, u32[]{:S(2)}, u32[]{:S(2)}) collective-permute-start(f32[4,2,128]{2,1,0:T(2,128)S(1)} %pad_maximum_fusion.2), channel_id=1, source_target_pairs={{64,0},{24,8},{80,16},{40,24},{96,32},{56,40},{112,48},{8,56},{128... | collective-permute-start | bytes 12296 | tf_op jit(solution)/shard_map/ppermute | solution.py:32
  121.9 12.7 %collective-permute-start.25 = (f16[24,32,128]{2,1,0:T(8,128)(2,1)S(1)}, f16[24,32,128]{2,1,0:T(8,128)(2,1)}, u32[]{:S(2)}, u32[]{:S(2)}) collective-permute-start(f16[24,32,128]{2,1,0:T(8,128)(2,1)S(1)} %fusion.21), channel_id=1, source_target_pairs={{0,4},{2,6},{4,0},{6,2},{1,5},{3,7},{5,1},{7,3},{8,12},{10,14},{12... | collective-permute-start | bytes 589832 | tf_op jit(solution)/shard_map/ppermute | solution.py:93
  (39 other events, 509.7 us)

commit v5 on v2

--- a/solution.py
+++ b/solution.py
@@ -41,14 +41,6 @@
         return (y, x + shift, c) if c == phase else (y + shift, x, c)
 
     return permute_doc(value, source)
-
-
-def gather_ring(value, phase):
-    return jnp.concatenate([value] + [from_ring(value, phase, s) for s in (1, 2, 3)], axis=0)
-
-
-def gather_sibling(value):
-    return jnp.concatenate([value, from_sibling(value)], axis=0)
 
 
 def gather_rest(low, high):
@@ -66,19 +58,18 @@
 
 
 def place_right(doc, doc_at):
-    core = doc % CORES
-    dx = (doc // CORES - doc_at // CORES) % SIDE
-    dy = (doc // (SIDE * CORES) - doc_at // (SIDE * CORES)) % SIDE
-    dcore = (doc - doc_at) % CORES
-    inner = jnp.where(core == 0, dx, dy)
-    outer = jnp.where(core == 0, dy, dx)
-    piece = (dcore * SIDE + outer) * 2 + inner // 2
-    return piece, inner % 2, (dcore * SIDE + outer) * SIDE + inner
+    dx = ((doc >> 1) - (doc_at >> 1)) & (SIDE - 1)
+    dy = ((doc >> 3) - (doc_at >> 3)) & (SIDE - 1)
+    dcore = (doc ^ doc_at) & (CORES - 1)
+    inner = jnp.where((doc & 1) == 0, dx, dy)
+    outer = jnp.where((doc & 1) == 0, dy, dx)
+    plane = (dcore << 2) | outer
+    return (plane << 1) | (inner >> 1), inner & 1, (plane << 2) | inner
 
 
 def place_owner(owner, term_at):
     apart = owner ^ term_at
-    return (apart % 2) * 2 + apart // 2
+    return ((apart & 1) << 1) | (apart >> 1)
 
 
 def swap_term(value, bit, n_term):
@@ -196,7 +187,8 @@
         weight_hbm, idf_hbm, length_hbm = refs[n_term : n_term + 3]
         piece_refs = refs[n_term + 3 : n_term + 3 + len(pieces)]
         out_hbm, *scratch = refs[n_term + 3 + len(pieces) :]
-        weight_ref, idf_ref, length_ref, left_ref, tile_buf, gram_ref, loaded, arrived, written = scratch
+        weight_ref, idf_ref, length_ref, left_ref, tile_buf, gram_ref, note_ref = scratch[:7]
+        loaded, arrived, written = scratch[7:]
         loads = [
             pltpu.make_async_copy(src, dst, loaded.at[n])
             for n, (src, dst) in enumerate(
@@ -208,12 +200,13 @@
 
         def fetch(k, carry):
             right = pair_ref[first + k, 1]
-            piece, spot, _ = place_right(right // blocks, doc_at)
-            spot = spot * payload_rows + (right % blocks) * (slots * terms)
+            piece, spot, right_doc = place_right(right >> 1, doc_at)
+            note_ref[k] = right_doc
+            spot = spot * payload_rows + (right & 1) * (slots * terms)
             spot = pl.multiple_of(spot, SMALL_ROWS)
             for quad in range(len(pieces) // 4):
 
-                @pl.when(piece // 4 == quad)
+                @pl.when((piece >> 2) == quad)
                 def _():
                     for p in range(4 * quad, 4 * quad + 4):
 
@@ -249,10 +242,11 @@
             for p in range(UNROLL):
                 k = step * UNROLL + p
                 left = pair_ref[first + k, 0] - doc_at * blocks
-                right_block = pair_ref[first + k, 1] % blocks
-                _, _, right_doc = place_right(pair_ref[first + k, 1] // blocks, doc_at)
-                id_row = right_doc * own_slots // rows
-                id_at = right_doc * own_slots % rows + right_block * slots
+                right_block = pair_ref[first + k, 1] & 1
+                right_doc = note_ref[k]
+                id_row = right_doc >> 4
+                id_at = ((right_doc & 15) << 3) + right_block * slots
+                their_ids = [ids_ref[id_row, id_at + j] for j in range(slots)]
                 len_row = length_ref[right_doc, pl.ds(right_block, 1), :]
                 parts = []
                 for i in range(slots):
@@ -260,7 +254,7 @@
                     found = jnp.int32(0)
                     place = jnp.int32(0)
                     for j in range(slots):
-                        same = ids_ref[id_row, id_at + j] == wanted
+                        same = their_ids[j] == wanted
                         found = jnp.where(same, 1, found)
                         place = jnp.where(same, j, place)
                     start = pl.multiple_of(place * terms, terms)
@@ -303,6 +297,7 @@
             pltpu.VMEM(weight.shape, jnp.bfloat16),
             pltpu.VMEM((size, slots * terms, rows), jnp.bfloat16),
             pltpu.VMEM((n_term, size, part, rows), jnp.float32),
+            pltpu.SMEM((size,), jnp.int32),
             pltpu.SemaphoreType.DMA((3,)),
             pltpu.SemaphoreType.DMA((size,)),
             pltpu.SemaphoreType.DMA((groups,)),
@@ -334,12 +329,9 @@
     kept = []
     ready = []
     first = 0
-    chosen = pairs
-    for step, size in enumerate(CHUNKS):
-        if step >= 2:
-            chosen, _ = lax.optimization_barrier((chosen, ready[step - 2]))
+    for size in CHUNKS:
         grams = gram_chunk(
-            first, size, chosen, block_ids, all_ids, weight, squares, idf_tiles, len_rows, pieces
+            first, size, pairs, block_ids, all_ids, weight, squares, idf_tiles, len_rows, pieces
         )
         first += size
         near = swap_term(grams[2:].astype(jnp.float16), 1, n_term)
@@ -348,14 +340,19 @@
         far = swap_term(pass_on, 2, n_term)
         kept.append((grams, near, far))
     early, _ = lax.optimization_barrier((tuple(kept[:-1]), ready[-1]))
-    norm, _ = lax.optimization_barrier((lax.rsqrt(sum(squares) + epsilon), ready[-2]))
-    norm_ring = gather_ring(norm[None], 0)
-    norm_ring, _ = lax.optimization_barrier((norm_ring, ready[-1]))
-    norm_rows = gather_sibling(gather_ring(norm_ring, 1))
-    right = pairs[:, 1]
-    _, _, right_doc = place_right(right // blocks, doc_at)
-    norm_rows = norm_rows.reshape(n_doc * blocks, rows)[right_doc * blocks + right % blocks]
-    live = jnp.arange(pairs.shape[0], dtype=jnp.int32) < pair_count[0]
+    norm_rows = lax.rsqrt(sum(squares) + epsilon)[None]
+    for dy, dx, dcore in ((0, 0, 1), (0, 1, 0), (0, 2, 0), (1, 0, 0), (2, 0, 0)):
+        other = permute_doc(norm_rows, lambda y, x, c: (y + dy, x + dx, c + dcore))
+        norm_rows = jnp.concatenate([norm_rows, other], axis=0)
+    right, counted, doc_late, _ = lax.optimization_barrier(
+        (pairs[:, 1], pair_count, jnp.broadcast_to(doc_at, (1,)), ready[1])
+    )
+    doc = right >> 1
+    dx = ((doc >> 1) - (doc_late >> 1)) & (SIDE - 1)
+    dy = ((doc >> 3) - (doc_late >> 3)) & (SIDE - 1)
+    apart = (((dy * SIDE + dx) * CORES + ((doc ^ doc_late) & 1)) << 1) | (right & 1)
+    norm_rows = norm_rows.reshape(n_doc * blocks, rows)[apart]
+    live = jnp.arange(pairs.shape[0], dtype=jnp.int32) < counted[0]
     right_norm = jnp.where(live[:, None], norm_rows * (1.0 / GRAM_SCALE), 0.0)[:, None, :]
 
     def total(grams, near, far):

time: 145 us -> 138 us (0.952)
  the two profiles are of different devices: /device:TPU:1 before, /device:TPU:31 now
where the time goes in v5:
time: 138 us; the launch traced here: 137 us
  waiting for transfers between devices  56.4 us (41%)
  starting transfers between devices  38.3 us (28%)
  Pallas kernels  23.6 us (17%)
  other arithmetic  14.1 us (10%)
  local copies, waits for them, and re-layouts  3.83 us (3%)
    ppermute x29, waiting for transfers between devices, permute_doc(): return lax.ppermute(value, 'doc', moves)  33.1 us
    ppermute x29, starting transfers between devices, permute_doc(): return lax.ppermute(value, 'doc', moves)  28.6 us
    ppermute x9, waiting for transfers between devices, swap_term(): return lax.ppermute(value, 'term', [(a, a ^ bit) for a in range(n_term)])  23.3 us
    pallas_call x3, Pallas kernels, gram_chunk(): pl.pallas_call(kernel, in_specs=[smem] * 3 + [vmem] * n_term + [anywhere]...  19.1 us
    ppermute x9, starting transfers between devices, swap_term(): return lax.ppermute(value, 'term', [(a, a ^ bit) for a in range(n_term)])  9.72 us
    another operation x3, other arithmetic  5.08 us
    convert_element_type x3, other arithmetic, whole(): pass_on = (grams[1] + near[1].astype(jnp.float32)).astype(jnp.float16)  4.07 us
  transfers between devices with their start and end apart: 38, of which 18 were waited for; matrix products, arithmetic and copies ran while one was open for 10% of the time, Pallas kernels for 12%

profile of v5, /device:TPU:31, one launch (start us, length us, event | category | flops | bytes accessed | tf_op | source)
XLA Modules:
  0.0 137.2 jit_solution(18177846784969280114)
XLA Ops:
  0.0 2.0 %prepare.1 = (bf16[1056,128]{1,0:T(8,128)(2,1)}, bf16[2,128,512]{2,1,0:T(8,128)(2,1)}) custom-call(s32[2,4]{1,0:T(2,128)} %own_ref.5, s32[2,4]{1,0:T(2,128)} %live_ref.1, s32[2,128]{1,0:T(2,128)} %bitcast.38, s32[2,4,128,128]{3,2,1,0:T(8,128)} %count_ref.1), custom_call_target="tpu_custom_call" | custom-call | tf_op jit(solution)/shard_map/prepare/pallas_call | solution.py:104
  2.0 2.2 %collective-permute-start.1 = (bf16[1056,128]{1,0:T(8,128)(2,1)}, bf16[1056,128]{1,0:T(8,128)(2,1)S(1)}, u32[]{:S(2)}, u32[]{:S(2)}) collective-permute-start(bf16[1056,128]{1,0:T(8,128)(2,1)} %get-tuple-element.38), channel_id=1, source_target_pairs={{32,0},{136,8},{48,16},{152,24},{0,32},{168,40},{16,48},{184,56},{... | collective-permute-start | bytes 811016 | tf_op jit(solution)/shard_map/ppermute | solution.py:32
  6.0 1.8 %collective-permute-done.2 = bf16[1056,128]{1,0:T(8,128)(2,1)S(1)} collective-permute-done((bf16[1056,128]{1,0:T(8,128)(2,1)}, bf16[1056,128]{1,0:T(8,128)(2,1)S(1)}, u32[]{:S(2)}, u32[]{:S(2)}) %collective-permute-start.2) | collective-permute-done | bytes 270368 | tf_op jit(solution)/shard_map/ppermute | solution.py:32
  7.8 1.6 %collective-permute-done.1 = bf16[1056,128]{1,0:T(8,128)(2,1)S(1)} collective-permute-done((bf16[1056,128]{1,0:T(8,128)(2,1)}, bf16[1056,128]{1,0:T(8,128)(2,1)S(1)}, u32[]{:S(2)}, u32[]{:S(2)}) %collective-permute-start.1) | collective-permute-done | bytes 270368 | tf_op jit(solution)/shard_map/ppermute | solution.py:32
  9.4 2.9 %collective-permute-done = bf16[1056,128]{1,0:T(8,128)(2,1)S(1)} collective-permute-done((bf16[1056,128]{1,0:T(8,128)(2,1)}, bf16[1056,128]{1,0:T(8,128)(2,1)S(1)}, u32[]{:S(2)}, u32[]{:S(2)}) %collective-permute-start) | collective-permute-done | bytes 270368 | tf_op jit(solution)/shard_map/ppermute | solution.py:32
  12.3 2.0 %collective-permute-start.6 = (bf16[4,32,128]{2,1,0:T(8,128)(2,1)S(1)}, bf16[4,32,128]{2,1,0:T(8,128)(2,1)S(1)}, u32[]{:S(2)}, u32[]{:S(2)}) collective-permute-start(bf16[4,32,128]{2,1,0:T(8,128)(2,1)S(1)} %pad_maximum_fusion.refs_0_), channel_id=1, source_target_pairs={{8,0},{0,8},{24,16},{16,24},{40,32},{32,40},{56,48},{48,56},{72,64... | collective-permute-start | bytes 98312 | tf_op jit(solution)/shard_map/ppermute | solution.py:32
  14.7 2.1 %collective-permute-start.4 = (bf16[4,32,128]{2,1,0:T(8,128)(2,1)S(1)}, bf16[4,32,128]{2,1,0:T(8,128)(2,1)S(1)}, u32[]{:S(2)}, u32[]{:S(2)}) collective-permute-start(bf16[4,32,128]{2,1,0:T(8,128)(2,1)S(1)} %pad_maximum_fusion.refs_0_), channel_id=1, source_target_pairs={{128,0},{40,8},{144,16},{56,24},{160,32},{8,40},{176,48},{24,56},{... | collective-permute-start | bytes 98312 | tf_op jit(solution)/shard_map/ppermute | solution.py:32
  19.0 2.8 %collective-permute-start.8 = (bf16[4,32,128]{2,1,0:T(8,128)(2,1)S(1)}, bf16[4,32,128]{2,1,0:T(8,128)(2,1)S(1)}, u32[]{:S(2)}, u32[]{:S(2)}) collective-permute-start(bf16[4,32,128]{2,1,0:T(8,128)(2,1)S(1)} %collective-permute-done.4.refs_2_), channel_id=1, source_target_pairs={{8,0},{0,8},{24,16},{16,24},{40,32},{32,40},{56,48},{48,56},{72,64... | collective-permute-start | bytes 98312 | tf_op jit(solution)/shard_map/ppermute | solution.py:32
  23.8 2.5 %weigh.1 = (s32[2,128]{1,0:T(2,128)}, f32[32,8,128]{2,1,0:T(8,128)}, f32[8,128,128]{2,1,0:T(8,128)}, f32[2,128,512]{2,1,0:T(8,128)}, f32[2,128]{1,0:T(2,128)}) custom-call(s32[2,4]{1,0:T(2,128)} %own_ref.5, bf16[2,128,512]{2,1,0:T(8,128)(2,1)} %get-tuple-element.37.own_ref, bf16[4,32,128]{2,1,0:T(8,128)(2,1)} %copy-done.10, bf16[4,32,128]{2,1,0:T(8,128)(2,1)} %copy-done.14, ...), custom_call_target="tpu_custom_call" | custom-call | tf_op jit(solution)/shard_map/weigh/pallas_call | solution.py:159
  26.3 4.3 %collective-permute-start.12 = (f32[2,128]{1,0:T(2,128)}, f32[2,128]{1,0:T(2,128)S(1)}, u32[]{:S(2)}, u32[]{:S(2)}) collective-permute-start(f32[2,128]{1,0:T(2,128)} %get-tuple-element.40.refs_0_), channel_id=1, source_target_pairs={{0,6},{2,4},{4,2},{6,0},{1,7},{3,5},{5,3},{7,1},{8,14},{10,12},{12... | collective-permute-start | bytes 3080 | tf_op jit(solution)/shard_map/ppermute | solution.py:76
  32.4 1.6 %collective-permute-done.11.refs_2_ = f32[2,128]{1,0:T(2,128)S(1)} collective-permute-done((f32[2,128]{1,0:T(2,128)}, f32[2,128]{1,0:T(2,128)S(1)}, u32[]{:S(2)}, u32[]{:S(2)}) %collective-permute-start.11) | collective-permute-done | bytes 1056 | tf_op jit(solution)/shard_map/ppermute | solution.py:76
  38.8 3.3 %collective-permute-done.33 = f32[2,2,128]{2,1,0:T(2,128)S(1)} collective-permute-done((f32[2,2,128]{2,1,0:T(2,128)S(1)}, f32[2,2,128]{2,1,0:T(2,128)S(1)}, u32[]{:S(2)}, u32[]{:S(2)}) %collective-permute-start.33) | collective-permute-done | bytes 2080 | tf_op jit(solution)/shard_map/ppermute | solution.py:32
  42.6 3.4 %collective-permute-done.34 = f32[4,2,128]{2,1,0:T(2,128)S(1)} collective-permute-done((f32[4,2,128]{2,1,0:T(2,128)S(1)}, f32[4,2,128]{2,1,0:T(2,128)S(1)}, u32[]{:S(2)}, u32[]{:S(2)}) %collective-permute-start.34) | collective-permute-done | bytes 4128 | tf_op jit(solution)/shard_map/ppermute | solution.py:32
  46.8 2.9 %collective-permute-done.35 = f32[8,2,128]{2,1,0:T(2,128)S(1)} collective-permute-done((f32[8,2,128]{2,1,0:T(2,128)S(1)}, f32[8,2,128]{2,1,0:T(2,128)S(1)}, u32[]{:S(2)}, u32[]{:S(2)}) %collective-permute-start.35) | collective-permute-done | bytes 8224 | tf_op jit(solution)/shard_map/ppermute | solution.py:32
  50.4 3.5 %collective-permute-done.36 = f32[16,2,128]{2,1,0:T(2,128)S(1)} collective-permute-done((f32[16,2,128]{2,1,0:T(2,128)S(1)}, f32[16,2,128]{2,1,0:T(2,128)S(1)}, u32[]{:S(2)}, u32[]{:S(2)}) %collective-permute-start.36) | collective-permute-done | bytes 16416 | tf_op jit(solution)/shard_map/ppermute | solution.py:32
  53.9 4.6 %collective-permute-start.20 = (bf16[2112,128]{1,0:T(8,128)(2,1)S(1)}, bf16[2112,128]{1,0:T(8,128)(2,1)S(1)}, u32[]{:S(2)}, u32[]{:S(2)}) collective-permute-start(bf16[2112,128]{1,0:T(8,128)(2,1)S(1)} %constant_dynamic-update-slice_fusion.2.refs_8_), channel_id=1, source_target_pairs={{8,0},{0,8},{24,16},{16,24},{40,32},{32,40},{56,48},{48,56},{72,64... | collective-permute-start | bytes 1622024 | tf_op jit(solution)/shard_map/ppermute | solution.py:32
  58.9 2.6 %collective-permute-start.17 = (bf16[2112,128]{1,0:T(8,128)(2,1)S(1)}, bf16[2112,128]{1,0:T(8,128)(2,1)}, u32[]{:S(2)}, u32[]{:S(2)}) collective-permute-start(bf16[2112,128]{1,0:T(8,128)(2,1)S(1)} %collective-permute-done.16.refs_14_), channel_id=1, source_target_pairs={{192,0},{56,8},{208,16},{8,24},{224,32},{24,40},{240,48},{40,56},{... | collective-permute-start | bytes 1622024 | tf_op jit(solution)/shard_map/ppermute | solution.py:32
  62.5 5.9 %collective-permute-done.14.refs_10_ = bf16[2112,128]{1,0:T(8,128)(2,1)} collective-permute-done((bf16[2112,128]{1,0:T(8,128)(2,1)S(1)}, bf16[2112,128]{1,0:T(8,128)(2,1)}, u32[]{:S(2)}, u32[]{:S(2)}) %collective-permute-start.14) | collective-permute-done | bytes 540704 | tf_op jit(solution)/shard_map/ppermute | solution.py:32
  69.4 4.8 %collective-permute-done.15.refs_11_ = bf16[2112,128]{1,0:T(8,128)(2,1)} collective-permute-done((bf16[2112,128]{1,0:T(8,128)(2,1)S(1)}, bf16[2112,128]{1,0:T(8,128)(2,1)}, u32[]{:S(2)}, u32[]{:S(2)}) %collective-permute-start.15) | collective-permute-done | bytes 540704 | tf_op jit(solution)/shard_map/ppermute | solution.py:32
  77.9 5.6 %gram.5 = f32[4,16,32,128]{3,2,1,0:T(8,128)} custom-call(s32[64,2]{1,0:T(8,128)} %copy.7.pair_ref, s32[2,4]{1,0:T(2,128)} %own_ref.5, s32[2,128]{1,0:T(2,128)} %get-tuple-element.39.ids_ref, f32[2,128]{1,0:T(2,128)} %get-tuple-element.40.refs_0_, f32[2,128]{1,0:T(2,128)} %copy-done.20, f32[2,128]{1,0:T(2,128)} %copy-done.19, f32[2,128]{1,0:T(2,128)} %copy-done.18, ...), custom_call_target="tpu_custom_call" | custom-call | tf_op jit(solution)/shard_map/gram/pallas_call | solution.py:288
  83.5 1.8 %slice_convert_fusion.2 = f16[2,16,32,128]{3,2,1,0:T(8,128)(2,1)} fusion(f32[4,16,32,128]{3,2,1,0:T(8,128)} %gram.5), kind=kLoop, calls=%fused_computation.6 | loop fusion | flops 131072 | bytes 786432 | tf_op jit(solution)/shard_map/convert
  85.3 6.6 %gram.4 = f32[4,24,32,128]{3,2,1,0:T(8,128)} custom-call(s32[64,2]{1,0:T(8,128)} %copy.7.pair_ref, s32[2,4]{1,0:T(2,128)} %own_ref.5, s32[2,128]{1,0:T(2,128)} %get-tuple-element.39.ids_ref, f32[2,128]{1,0:T(2,128)} %get-tuple-element.40.refs_0_, f32[2,128]{1,0:T(2,128)} %copy-done.20, f32[2,128]{1,0:T(2,128)} %copy-done.19, f32[2,128]{1,0:T(2,128)} %copy-done.18, ...), custom_call_target="tpu_custom_call" | custom-call | tf_op jit(solution)/shard_map/gram/pallas_call | solution.py:288
  91.9 2.0 %slice_convert_fusion = f16[2,24,32,128]{3,2,1,0:T(8,128)(2,1)} fusion(f32[4,24,32,128]{3,2,1,0:T(8,128)} %gram.4), kind=kLoop, calls=%fused_computation.4 | loop fusion | flops 196608 | bytes 1179648 | tf_op jit(solution)/shard_map/convert.1
  93.9 1.5 %collective-permute-start.29 = (f16[2,24,32,128]{3,2,1,0:T(8,128)(2,1)}, f16[2,24,32,128]{3,2,1,0:T(8,128)(2,1)S(1)}, u32[]{:S(2)}, u32[]{:S(2)}) collective-permute-start(f16[2,24,32,128]{3,2,1,0:T(8,128)(2,1)} %slice_convert_fusion), channel_id=1, source_target_pairs={{0,2},{2,0},{4,6},{6,4},{1,3},{3,1},{5,7},{7,5},{8,10},{10,8},{12,... | collective-permute-start | bytes 1179656 | tf_op jit(solution)/shard_map/ppermute | solution.py:76
  95.3 6.9 %gram.3 = f32[4,24,32,128]{3,2,1,0:T(8,128)} custom-call(s32[64,2]{1,0:T(8,128)} %copy.7.pair_ref, s32[2,4]{1,0:T(2,128)} %own_ref.5, s32[2,128]{1,0:T(2,128)} %get-tuple-element.39.ids_ref, f32[2,128]{1,0:T(2,128)} %get-tuple-element.40.refs_0_, f32[2,128]{1,0:T(2,128)} %copy-done.20, f32[2,128]{1,0:T(2,128)} %copy-done.19, f32[2,128]{1,0:T(2,128)} %copy-done.18, ...), custom_call_target="tpu_custom_call" | custom-call | tf_op jit(solution)/shard_map/gram/pallas_call | solution.py:288
  103.7 1.6 %fusion.8 = f16[16,32,128]{2,1,0:T(8,128)(2,1)} fusion(f32[4,16,32,128]{3,2,1,0:T(8,128)S(1)} %copy-done.9, f16[2,16,32,128]{3,2,1,0:T(8,128)(2,1)} %collective-permute-done.31), kind=kLoop, calls=%fused_computation.20 | loop fusion | flops 196608 | bytes 524288 | tf_op jit(solution)/shard_map/convert_element_type | solution.py:338
  105.3 3.4 %collective-permute-start.37 = (f16[16,32,128]{2,1,0:T(8,128)(2,1)}, f16[16,32,128]{2,1,0:T(8,128)(2,1)}, u32[]{:S(2)}, u32[]{:S(2)}) collective-permute-start(f16[16,32,128]{2,1,0:T(8,128)(2,1)} %fusion.8), channel_id=1, source_target_pairs={{0,4},{2,6},{4,0},{6,2},{1,5},{3,7},{5,1},{7,3},{8,12},{10,14},{12... | collective-permute-start | bytes 393224 | tf_op jit(solution)/shard_map/ppermute | solution.py:76
  109.5 10.5 %collective-permute-done.27 = f16[2,24,32,128]{3,2,1,0:T(8,128)(2,1)S(1)} collective-permute-done((f16[2,24,32,128]{3,2,1,0:T(8,128)(2,1)S(1)}, f16[2,24,32,128]{3,2,1,0:T(8,128)(2,1)S(1)}, u32[]{:S(2)}, u32[]{:S(2)}) %collective-permute-start.27) | collective-permute-done | bytes 393248 | tf_op jit(solution)/shard_map/ppermute | solution.py:76
  120.0 1.7 %fusion.6 = f16[24,32,128]{2,1,0:T(8,128)(2,1)} fusion(f32[4,24,32,128]{3,2,1,0:T(8,128)} %gram.3, f16[2,24,32,128]{3,2,1,0:T(8,128)(2,1)S(1)} %collective-permute-done.27), kind=kLoop, calls=%fused_computation.18 | loop fusion | flops 294912 | bytes 786432 | tf_op jit(solution)/shard_map/convert_element_type | solution.py:338
  122.4 10.6 %collective-permute-done.28 = f16[24,32,128]{2,1,0:T(8,128)(2,1)} collective-permute-done((f16[24,32,128]{2,1,0:T(8,128)(2,1)}, f16[24,32,128]{2,1,0:T(8,128)(2,1)}, u32[]{:S(2)}, u32[]{:S(2)}) %collective-permute-start.28) | collective-permute-done | bytes 196640 | tf_op jit(solution)/shard_map/ppermute | solution.py:76
  133.0 1.3 bitcast_add_fusion
  135.5 1.7 %fusion.5 = f32[64,32,128]{2,1,0:T(8,128)} fusion(f32[64,32,128]{2,1,0:T(8,128)} %fusion, f16[16,32,128]{2,1,0:T(8,128)(2,1)} %collective-permute-done.37, f32[4,16,32,128]{3,2,1,0:T(8,128)S(1)} %copy-done.9, f32[16,128]{1,0:T(8,128)S(1)} %slice.124, f16[2,16,32,128]{3,2,1,0:T(8,128)(2,1)} %collective-permute-done.31), kind=kLoop, calls=%fused_computation.17 | loop fusion | flops 327680 | bytes 794624 | tf_op jit(solution)/shard_map/scatter | solution.py:365
  (129 shorter events, 24.1 us)
Async XLA Ops:
  2.0 5.8 %collective-permute-start.2 = (bf16[1056,128]{1,0:T(8,128)(2,1)}, bf16[1056,128]{1,0:T(8,128)(2,1)S(1)}, u32[]{:S(2)}, u32[]{:S(2)}) collective-permute-start(bf16[1056,128]{1,0:T(8,128)(2,1)} %get-tuple-element.38), channel_id=1, source_target_pairs={{48,0},{200,8},{0,16},{216,24},{16,32},{232,40},{32,48},{248,56},{... | collective-permute-start | bytes 811016 | tf_op jit(solution)/shard_map/ppermute | solution.py:32
  2.0 7.4 %collective-permute-start.1 = (bf16[1056,128]{1,0:T(8,128)(2,1)}, bf16[1056,128]{1,0:T(8,128)(2,1)S(1)}, u32[]{:S(2)}, u32[]{:S(2)}) collective-permute-start(bf16[1056,128]{1,0:T(8,128)(2,1)} %get-tuple-element.38), channel_id=1, source_target_pairs={{32,0},{136,8},{48,16},{152,24},{0,32},{168,40},{16,48},{184,56},{... | collective-permute-start | bytes 811016 | tf_op jit(solution)/shard_map/ppermute | solution.py:32
  4.2 8.1 %collective-permute-start = (bf16[1056,128]{1,0:T(8,128)(2,1)}, bf16[1056,128]{1,0:T(8,128)(2,1)S(1)}, u32[]{:S(2)}, u32[]{:S(2)}) collective-permute-start(bf16[1056,128]{1,0:T(8,128)(2,1)} %get-tuple-element.38), channel_id=1, source_target_pairs={{16,0},{72,8},{32,16},{88,24},{48,32},{104,40},{0,48},{120,56},{80... | collective-permute-start | bytes 811016 | tf_op jit(solution)/shard_map/ppermute | solution.py:32
  12.3 10.1 %collective-permute-start.6 = (bf16[4,32,128]{2,1,0:T(8,128)(2,1)S(1)}, bf16[4,32,128]{2,1,0:T(8,128)(2,1)S(1)}, u32[]{:S(2)}, u32[]{:S(2)}) collective-permute-start(bf16[4,32,128]{2,1,0:T(8,128)(2,1)S(1)} %pad_maximum_fusion.refs_0_), channel_id=1, source_target_pairs={{8,0},{0,8},{24,16},{16,24},{40,32},{32,40},{56,48},{48,56},{72,64... | collective-permute-start | bytes 98312 | tf_op jit(solution)/shard_map/ppermute | solution.py:32
  14.7 4.3 %collective-permute-start.4 = (bf16[4,32,128]{2,1,0:T(8,128)(2,1)S(1)}, bf16[4,32,128]{2,1,0:T(8,128)(2,1)S(1)}, u32[]{:S(2)}, u32[]{:S(2)}) collective-permute-start(bf16[4,32,128]{2,1,0:T(8,128)(2,1)S(1)} %pad_maximum_fusion.refs_0_), channel_id=1, source_target_pairs={{128,0},{40,8},{144,16},{56,24},{160,32},{8,40},{176,48},{24,56},{... | collective-permute-start | bytes 98312 | tf_op jit(solution)/shard_map/ppermute | solution.py:32
  16.8 5.0 %collective-permute-start.3 = (bf16[4,32,128]{2,1,0:T(8,128)(2,1)S(1)}, bf16[4,32,128]{2,1,0:T(8,128)(2,1)S(1)}, u32[]{:S(2)}, u32[]{:S(2)}) collective-permute-start(bf16[4,32,128]{2,1,0:T(8,128)(2,1)S(1)} %pad_maximum_fusion.refs_0_), channel_id=1, source_target_pairs={{64,0},{24,8},{80,16},{40,24},{96,32},{56,40},{112,48},{8,56},{128... | collective-permute-start | bytes 98312 | tf_op jit(solution)/shard_map/ppermute | solution.py:32
  17.0 41.6 %collective-permute-start.19 = (bf16[2112,128]{1,0:T(8,128)(2,1)S(1)}, bf16[2112,128]{1,0:T(8,128)(2,1)S(1)}, u32[]{:S(2)}, u32[]{:S(2)}) collective-permute-start(bf16[2112,128]{1,0:T(8,128)(2,1)S(1)} %constant_dynamic-update-slice_fusion.refs_7_), channel_id=1, source_target_pairs={{8,0},{0,8},{24,16},{16,24},{40,32},{32,40},{56,48},{48,56},{72,64... | collective-permute-start | bytes 1622024 | tf_op jit(solution)/shard_map/ppermute | solution.py:32
  17.4 5.5 %collective-permute-start.9 = (bf16[4,32,128]{2,1,0:T(8,128)(2,1)S(1)}, bf16[4,32,128]{2,1,0:T(8,128)(2,1)S(1)}, u32[]{:S(2)}, u32[]{:S(2)}) collective-permute-start(bf16[4,32,128]{2,1,0:T(8,128)(2,1)S(1)} %collective-permute-done.5.refs_3_), channel_id=1, source_target_pairs={{8,0},{0,8},{24,16},{16,24},{40,32},{32,40},{56,48},{48,56},{72,64... | collective-permute-start | bytes 98312 | tf_op jit(solution)/shard_map/ppermute | solution.py:32
  19.0 3.9 %collective-permute-start.8 = (bf16[4,32,128]{2,1,0:T(8,128)(2,1)S(1)}, bf16[4,32,128]{2,1,0:T(8,128)(2,1)S(1)}, u32[]{:S(2)}, u32[]{:S(2)}) collective-permute-start(bf16[4,32,128]{2,1,0:T(8,128)(2,1)S(1)} %collective-permute-done.4.refs_2_), channel_id=1, source_target_pairs={{8,0},{0,8},{24,16},{16,24},{40,32},{32,40},{56,48},{48,56},{72,64... | collective-permute-start | bytes 98312 | tf_op jit(solution)/shard_map/ppermute | solution.py:32
  22.4 36.2 %collective-permute-start.18 = (bf16[2112,128]{1,0:T(8,128)(2,1)S(1)}, bf16[2112,128]{1,0:T(8,128)(2,1)S(1)}, u32[]{:S(2)}, u32[]{:S(2)}) collective-permute-start(bf16[2112,128]{1,0:T(8,128)(2,1)S(1)} %constant_dynamic-update-slice_fusion.refs_7_), channel_id=1, source_target_pairs={{192,0},{56,8},{208,16},{8,24},{224,32},{24,40},{240,48},{40,56},{... | collective-permute-start | bytes 1622024 | tf_op jit(solution)/shard_map/ppermute | solution.py:32
  26.3 5.4 %collective-permute-start.12 = (f32[2,128]{1,0:T(2,128)}, f32[2,128]{1,0:T(2,128)S(1)}, u32[]{:S(2)}, u32[]{:S(2)}) collective-permute-start(f32[2,128]{1,0:T(2,128)} %get-tuple-element.40.refs_0_), channel_id=1, source_target_pairs={{0,6},{2,4},{4,2},{6,0},{1,7},{3,5},{5,3},{7,1},{8,14},{10,12},{12... | collective-permute-start | bytes 3080 | tf_op jit(solution)/shard_map/ppermute | solution.py:76
  30.7 4.7 %collective-permute-start.10 = (f32[2,128]{1,0:T(2,128)}, f32[2,128]{1,0:T(2,128)S(1)}, u32[]{:S(2)}, u32[]{:S(2)}) collective-permute-start(f32[2,128]{1,0:T(2,128)} %get-tuple-element.40.refs_0_), channel_id=1, source_target_pairs={{0,2},{2,0},{4,6},{6,4},{1,3},{3,1},{5,7},{7,5},{8,10},{10,8},{12,... | collective-permute-start | bytes 3080 | tf_op jit(solution)/shard_map/ppermute | solution.py:76
  31.7 27.1 %collective-permute-start.13 = (bf16[2112,128]{1,0:T(8,128)(2,1)S(1)}, bf16[2112,128]{1,0:T(8,128)(2,1)S(1)}, u32[]{:S(2)}, u32[]{:S(2)}) collective-permute-start(bf16[2112,128]{1,0:T(8,128)(2,1)S(1)} %constant_dynamic-update-slice_fusion.refs_7_), channel_id=1, source_target_pairs={{64,0},{24,8},{80,16},{40,24},{96,32},{56,40},{112,48},{8,56},{128... | collective-permute-start | bytes 1622024 | tf_op jit(solution)/shard_map/ppermute | solution.py:32
  34.0 24.9 %collective-permute-start.16 = (bf16[2112,128]{1,0:T(8,128)(2,1)S(1)}, bf16[2112,128]{1,0:T(8,128)(2,1)S(1)}, u32[]{:S(2)}, u32[]{:S(2)}) collective-permute-start(bf16[2112,128]{1,0:T(8,128)(2,1)S(1)} %constant_dynamic-update-slice_fusion.2.refs_8_), channel_id=1, source_target_pairs={{192,0},{56,8},{208,16},{8,24},{224,32},{24,40},{240,48},{40,56},{... | collective-permute-start | bytes 1622024 | tf_op jit(solution)/shard_map/ppermute | solution.py:32
  38.1 3.9 %collective-permute-start.33 = (f32[2,2,128]{2,1,0:T(2,128)S(1)}, f32[2,2,128]{2,1,0:T(2,128)S(1)}, u32[]{:S(2)}, u32[]{:S(2)}) collective-permute-start(f32[2,2,128]{2,1,0:T(2,128)S(1)} %pad_maximum_fusion.3), channel_id=1, source_target_pairs={{16,0},{24,8},{32,16},{40,24},{48,32},{56,40},{0,48},{8,56},{80,64... | collective-permute-start | bytes 6152 | tf_op jit(solution)/shard_map/ppermute | solution.py:32
  42.1 4.0 %collective-permute-start.34 = (f32[4,2,128]{2,1,0:T(2,128)S(1)}, f32[4,2,128]{2,1,0:T(2,128)S(1)}, u32[]{:S(2)}, u32[]{:S(2)}) collective-permute-start(f32[4,2,128]{2,1,0:T(2,128)S(1)} %pad_maximum_fusion.2), channel_id=1, source_target_pairs={{32,0},{40,8},{48,16},{56,24},{0,32},{8,40},{16,48},{24,56},{96,64... | collective-permute-start | bytes 12296 | tf_op jit(solution)/shard_map/ppermute | solution.py:32
  46.0 3.7 %collective-permute-start.35 = (f32[8,2,128]{2,1,0:T(2,128)S(1)}, f32[8,2,128]{2,1,0:T(2,128)S(1)}, u32[]{:S(2)}, u32[]{:S(2)}) collective-permute-start(f32[8,2,128]{2,1,0:T(2,128)S(1)} %pad_maximum_fusion.1), channel_id=1, source_target_pairs={{64,0},{72,8},{80,16},{88,24},{96,32},{104,40},{112,48},{120,56},{... | collective-permute-start | bytes 24584 | tf_op jit(solution)/shard_map/ppermute | solution.py:32
  49.8 4.2 %collective-permute-start.36 = (f32[16,2,128]{2,1,0:T(2,128)S(1)}, f32[16,2,128]{2,1,0:T(2,128)S(1)}, u32[]{:S(2)}, u32[]{:S(2)}) collective-permute-start(f32[16,2,128]{2,1,0:T(2,128)S(1)} %get-tuple-element.59), channel_id=1, source_target_pairs={{128,0},{136,8},{144,16},{152,24},{160,32},{168,40},{176,48},{184,... | collective-permute-start | bytes 49160 | tf_op jit(solution)/shard_map/ppermute | solution.py:32
  53.9 7.6 %collective-permute-start.20 = (bf16[2112,128]{1,0:T(8,128)(2,1)S(1)}, bf16[2112,128]{1,0:T(8,128)(2,1)S(1)}, u32[]{:S(2)}, u32[]{:S(2)}) collective-permute-start(bf16[2112,128]{1,0:T(8,128)(2,1)S(1)} %constant_dynamic-update-slice_fusion.2.refs_8_), channel_id=1, source_target_pairs={{8,0},{0,8},{24,16},{16,24},{40,32},{32,40},{56,48},{48,56},{72,64... | collective-permute-start | bytes 1622024 | tf_op jit(solution)/shard_map/ppermute | solution.py:32
  58.6 9.8 %collective-permute-start.14 = (bf16[2112,128]{1,0:T(8,128)(2,1)S(1)}, bf16[2112,128]{1,0:T(8,128)(2,1)}, u32[]{:S(2)}, u32[]{:S(2)}) collective-permute-start(bf16[2112,128]{1,0:T(8,128)(2,1)S(1)} %constant_dynamic-update-slice_fusion.2.refs_8_), channel_id=1, source_target_pairs={{64,0},{24,8},{80,16},{40,24},{96,32},{56,40},{112,48},{8,56},{128... | collective-permute-start | bytes 1622024 | tf_op jit(solution)/shard_map/ppermute | solution.py:32
  58.6 10.7 %collective-permute-start.25 = (bf16[2112,128]{1,0:T(8,128)(2,1)S(1)}, bf16[2112,128]{1,0:T(8,128)(2,1)S(1)}, u32[]{:S(2)}, u32[]{:S(2)}) collective-permute-start(bf16[2112,128]{1,0:T(8,128)(2,1)S(1)} %collective-permute-done.18.refs_13_), channel_id=1, source_target_pairs={{8,0},{0,8},{24,16},{16,24},{40,32},{32,40},{56,48},{48,56},{72,64... | collective-permute-start | bytes 1622024 | tf_op jit(solution)/shard_map/ppermute | solution.py:32
  58.8 15.4 %collective-permute-start.15 = (bf16[2112,128]{1,0:T(8,128)(2,1)S(1)}, bf16[2112,128]{1,0:T(8,128)(2,1)}, u32[]{:S(2)}, u32[]{:S(2)}) collective-permute-start(bf16[2112,128]{1,0:T(8,128)(2,1)S(1)} %collective-permute-done.13.refs_9_), channel_id=1, source_target_pairs={{64,0},{24,8},{80,16},{40,24},{96,32},{56,40},{112,48},{8,56},{128... | collective-permute-start | bytes 1622024 | tf_op jit(solution)/shard_map/ppermute | solution.py:32
  58.9 16.2 %collective-permute-start.17 = (bf16[2112,128]{1,0:T(8,128)(2,1)S(1)}, bf16[2112,128]{1,0:T(8,128)(2,1)}, u32[]{:S(2)}, u32[]{:S(2)}) collective-permute-start(bf16[2112,128]{1,0:T(8,128)(2,1)S(1)} %collective-permute-done.16.refs_14_), channel_id=1, source_target_pairs={{192,0},{56,8},{208,16},{8,24},{224,32},{24,40},{240,48},{40,56},{... | collective-permute-start | bytes 1622024 | tf_op jit(solution)/shard_map/ppermute | solution.py:32
  61.5 15.1 %collective-permute-start.21 = (bf16[2112,128]{1,0:T(8,128)(2,1)S(1)}, bf16[2112,128]{1,0:T(8,128)(2,1)}, u32[]{:S(2)}, u32[]{:S(2)}) collective-permute-start(bf16[2112,128]{1,0:T(8,128)(2,1)S(1)} %collective-permute-done.13.refs_9_), channel_id=1, source_target_pairs={{8,0},{0,8},{24,16},{16,24},{40,32},{32,40},{56,48},{48,56},{72,64... | collective-permute-start | bytes 1622024 | tf_op jit(solution)/shard_map/ppermute | solution.py:32
  68.4 8.2 %collective-permute-start.26 = (bf16[2112,128]{1,0:T(8,128)(2,1)S(1)}, bf16[2112,128]{1,0:T(8,128)(2,1)}, u32[]{:S(2)}, u32[]{:S(2)}) collective-permute-start(bf16[2112,128]{1,0:T(8,128)(2,1)S(1)} %collective-permute-done.16.refs_14_), channel_id=1, source_target_pairs={{8,0},{0,8},{24,16},{16,24},{40,32},{32,40},{56,48},{48,56},{72,64... | collective-permute-start | bytes 1622024 | tf_op jit(solution)/shard_map/ppermute | solution.py:32
  69.4 7.3 %collective-permute-start.22 = (bf16[2112,128]{1,0:T(8,128)(2,1)}, bf16[2112,128]{1,0:T(8,128)(2,1)}, u32[]{:S(2)}, u32[]{:S(2)}) collective-permute-start(bf16[2112,128]{1,0:T(8,128)(2,1)} %collective-permute-done.14.refs_10_), channel_id=1, source_target_pairs={{8,0},{0,8},{24,16},{16,24},{40,32},{32,40},{56,48},{48,56},{72,64... | collective-permute-start | bytes 1622024 | tf_op jit(solution)/shard_map/ppermute | solution.py:32
  85.3 18.4 %collective-permute-start.31 = (f16[2,16,32,128]{3,2,1,0:T(8,128)(2,1)}, f16[2,16,32,128]{3,2,1,0:T(8,128)(2,1)}, u32[]{:S(2)}, u32[]{:S(2)}) collective-permute-start(f16[2,16,32,128]{3,2,1,0:T(8,128)(2,1)} %slice_convert_fusion.2), channel_id=1, source_target_pairs={{0,2},{2,0},{4,6},{6,4},{1,3},{3,1},{5,7},{7,5},{8,10},{10,8},{12,... | collective-permute-start | bytes 786440 | tf_op jit(solution)/shard_map/ppermute | solution.py:76
  93.9 14.8 %collective-permute-start.29 = (f16[2,24,32,128]{3,2,1,0:T(8,128)(2,1)}, f16[2,24,32,128]{3,2,1,0:T(8,128)(2,1)S(1)}, u32[]{:S(2)}, u32[]{:S(2)}) collective-permute-start(f16[2,24,32,128]{3,2,1,0:T(8,128)(2,1)} %slice_convert_fusion), channel_id=1, source_target_pairs={{0,2},{2,0},{4,6},{6,4},{1,3},{3,1},{5,7},{7,5},{8,10},{10,8},{12,... | collective-permute-start | bytes 1179656 | tf_op jit(solution)/shard_map/ppermute | solution.py:76
  103.5 16.4 %collective-permute-start.27 = (f16[2,24,32,128]{3,2,1,0:T(8,128)(2,1)S(1)}, f16[2,24,32,128]{3,2,1,0:T(8,128)(2,1)S(1)}, u32[]{:S(2)}, u32[]{:S(2)}) collective-permute-start(f16[2,24,32,128]{3,2,1,0:T(8,128)(2,1)S(1)} %slice_convert_fusion.1), channel_id=1, source_target_pairs={{0,2},{2,0},{4,6},{6,4},{1,3},{3,1},{5,7},{7,5},{8,10},{10,8},{12,... | collective-permute-start | bytes 1179656 | tf_op jit(solution)/shard_map/ppermute | solution.py:76
  105.3 30.2 %collective-permute-start.37 = (f16[16,32,128]{2,1,0:T(8,128)(2,1)}, f16[16,32,128]{2,1,0:T(8,128)(2,1)}, u32[]{:S(2)}, u32[]{:S(2)}) collective-permute-start(f16[16,32,128]{2,1,0:T(8,128)(2,1)} %fusion.8), channel_id=1, source_target_pairs={{0,4},{2,6},{4,0},{6,2},{1,5},{3,7},{5,1},{7,3},{8,12},{10,14},{12... | collective-permute-start | bytes 393224 | tf_op jit(solution)/shard_map/ppermute | solution.py:76
  109.4 13.0 %collective-permute-start.30 = (f16[24,32,128]{2,1,0:T(8,128)(2,1)}, f16[24,32,128]{2,1,0:T(8,128)(2,1)}, u32[]{:S(2)}, u32[]{:S(2)}) collective-permute-start(f16[24,32,128]{2,1,0:T(8,128)(2,1)} %fusion.7), channel_id=1, source_target_pairs={{0,4},{2,6},{4,0},{6,2},{1,5},{3,7},{5,1},{7,3},{8,12},{10,14},{12... | collective-permute-start | bytes 589832 | tf_op jit(solution)/shard_map/ppermute | solution.py:76
  121.7 11.3 %collective-permute-start.28 = (f16[24,32,128]{2,1,0:T(8,128)(2,1)}, f16[24,32,128]{2,1,0:T(8,128)(2,1)}, u32[]{:S(2)}, u32[]{:S(2)}) collective-permute-start(f16[24,32,128]{2,1,0:T(8,128)(2,1)} %fusion.6), channel_id=1, source_target_pairs={{0,4},{2,6},{4,0},{6,2},{1,5},{3,7},{5,1},{7,3},{8,12},{10,14},{12... | collective-permute-start | bytes 589832 | tf_op jit(solution)/shard_map/ppermute | solution.py:76
  (28 other events, 466.7 us)

commit v6 on v5

--- a/solution.py
+++ b/solution.py
@@ -9,7 +9,7 @@
 SIDE = 4
 CORES = 2
 UNROLL = 4
-CHUNKS = (24, 24, 16)
+CHUNKS = (36, 28)
 GRAM_SCALE = 32.0
 SMALL_ROWS = 32
 
@@ -339,14 +339,14 @@
         ready.append(pass_on)
         far = swap_term(pass_on, 2, n_term)
         kept.append((grams, near, far))
-    early, _ = lax.optimization_barrier((tuple(kept[:-1]), ready[-1]))
-    norm_rows = lax.rsqrt(sum(squares) + epsilon)[None]
+    late_squares, late_pairs, counted, doc_late, _ = lax.optimization_barrier(
+        (squares, pairs, pair_count, jnp.broadcast_to(doc_at, (1,)), kept[0][0])
+    )
+    norm_rows = lax.rsqrt(sum(late_squares) + epsilon)[None]
     for dy, dx, dcore in ((0, 0, 1), (0, 1, 0), (0, 2, 0), (1, 0, 0), (2, 0, 0)):
         other = permute_doc(norm_rows, lambda y, x, c: (y + dy, x + dx, c + dcore))
         norm_rows = jnp.concatenate([norm_rows, other], axis=0)
-    right, counted, doc_late, _ = lax.optimization_barrier(
-        (pairs[:, 1], pair_count, jnp.broadcast_to(doc_at, (1,)), ready[1])
-    )
+    right = late_pairs[:, 1]
     doc = right >> 1
     dx = ((doc >> 1) - (doc_late >> 1)) & (SIDE - 1)
     dy = ((doc >> 3) - (doc_late >> 3)) & (SIDE - 1)
@@ -354,15 +354,12 @@
     norm_rows = norm_rows.reshape(n_doc * blocks, rows)[apart]
     live = jnp.arange(pairs.shape[0], dtype=jnp.int32) < counted[0]
     right_norm = jnp.where(live[:, None], norm_rows * (1.0 / GRAM_SCALE), 0.0)[:, None, :]
-
-    def total(grams, near, far):
-        return grams[0] + near[0].astype(jnp.float32) + far.astype(jnp.float32)
-
-    last = pairs.shape[0] - CHUNKS[-1]
-    result = jnp.concatenate([total(*each) for each in early], axis=0)
-    result = jnp.pad(result, ((0, CHUNKS[-1]), (0, 0), (0, 0))) * right_norm
-    result, final = lax.optimization_barrier((result, kept[-1]))
-    return result.at[last:].set(total(*final) * right_norm[last:])
+    early, _ = lax.optimization_barrier((tuple(kept[:-1]), ready[-1]))
+    totals = [
+        grams[0] + near[0].astype(jnp.float32) + far.astype(jnp.float32)
+        for grams, near, far in (*early, kept[-1])
+    ]
+    return jnp.concatenate(totals, axis=0) * right_norm
 
 
 def solution(mesh):

time: 138 us -> 148 us (1.072)
  the two profiles are of different devices: /device:TPU:31 before, /device:TPU:32 now
where the time goes in v6:
time: 148 us; the launch traced here: 146 us
  waiting for transfers between devices  70.5 us (48%)
  starting transfers between devices  40.7 us (28%)
  Pallas kernels  20.2 us (14%)
  other arithmetic  9.15 us (6%)
  local copies, waits for them, and re-layouts  4 us (3%)
    ppermute x29, waiting for transfers between devices, permute_doc(): return lax.ppermute(value, 'doc', moves)  50.5 us
    ppermute x29, starting transfers between devices, permute_doc(): return lax.ppermute(value, 'doc', moves)  24.8 us
    ppermute x7, waiting for transfers between devices, swap_term(): return lax.ppermute(value, 'term', [(a, a ^ bit) for a in range(n_term)])  20 us
    ppermute x7, starting transfers between devices, swap_term(): return lax.ppermute(value, 'term', [(a, a ^ bit) for a in range(n_term)])  15.9 us
    pallas_call x2, Pallas kernels, gram_chunk(): pl.pallas_call(kernel, in_specs=[smem] * 3 + [vmem] * n_term + [anywhere]...  15.7 us
    another operation x2, other arithmetic  3.57 us
  transfers between devices with their start and end apart: 36, of which 23 were waited for; matrix products, arithmetic and copies ran while one was open for 4% of the time, Pallas kernels for 2%

profile of v6, /device:TPU:32, one launch (start us, length us, event | category | flops | bytes accessed | tf_op | source)
XLA Modules:
  0.0 145.7 jit_solution(10299679119048038326)
XLA Ops:
  0.0 2.0 %prepare.1 = (bf16[1056,128]{1,0:T(8,128)(2,1)}, bf16[2,128,512]{2,1,0:T(8,128)(2,1)}) custom-call(s32[2,4]{1,0:T(2,128)} %own_ref.3, s32[2,4]{1,0:T(2,128)} %live_ref.1, s32[2,128]{1,0:T(2,128)} %bitcast.32, s32[2,4,128,128]{3,2,1,0:T(8,128)} %count_ref.1), custom_call_target="tpu_custom_call" | custom-call | tf_op jit(solution)/shard_map/prepare/pallas_call | solution.py:104
  2.0 1.5 %collective-permute-start.2 = (bf16[1056,128]{1,0:T(8,128)(2,1)}, bf16[1056,128]{1,0:T(8,128)(2,1)S(1)}, u32[]{:S(2)}, u32[]{:S(2)}) collective-permute-start(bf16[1056,128]{1,0:T(8,128)(2,1)} %get-tuple-element.23), channel_id=1, source_target_pairs={{48,0},{200,8},{0,16},{216,24},{16,32},{232,40},{32,48},{248,56},{... | collective-permute-start | bytes 811016 | tf_op jit(solution)/shard_map/ppermute | solution.py:32
  3.5 2.7 %collective-permute-start.1 = (bf16[1056,128]{1,0:T(8,128)(2,1)}, bf16[1056,128]{1,0:T(8,128)(2,1)S(1)}, u32[]{:S(2)}, u32[]{:S(2)}) collective-permute-start(bf16[1056,128]{1,0:T(8,128)(2,1)} %get-tuple-element.23), channel_id=1, source_target_pairs={{32,0},{136,8},{48,16},{152,24},{0,32},{168,40},{16,48},{184,56},{... | collective-permute-start | bytes 811016 | tf_op jit(solution)/shard_map/ppermute | solution.py:32
  9.4 4.4 %collective-permute-done.1 = bf16[1056,128]{1,0:T(8,128)(2,1)S(1)} collective-permute-done((bf16[1056,128]{1,0:T(8,128)(2,1)}, bf16[1056,128]{1,0:T(8,128)(2,1)S(1)}, u32[]{:S(2)}, u32[]{:S(2)}) %collective-permute-start.1) | collective-permute-done | bytes 270368 | tf_op jit(solution)/shard_map/ppermute | solution.py:32
  13.8 3.1 %collective-permute-start.14 = (bf16[2112,128]{1,0:T(8,128)(2,1)S(1)}, bf16[2112,128]{1,0:T(8,128)(2,1)S(1)}, u32[]{:S(2)}, u32[]{:S(2)}) collective-permute-start(bf16[2112,128]{1,0:T(8,128)(2,1)S(1)} %constant_dynamic-update-slice_fusion.2.refs_8_), channel_id=1, source_target_pairs={{64,0},{24,8},{80,16},{40,24},{96,32},{56,40},{112,48},{8,56},{128... | collective-permute-start | bytes 1622024 | tf_op jit(solution)/shard_map/ppermute | solution.py:32
  17.0 3.3 %collective-permute-start.13 = (bf16[2112,128]{1,0:T(8,128)(2,1)S(1)}, bf16[2112,128]{1,0:T(8,128)(2,1)S(1)}, u32[]{:S(2)}, u32[]{:S(2)}) collective-permute-start(bf16[2112,128]{1,0:T(8,128)(2,1)S(1)} %constant_dynamic-update-slice_fusion.refs_7_), channel_id=1, source_target_pairs={{64,0},{24,8},{80,16},{40,24},{96,32},{56,40},{112,48},{8,56},{128... | collective-permute-start | bytes 1622024 | tf_op jit(solution)/shard_map/ppermute | solution.py:32
  20.3 3.3 %collective-permute-start.3 = (bf16[4,32,128]{2,1,0:T(8,128)(2,1)S(1)}, bf16[4,32,128]{2,1,0:T(8,128)(2,1)S(1)}, u32[]{:S(2)}, u32[]{:S(2)}) collective-permute-start(bf16[4,32,128]{2,1,0:T(8,128)(2,1)S(1)} %pad_maximum_fusion.refs_0_), channel_id=1, source_target_pairs={{64,0},{24,8},{80,16},{40,24},{96,32},{56,40},{112,48},{8,56},{128... | collective-permute-start | bytes 98312 | tf_op jit(solution)/shard_map/ppermute | solution.py:32
  23.6 6.3 %collective-permute-done.3.refs_1_ = bf16[4,32,128]{2,1,0:T(8,128)(2,1)S(1)} collective-permute-done((bf16[4,32,128]{2,1,0:T(8,128)(2,1)S(1)}, bf16[4,32,128]{2,1,0:T(8,128)(2,1)S(1)}, u32[]{:S(2)}, u32[]{:S(2)}) %collective-permute-start.3) | collective-permute-done | bytes 32800 | tf_op jit(solution)/shard_map/ppermute | solution.py:32
  30.0 2.7 %collective-permute-start.4 = (bf16[4,32,128]{2,1,0:T(8,128)(2,1)S(1)}, bf16[4,32,128]{2,1,0:T(8,128)(2,1)S(1)}, u32[]{:S(2)}, u32[]{:S(2)}) collective-permute-start(bf16[4,32,128]{2,1,0:T(8,128)(2,1)S(1)} %pad_maximum_fusion.refs_0_), channel_id=1, source_target_pairs={{128,0},{40,8},{144,16},{56,24},{160,32},{8,40},{176,48},{24,56},{... | collective-permute-start | bytes 98312 | tf_op jit(solution)/shard_map/ppermute | solution.py:32
  32.6 2.8 %collective-permute-done.4.refs_2_ = bf16[4,32,128]{2,1,0:T(8,128)(2,1)S(1)} collective-permute-done((bf16[4,32,128]{2,1,0:T(8,128)(2,1)S(1)}, bf16[4,32,128]{2,1,0:T(8,128)(2,1)S(1)}, u32[]{:S(2)}, u32[]{:S(2)}) %collective-permute-start.4) | collective-permute-done | bytes 32800 | tf_op jit(solution)/shard_map/ppermute | solution.py:32
  36.4 4.5 %collective-permute-done.5.refs_3_ = bf16[4,32,128]{2,1,0:T(8,128)(2,1)S(1)} collective-permute-done((bf16[4,32,128]{2,1,0:T(8,128)(2,1)S(1)}, bf16[4,32,128]{2,1,0:T(8,128)(2,1)S(1)}, u32[]{:S(2)}, u32[]{:S(2)}) %collective-permute-start.5) | collective-permute-done | bytes 32800 | tf_op jit(solution)/shard_map/ppermute | solution.py:32
  46.4 2.5 %weigh.1 = (s32[2,128]{1,0:T(2,128)}, f32[32,8,128]{2,1,0:T(8,128)}, f32[8,128,128]{2,1,0:T(8,128)}, f32[2,128,512]{2,1,0:T(8,128)}, f32[2,128]{1,0:T(2,128)}) custom-call(s32[2,4]{1,0:T(2,128)} %own_ref.3, bf16[2,128,512]{2,1,0:T(8,128)(2,1)} %get-tuple-element.22.own_ref, bf16[4,32,128]{2,1,0:T(8,128)(2,1)} %copy-done.10, bf16[4,32,128]{2,1,0:T(8,128)(2,1)} %copy-done.11, ...), custom_call_target="tpu_custom_call" | custom-call | tf_op jit(solution)/shard_map/weigh/pallas_call | solution.py:159
  49.0 3.7 %collective-permute-done.10.refs_1_ = f32[2,128]{1,0:T(2,128)S(1)} collective-permute-done((f32[2,128]{1,0:T(2,128)}, f32[2,128]{1,0:T(2,128)S(1)}, u32[]{:S(2)}, u32[]{:S(2)}) %collective-permute-start.10) | collective-permute-done | bytes 1056 | tf_op jit(solution)/shard_map/ppermute | solution.py:76
  52.7 3.3 %collective-permute-start.11 = (f32[2,128]{1,0:T(2,128)}, f32[2,128]{1,0:T(2,128)S(1)}, u32[]{:S(2)}, u32[]{:S(2)}) collective-permute-start(f32[2,128]{1,0:T(2,128)} %get-tuple-element.33.refs_0_), channel_id=1, source_target_pairs={{0,4},{2,6},{4,0},{6,2},{1,5},{3,7},{5,1},{7,3},{8,12},{10,14},{12... | collective-permute-start | bytes 3080 | tf_op jit(solution)/shard_map/ppermute | solution.py:76
  55.9 1.8 %collective-permute-done.11.refs_2_ = f32[2,128]{1,0:T(2,128)S(1)} collective-permute-done((f32[2,128]{1,0:T(2,128)}, f32[2,128]{1,0:T(2,128)S(1)}, u32[]{:S(2)}, u32[]{:S(2)}) %collective-permute-start.11) | collective-permute-done | bytes 1056 | tf_op jit(solution)/shard_map/ppermute | solution.py:76
  57.7 1.6 %collective-permute-start.12 = (f32[2,128]{1,0:T(2,128)}, f32[2,128]{1,0:T(2,128)S(1)}, u32[]{:S(2)}, u32[]{:S(2)}) collective-permute-start(f32[2,128]{1,0:T(2,128)} %get-tuple-element.33.refs_0_), channel_id=1, source_target_pairs={{0,6},{2,4},{4,2},{6,0},{1,7},{3,5},{5,3},{7,1},{8,14},{10,12},{12... | collective-permute-start | bytes 3080 | tf_op jit(solution)/shard_map/ppermute | solution.py:76
  59.3 2.2 %collective-permute-done.12.refs_3_ = f32[2,128]{1,0:T(2,128)S(1)} collective-permute-done((f32[2,128]{1,0:T(2,128)}, f32[2,128]{1,0:T(2,128)S(1)}, u32[]{:S(2)}, u32[]{:S(2)}) %collective-permute-start.12) | collective-permute-done | bytes 1056 | tf_op jit(solution)/shard_map/ppermute | solution.py:76
  62.0 2.0 %collective-permute-start.15 = (bf16[2112,128]{1,0:T(8,128)(2,1)S(1)}, bf16[2112,128]{1,0:T(8,128)(2,1)}, u32[]{:S(2)}, u32[]{:S(2)}) collective-permute-start(bf16[2112,128]{1,0:T(8,128)(2,1)S(1)} %collective-permute-done.13.refs_9_), channel_id=1, source_target_pairs={{64,0},{24,8},{80,16},{40,24},{96,32},{56,40},{112,48},{8,56},{128... | collective-permute-start | bytes 1622024 | tf_op jit(solution)/shard_map/ppermute | solution.py:32
  64.8 6.7 %collective-permute-done.15.refs_11_ = bf16[2112,128]{1,0:T(8,128)(2,1)} collective-permute-done((bf16[2112,128]{1,0:T(8,128)(2,1)S(1)}, bf16[2112,128]{1,0:T(8,128)(2,1)}, u32[]{:S(2)}, u32[]{:S(2)}) %collective-permute-start.15) | collective-permute-done | bytes 540704 | tf_op jit(solution)/shard_map/ppermute | solution.py:32
  71.5 3.2 %collective-permute-done.17.refs_12_ = bf16[2112,128]{1,0:T(8,128)(2,1)} collective-permute-done((bf16[2112,128]{1,0:T(8,128)(2,1)S(1)}, bf16[2112,128]{1,0:T(8,128)(2,1)}, u32[]{:S(2)}, u32[]{:S(2)}) %collective-permute-start.17) | collective-permute-done | bytes 540704 | tf_op jit(solution)/shard_map/ppermute | solution.py:32
  77.8 8.5 %gram.2 = f32[4,36,32,128]{3,2,1,0:T(8,128)} custom-call(s32[64,2]{1,0:T(8,128)} %copy.7.pair_ref, s32[2,4]{1,0:T(2,128)} %own_ref.3, s32[2,128]{1,0:T(2,128)} %get-tuple-element.24.ids_ref, f32[2,128]{1,0:T(2,128)} %get-tuple-element.33.refs_0_, f32[2,128]{1,0:T(2,128)} %copy-done.19, f32[2,128]{1,0:T(2,128)} %copy-done.21, f32[2,128]{1,0:T(2,128)} %copy-done.23, ...), custom_call_target="tpu_custom_call" | custom-call | tf_op jit(solution)/shard_map/gram/pallas_call | solution.py:288
  87.8 7.3 %gram.3 = f32[4,28,32,128]{3,2,1,0:T(8,128)} custom-call(s32[64,2]{1,0:T(8,128)} %copy.7.pair_ref, s32[2,4]{1,0:T(2,128)} %own_ref.3, s32[2,128]{1,0:T(2,128)} %get-tuple-element.24.ids_ref, f32[2,128]{1,0:T(2,128)} %get-tuple-element.33.refs_0_, f32[2,128]{1,0:T(2,128)} %copy-done.19, f32[2,128]{1,0:T(2,128)} %copy-done.21, f32[2,128]{1,0:T(2,128)} %copy-done.23, ...), custom_call_target="tpu_custom_call" | custom-call | tf_op jit(solution)/shard_map/gram/pallas_call | solution.py:288
  95.0 2.2 %slice_convert_fusion.1 = f16[2,28,32,128]{3,2,1,0:T(8,128)(2,1)} fusion(f32[4,28,32,128]{3,2,1,0:T(8,128)} %gram.3), kind=kLoop, calls=%fused_computation.3 | loop fusion | flops 229376 | bytes 1376256 | tf_op jit(solution)/shard_map/convert
  97.2 2.4 %collective-permute-start.29 = (f16[2,28,32,128]{3,2,1,0:T(8,128)(2,1)}, f16[2,28,32,128]{3,2,1,0:T(8,128)(2,1)S(1)}, u32[]{:S(2)}, u32[]{:S(2)}) collective-permute-start(f16[2,28,32,128]{3,2,1,0:T(8,128)(2,1)} %slice_convert_fusion.1), channel_id=1, source_target_pairs={{0,2},{2,0},{4,6},{6,4},{1,3},{3,1},{5,7},{7,5},{8,10},{10,8},{12,... | collective-permute-start | bytes 1376264 | tf_op jit(solution)/shard_map/ppermute | solution.py:76
  100.9 3.6 %collective-permute-done.32 = f32[2,2,128]{2,1,0:T(2,128)S(1)} collective-permute-done((f32[2,2,128]{2,1,0:T(2,128)S(1)}, f32[2,2,128]{2,1,0:T(2,128)S(1)}, u32[]{:S(2)}, u32[]{:S(2)}) %collective-permute-start.32) | collective-permute-done | bytes 2080 | tf_op jit(solution)/shard_map/ppermute | solution.py:32
  105.3 4.3 %collective-permute-done.33 = f32[4,2,128]{2,1,0:T(2,128)S(1)} collective-permute-done((f32[4,2,128]{2,1,0:T(2,128)S(1)}, f32[4,2,128]{2,1,0:T(2,128)S(1)}, u32[]{:S(2)}, u32[]{:S(2)}) %collective-permute-start.33) | collective-permute-done | bytes 4128 | tf_op jit(solution)/shard_map/ppermute | solution.py:32
  110.1 3.2 %collective-permute-done.34 = f32[8,2,128]{2,1,0:T(2,128)S(1)} collective-permute-done((f32[8,2,128]{2,1,0:T(2,128)S(1)}, f32[8,2,128]{2,1,0:T(2,128)S(1)}, u32[]{:S(2)}, u32[]{:S(2)}) %collective-permute-start.34) | collective-permute-done | bytes 8224 | tf_op jit(solution)/shard_map/ppermute | solution.py:32
  113.4 5.2 %collective-permute-done.35 = f32[16,2,128]{2,1,0:T(2,128)S(1)} collective-permute-done((f32[16,2,128]{2,1,0:T(2,128)S(1)}, f32[16,2,128]{2,1,0:T(2,128)S(1)}, u32[]{:S(2)}, u32[]{:S(2)}) %collective-permute-start.35) | collective-permute-done | bytes 16416 | tf_op jit(solution)/shard_map/ppermute | solution.py:32
  120.3 4.4 %collective-permute-start.30 = (f16[28,32,128]{2,1,0:T(8,128)(2,1)S(1)}, f16[28,32,128]{2,1,0:T(8,128)(2,1)S(1)}, u32[]{:S(2)}, u32[]{:S(2)}) collective-permute-start(f16[28,32,128]{2,1,0:T(8,128)(2,1)S(1)} %fusion.5), channel_id=1, source_target_pairs={{0,4},{2,6},{4,0},{6,2},{1,5},{3,7},{5,1},{7,3},{8,12},{10,14},{12... | collective-permute-start | bytes 688136 | tf_op jit(solution)/shard_map/ppermute | solution.py:76
  126.3 4.1 %collective-permute-start.28 = (f16[36,32,128]{2,1,0:T(8,128)(2,1)S(1)}, f16[36,32,128]{2,1,0:T(8,128)(2,1)S(1)}, u32[]{:S(2)}, u32[]{:S(2)}) collective-permute-start(f16[36,32,128]{2,1,0:T(8,128)(2,1)S(1)} %fusion.4), channel_id=1, source_target_pairs={{0,4},{2,6},{4,0},{6,2},{1,5},{3,7},{5,1},{7,3},{8,12},{10,14},{12... | collective-permute-start | bytes 884744 | tf_op jit(solution)/shard_map/ppermute | solution.py:76
  130.5 8.6 %collective-permute-done.30 = f16[28,32,128]{2,1,0:T(8,128)(2,1)S(1)} collective-permute-done((f16[28,32,128]{2,1,0:T(8,128)(2,1)S(1)}, f16[28,32,128]{2,1,0:T(8,128)(2,1)S(1)}, u32[]{:S(2)}, u32[]{:S(2)}) %collective-permute-start.30) | collective-permute-done | bytes 229408 | tf_op jit(solution)/shard_map/ppermute | solution.py:76
  140.2 3.3 %collective-permute-done.28 = f16[36,32,128]{2,1,0:T(8,128)(2,1)S(1)} collective-permute-done((f16[36,32,128]{2,1,0:T(8,128)(2,1)S(1)}, f16[36,32,128]{2,1,0:T(8,128)(2,1)S(1)}, u32[]{:S(2)}, u32[]{:S(2)}) %collective-permute-start.28) | collective-permute-done | bytes 294944 | tf_op jit(solution)/shard_map/ppermute | solution.py:76
  (128 shorter events, 24.2 us)
Async XLA Ops:
  2.0 11.8 %collective-permute-start.2 = (bf16[1056,128]{1,0:T(8,128)(2,1)}, bf16[1056,128]{1,0:T(8,128)(2,1)S(1)}, u32[]{:S(2)}, u32[]{:S(2)}) collective-permute-start(bf16[1056,128]{1,0:T(8,128)(2,1)} %get-tuple-element.23), channel_id=1, source_target_pairs={{48,0},{200,8},{0,16},{216,24},{16,32},{232,40},{32,48},{248,56},{... | collective-permute-start | bytes 811016 | tf_op jit(solution)/shard_map/ppermute | solution.py:32
  3.5 10.3 %collective-permute-start.1 = (bf16[1056,128]{1,0:T(8,128)(2,1)}, bf16[1056,128]{1,0:T(8,128)(2,1)S(1)}, u32[]{:S(2)}, u32[]{:S(2)}) collective-permute-start(bf16[1056,128]{1,0:T(8,128)(2,1)} %get-tuple-element.23), channel_id=1, source_target_pairs={{32,0},{136,8},{48,16},{152,24},{0,32},{168,40},{16,48},{184,56},{... | collective-permute-start | bytes 811016 | tf_op jit(solution)/shard_map/ppermute | solution.py:32
  6.2 10.7 %collective-permute-start = (bf16[1056,128]{1,0:T(8,128)(2,1)}, bf16[1056,128]{1,0:T(8,128)(2,1)S(1)}, u32[]{:S(2)}, u32[]{:S(2)}) collective-permute-start(bf16[1056,128]{1,0:T(8,128)(2,1)} %get-tuple-element.23), channel_id=1, source_target_pairs={{16,0},{72,8},{32,16},{88,24},{48,32},{104,40},{0,48},{120,56},{80... | collective-permute-start | bytes 811016 | tf_op jit(solution)/shard_map/ppermute | solution.py:32
  13.8 48.2 %collective-permute-start.14 = (bf16[2112,128]{1,0:T(8,128)(2,1)S(1)}, bf16[2112,128]{1,0:T(8,128)(2,1)S(1)}, u32[]{:S(2)}, u32[]{:S(2)}) collective-permute-start(bf16[2112,128]{1,0:T(8,128)(2,1)S(1)} %constant_dynamic-update-slice_fusion.2.refs_8_), channel_id=1, source_target_pairs={{64,0},{24,8},{80,16},{40,24},{96,32},{56,40},{112,48},{8,56},{128... | collective-permute-start | bytes 1622024 | tf_op jit(solution)/shard_map/ppermute | solution.py:32
  16.9 47.1 %collective-permute-start.16 = (bf16[2112,128]{1,0:T(8,128)(2,1)S(1)}, bf16[2112,128]{1,0:T(8,128)(2,1)S(1)}, u32[]{:S(2)}, u32[]{:S(2)}) collective-permute-start(bf16[2112,128]{1,0:T(8,128)(2,1)S(1)} %constant_dynamic-update-slice_fusion.2.refs_8_), channel_id=1, source_target_pairs={{192,0},{56,8},{208,16},{8,24},{224,32},{24,40},{240,48},{40,56},{... | collective-permute-start | bytes 1622024 | tf_op jit(solution)/shard_map/ppermute | solution.py:32
  17.0 44.5 %collective-permute-start.13 = (bf16[2112,128]{1,0:T(8,128)(2,1)S(1)}, bf16[2112,128]{1,0:T(8,128)(2,1)S(1)}, u32[]{:S(2)}, u32[]{:S(2)}) collective-permute-start(bf16[2112,128]{1,0:T(8,128)(2,1)S(1)} %constant_dynamic-update-slice_fusion.refs_7_), channel_id=1, source_target_pairs={{64,0},{24,8},{80,16},{40,24},{96,32},{56,40},{112,48},{8,56},{128... | collective-permute-start | bytes 1622024 | tf_op jit(solution)/shard_map/ppermute | solution.py:32
  20.3 43.7 %collective-permute-start.18 = (bf16[2112,128]{1,0:T(8,128)(2,1)S(1)}, bf16[2112,128]{1,0:T(8,128)(2,1)S(1)}, u32[]{:S(2)}, u32[]{:S(2)}) collective-permute-start(bf16[2112,128]{1,0:T(8,128)(2,1)S(1)} %constant_dynamic-update-slice_fusion.refs_7_), channel_id=1, source_target_pairs={{192,0},{56,8},{208,16},{8,24},{224,32},{24,40},{240,48},{40,56},{... | collective-permute-start | bytes 1622024 | tf_op jit(solution)/shard_map/ppermute | solution.py:32
  20.3 9.6 %collective-permute-start.3 = (bf16[4,32,128]{2,1,0:T(8,128)(2,1)S(1)}, bf16[4,32,128]{2,1,0:T(8,128)(2,1)S(1)}, u32[]{:S(2)}, u32[]{:S(2)}) collective-permute-start(bf16[4,32,128]{2,1,0:T(8,128)(2,1)S(1)} %pad_maximum_fusion.refs_0_), channel_id=1, source_target_pairs={{64,0},{24,8},{80,16},{40,24},{96,32},{56,40},{112,48},{8,56},{128... | collective-permute-start | bytes 98312 | tf_op jit(solution)/shard_map/ppermute | solution.py:32
  30.0 5.4 %collective-permute-start.4 = (bf16[4,32,128]{2,1,0:T(8,128)(2,1)S(1)}, bf16[4,32,128]{2,1,0:T(8,128)(2,1)S(1)}, u32[]{:S(2)}, u32[]{:S(2)}) collective-permute-start(bf16[4,32,128]{2,1,0:T(8,128)(2,1)S(1)} %pad_maximum_fusion.refs_0_), channel_id=1, source_target_pairs={{128,0},{40,8},{144,16},{56,24},{160,32},{8,40},{176,48},{24,56},{... | collective-permute-start | bytes 98312 | tf_op jit(solution)/shard_map/ppermute | solution.py:32
  35.4 5.6 %collective-permute-start.5 = (bf16[4,32,128]{2,1,0:T(8,128)(2,1)S(1)}, bf16[4,32,128]{2,1,0:T(8,128)(2,1)S(1)}, u32[]{:S(2)}, u32[]{:S(2)}) collective-permute-start(bf16[4,32,128]{2,1,0:T(8,128)(2,1)S(1)} %pad_maximum_fusion.refs_0_), channel_id=1, source_target_pairs={{192,0},{56,8},{208,16},{8,24},{224,32},{24,40},{240,48},{40,56},{... | collective-permute-start | bytes 98312 | tf_op jit(solution)/shard_map/ppermute | solution.py:32
  48.9 3.8 %collective-permute-start.10 = (f32[2,128]{1,0:T(2,128)}, f32[2,128]{1,0:T(2,128)S(1)}, u32[]{:S(2)}, u32[]{:S(2)}) collective-permute-start(f32[2,128]{1,0:T(2,128)} %get-tuple-element.33.refs_0_), channel_id=1, source_target_pairs={{0,2},{2,0},{4,6},{6,4},{1,3},{3,1},{5,7},{7,5},{8,10},{10,8},{12,... | collective-permute-start | bytes 3080 | tf_op jit(solution)/shard_map/ppermute | solution.py:76
  52.7 5.0 %collective-permute-start.11 = (f32[2,128]{1,0:T(2,128)}, f32[2,128]{1,0:T(2,128)S(1)}, u32[]{:S(2)}, u32[]{:S(2)}) collective-permute-start(f32[2,128]{1,0:T(2,128)} %get-tuple-element.33.refs_0_), channel_id=1, source_target_pairs={{0,4},{2,6},{4,0},{6,2},{1,5},{3,7},{5,1},{7,3},{8,12},{10,14},{12... | collective-permute-start | bytes 3080 | tf_op jit(solution)/shard_map/ppermute | solution.py:76
  57.7 3.8 %collective-permute-start.12 = (f32[2,128]{1,0:T(2,128)}, f32[2,128]{1,0:T(2,128)S(1)}, u32[]{:S(2)}, u32[]{:S(2)}) collective-permute-start(f32[2,128]{1,0:T(2,128)} %get-tuple-element.33.refs_0_), channel_id=1, source_target_pairs={{0,6},{2,4},{4,2},{6,0},{1,7},{3,5},{5,3},{7,1},{8,14},{10,12},{12... | collective-permute-start | bytes 3080 | tf_op jit(solution)/shard_map/ppermute | solution.py:76
  61.5 2.7 %collective-permute-start.19 = (bf16[2112,128]{1,0:T(8,128)(2,1)S(1)}, bf16[2112,128]{1,0:T(8,128)(2,1)S(1)}, u32[]{:S(2)}, u32[]{:S(2)}) collective-permute-start(bf16[2112,128]{1,0:T(8,128)(2,1)S(1)} %constant_dynamic-update-slice_fusion.refs_7_), channel_id=1, source_target_pairs={{8,0},{0,8},{24,16},{16,24},{40,32},{32,40},{56,48},{48,56},{72,64... | collective-permute-start | bytes 1622024 | tf_op jit(solution)/shard_map/ppermute | solution.py:32
  61.5 3.2 %collective-permute-start.20 = (bf16[2112,128]{1,0:T(8,128)(2,1)S(1)}, bf16[2112,128]{1,0:T(8,128)(2,1)S(1)}, u32[]{:S(2)}, u32[]{:S(2)}) collective-permute-start(bf16[2112,128]{1,0:T(8,128)(2,1)S(1)} %constant_dynamic-update-slice_fusion.2.refs_8_), channel_id=1, source_target_pairs={{8,0},{0,8},{24,16},{16,24},{40,32},{32,40},{56,48},{48,56},{72,64... | collective-permute-start | bytes 1622024 | tf_op jit(solution)/shard_map/ppermute | solution.py:32
  62.0 9.5 %collective-permute-start.15 = (bf16[2112,128]{1,0:T(8,128)(2,1)S(1)}, bf16[2112,128]{1,0:T(8,128)(2,1)}, u32[]{:S(2)}, u32[]{:S(2)}) collective-permute-start(bf16[2112,128]{1,0:T(8,128)(2,1)S(1)} %collective-permute-done.13.refs_9_), channel_id=1, source_target_pairs={{64,0},{24,8},{80,16},{40,24},{96,32},{56,40},{112,48},{8,56},{128... | collective-permute-start | bytes 1622024 | tf_op jit(solution)/shard_map/ppermute | solution.py:32
  64.0 10.7 %collective-permute-start.17 = (bf16[2112,128]{1,0:T(8,128)(2,1)S(1)}, bf16[2112,128]{1,0:T(8,128)(2,1)}, u32[]{:S(2)}, u32[]{:S(2)}) collective-permute-start(bf16[2112,128]{1,0:T(8,128)(2,1)S(1)} %collective-permute-done.16.refs_14_), channel_id=1, source_target_pairs={{192,0},{56,8},{208,16},{8,24},{224,32},{24,40},{240,48},{40,56},{... | collective-permute-start | bytes 1622024 | tf_op jit(solution)/shard_map/ppermute | solution.py:32
  64.1 10.7 %collective-permute-start.21 = (bf16[2112,128]{1,0:T(8,128)(2,1)S(1)}, bf16[2112,128]{1,0:T(8,128)(2,1)S(1)}, u32[]{:S(2)}, u32[]{:S(2)}) collective-permute-start(bf16[2112,128]{1,0:T(8,128)(2,1)S(1)} %collective-permute-done.13.refs_9_), channel_id=1, source_target_pairs={{8,0},{0,8},{24,16},{16,24},{40,32},{32,40},{56,48},{48,56},{72,64... | collective-permute-start | bytes 1622024 | tf_op jit(solution)/shard_map/ppermute | solution.py:32
  64.2 12.7 %collective-permute-start.26 = (bf16[2112,128]{1,0:T(8,128)(2,1)S(1)}, bf16[2112,128]{1,0:T(8,128)(2,1)}, u32[]{:S(2)}, u32[]{:S(2)}) collective-permute-start(bf16[2112,128]{1,0:T(8,128)(2,1)S(1)} %collective-permute-done.16.refs_14_), channel_id=1, source_target_pairs={{8,0},{0,8},{24,16},{16,24},{40,32},{32,40},{56,48},{48,56},{72,64... | collective-permute-start | bytes 1622024 | tf_op jit(solution)/shard_map/ppermute | solution.py:32
  64.7 12.2 %collective-permute-start.22 = (bf16[2112,128]{1,0:T(8,128)(2,1)S(1)}, bf16[2112,128]{1,0:T(8,128)(2,1)}, u32[]{:S(2)}, u32[]{:S(2)}) collective-permute-start(bf16[2112,128]{1,0:T(8,128)(2,1)S(1)} %collective-permute-done.14.refs_10_), channel_id=1, source_target_pairs={{8,0},{0,8},{24,16},{16,24},{40,32},{32,40},{56,48},{48,56},{72,64... | collective-permute-start | bytes 1622024 | tf_op jit(solution)/shard_map/ppermute | solution.py:32
  71.5 5.4 %collective-permute-start.25 = (bf16[2112,128]{1,0:T(8,128)(2,1)S(1)}, bf16[2112,128]{1,0:T(8,128)(2,1)}, u32[]{:S(2)}, u32[]{:S(2)}) collective-permute-start(bf16[2112,128]{1,0:T(8,128)(2,1)S(1)} %collective-permute-done.18.refs_13_), channel_id=1, source_target_pairs={{8,0},{0,8},{24,16},{16,24},{40,32},{32,40},{56,48},{48,56},{72,64... | collective-permute-start | bytes 1622024 | tf_op jit(solution)/shard_map/ppermute | solution.py:32
  74.7 2.3 %collective-permute-start.23 = (bf16[2112,128]{1,0:T(8,128)(2,1)}, bf16[2112,128]{1,0:T(8,128)(2,1)}, u32[]{:S(2)}, u32[]{:S(2)}) collective-permute-start(bf16[2112,128]{1,0:T(8,128)(2,1)} %collective-permute-done.15.refs_11_), channel_id=1, source_target_pairs={{8,0},{0,8},{24,16},{16,24},{40,32},{32,40},{56,48},{48,56},{72,64... | collective-permute-start | bytes 1622024 | tf_op jit(solution)/shard_map/ppermute | solution.py:32
  74.7 3.0 %collective-permute-start.24 = (bf16[2112,128]{1,0:T(8,128)(2,1)}, bf16[2112,128]{1,0:T(8,128)(2,1)}, u32[]{:S(2)}, u32[]{:S(2)}) collective-permute-start(bf16[2112,128]{1,0:T(8,128)(2,1)} %collective-permute-done.17.refs_12_), channel_id=1, source_target_pairs={{8,0},{0,8},{24,16},{16,24},{40,32},{32,40},{56,48},{48,56},{72,64... | collective-permute-start | bytes 1622024 | tf_op jit(solution)/shard_map/ppermute | solution.py:32
  97.2 22.0 %collective-permute-start.29 = (f16[2,28,32,128]{3,2,1,0:T(8,128)(2,1)}, f16[2,28,32,128]{3,2,1,0:T(8,128)(2,1)S(1)}, u32[]{:S(2)}, u32[]{:S(2)}) collective-permute-start(f16[2,28,32,128]{3,2,1,0:T(8,128)(2,1)} %slice_convert_fusion.1), channel_id=1, source_target_pairs={{0,2},{2,0},{4,6},{6,4},{1,3},{3,1},{5,7},{7,5},{8,10},{10,8},{12,... | collective-permute-start | bytes 1376264 | tf_op jit(solution)/shard_map/ppermute | solution.py:76
  99.6 25.7 %collective-permute-start.27 = (f16[2,36,32,128]{3,2,1,0:T(8,128)(2,1)S(1)}, f16[2,36,32,128]{3,2,1,0:T(8,128)(2,1)}, u32[]{:S(2)}, u32[]{:S(2)}) collective-permute-start(f16[2,36,32,128]{3,2,1,0:T(8,128)(2,1)S(1)} %slice_convert_fusion), channel_id=1, source_target_pairs={{0,2},{2,0},{4,6},{6,4},{1,3},{3,1},{5,7},{7,5},{8,10},{10,8},{12,... | collective-permute-start | bytes 1769480 | tf_op jit(solution)/shard_map/ppermute | solution.py:76
  99.6 1.2 collective-permute-start.31
  100.9 3.6 %collective-permute-start.32 = (f32[2,2,128]{2,1,0:T(2,128)S(1)}, f32[2,2,128]{2,1,0:T(2,128)S(1)}, u32[]{:S(2)}, u32[]{:S(2)}) collective-permute-start(f32[2,2,128]{2,1,0:T(2,128)S(1)} %pad_maximum_fusion.3), channel_id=1, source_target_pairs={{16,0},{24,8},{32,16},{40,24},{48,32},{56,40},{0,48},{8,56},{80,64... | collective-permute-start | bytes 6152 | tf_op jit(solution)/shard_map/ppermute | solution.py:32
  104.5 5.1 %collective-permute-start.33 = (f32[4,2,128]{2,1,0:T(2,128)S(1)}, f32[4,2,128]{2,1,0:T(2,128)S(1)}, u32[]{:S(2)}, u32[]{:S(2)}) collective-permute-start(f32[4,2,128]{2,1,0:T(2,128)S(1)} %pad_maximum_fusion.2), channel_id=1, source_target_pairs={{32,0},{40,8},{48,16},{56,24},{0,32},{8,40},{16,48},{24,56},{96,64... | collective-permute-start | bytes 12296 | tf_op jit(solution)/shard_map/ppermute | solution.py:32
  109.6 3.7 %collective-permute-start.34 = (f32[8,2,128]{2,1,0:T(2,128)S(1)}, f32[8,2,128]{2,1,0:T(2,128)S(1)}, u32[]{:S(2)}, u32[]{:S(2)}) collective-permute-start(f32[8,2,128]{2,1,0:T(2,128)S(1)} %pad_maximum_fusion.1), channel_id=1, source_target_pairs={{64,0},{72,8},{80,16},{88,24},{96,32},{104,40},{112,48},{120,56},{... | collective-permute-start | bytes 24584 | tf_op jit(solution)/shard_map/ppermute | solution.py:32
  113.3 5.3 %collective-permute-start.35 = (f32[16,2,128]{2,1,0:T(2,128)S(1)}, f32[16,2,128]{2,1,0:T(2,128)S(1)}, u32[]{:S(2)}, u32[]{:S(2)}) collective-permute-start(f32[16,2,128]{2,1,0:T(2,128)S(1)} %get-tuple-element.41), channel_id=1, source_target_pairs={{128,0},{136,8},{144,16},{152,24},{160,32},{168,40},{176,48},{184,... | collective-permute-start | bytes 49160 | tf_op jit(solution)/shard_map/ppermute | solution.py:32
  120.3 18.8 %collective-permute-start.30 = (f16[28,32,128]{2,1,0:T(8,128)(2,1)S(1)}, f16[28,32,128]{2,1,0:T(8,128)(2,1)S(1)}, u32[]{:S(2)}, u32[]{:S(2)}) collective-permute-start(f16[28,32,128]{2,1,0:T(8,128)(2,1)S(1)} %fusion.5), channel_id=1, source_target_pairs={{0,4},{2,6},{4,0},{6,2},{1,5},{3,7},{5,1},{7,3},{8,12},{10,14},{12... | collective-permute-start | bytes 688136 | tf_op jit(solution)/shard_map/ppermute | solution.py:76
  126.3 17.2 %collective-permute-start.28 = (f16[36,32,128]{2,1,0:T(8,128)(2,1)S(1)}, f16[36,32,128]{2,1,0:T(8,128)(2,1)S(1)}, u32[]{:S(2)}, u32[]{:S(2)}) collective-permute-start(f16[36,32,128]{2,1,0:T(8,128)(2,1)S(1)} %fusion.4), channel_id=1, source_target_pairs={{0,4},{2,6},{4,0},{6,2},{1,5},{3,7},{5,1},{7,3},{8,12},{10,14},{12... | collective-permute-start | bytes 884744 | tf_op jit(solution)/shard_map/ppermute | solution.py:76
  (30 other events, 490.5 us)
